TPU v7x, 512 devices: a whole 4x4x16 slice. The times are simulated.
512 devices in a mesh: tile: 128 (over z, x, core), lev: 4 (over y).
Axes of the slice: x: 4, y: 4, z: 16, core: 2. Of those that a mesh axis runs over, the one named last changes fastest.
Arguments:
- probes: bfloat16 [512, 32, 8, 128], P('tile', None, 'lev'), may hold values from -1 to 1, as said below
- stddev: float32 [512, 32, 128], P('tile'), may hold values from 0.5 to 2
- diffusivity: float32 [128], replicated, may hold values from 0.03 to 0.24
- counts: int32 [128, 128], P('tile'), may hold values from 0 to 16, as said below
- columns: int32 [128, 128, 16], P('tile'), may hold values from 0 to 127
- jacobian: bfloat16 [128, 256, 32], P('tile'), may hold values from -1 to 1
- offsets: int32 [128, 256], replicated, may hold values from 0 to 96
- obs_weights: float32 [128, 256], replicated, may hold values from 0.25 to 4
Outputs:
- hessian_probe: float32 [512, 32, 8, 128], P('tile', None, 'lev')
- trace_share: float32 [128], P('tile')
Inputs may be any that keep to these rules, and one draw needn't show every extreme that they name: `counts`: in every draw one section receives 16 observations from every tile. `columns`: slots at or past counts[t,d] are unused. `probes`: each entry is +1 or -1.
All inputs are finite; a program needn't handle non-finite values.
Results may differ from a plain program's by a relative error of at most 0.00045.
The roundings to bfloat16 on the way count: a program that leaves them out, or rounds other values in their place, can miss the bound.
Values may be sent and summed in bfloat16 or wider, within the bound.
No kernel may reach another device: no remote copies, remote signals or barrier semaphores. Data moves between devices by JAX's collectives and lax.ppermute only.
A program may use at most 64 MiB of HBM per device.

v0:
```python
import math

import jax
import jax.numpy as jnp
from jax import lax
from jax.sharding import PartitionSpec as P

LEV = 128
CH = 256
PROBES = 8
NSTEP = 2


def padded_2(cells, sides, width):
    for axis, dim in sides:
        count = lax.axis_size(axis)
        head = lax.slice_in_dim(cells, 0, width, axis=dim)
        tail = lax.slice_in_dim(cells, cells.shape[dim] - width, cells.shape[dim], axis=dim)
        cells = jnp.concatenate(
            [
                lax.ppermute(tail, axis, [(i, (i + 1) % count) for i in range(count)]),
                cells,
                lax.ppermute(head, axis, [((i + 1) % count, i) for i in range(count)]),
            ],
            axis=dim,
        )
    return cells


def diffuse(extended, diffusivity):
    middle = extended[1:-1]
    padded = jnp.pad(middle, ((0, 0), (1, 1), (0, 0), (0, 0)))
    laplace = extended[2:] + extended[:-2] + padded[:, 2:] + padded[:, :-2] - 4.0 * middle
    return middle + diffusivity * laplace


def smooth(profile, diffusivity):
    for repeat in range(NSTEP):
        extended = padded_2(profile, (("tile", 0),), 1)
        profile = diffuse(extended, diffusivity)
    return profile


def band_matrix(jacobian_rows, offset_rows):
    band_width = jacobian_rows.shape[-1]
    pad_spec = [(0, 0)] * (jacobian_rows.ndim - 1) + [(0, LEV - band_width)]
    widened = jnp.pad(jacobian_rows, pad_spec)
    bit_count = max((LEV - 1).bit_length(), 1)
    for bit_number in range(bit_count):
        step_size = 1 << bit_number
        moved = jnp.roll(widened, step_size, axis=-1)
        chosen = (offset_rows // step_size % 2 == 1)[..., None]
        widened = jnp.where(chosen, moved, widened)
    return widened


def respond(rows_in, dense_map, weights):
    brightness = lax.dot_general(
        rows_in, dense_map, (((1,), (1,)), ((), ())), preferred_element_type=jnp.float32
    )
    weighted = weights * brightness
    energy = jnp.sum(brightness * weighted, axis=1)
    adjoint = jnp.dot(weighted.astype(jnp.bfloat16), dense_map, preferred_element_type=jnp.float32)
    return (adjoint.astype(jnp.bfloat16), energy)


def body(probes, stddev, diffusivity, counts, columns, jacobian, offsets, obs_weights):
    tile_count = lax.axis_size("tile")
    my_section = lax.axis_index("tile")
    row_count, col_count, probe_count, levels = probes.shape
    slot_count = columns.shape[2]
    cell_count = row_count * col_count
    spread = stddev[:, :, None, :]
    profile = (spread * smooth(probes.astype(jnp.float32), diffusivity)).astype(jnp.bfloat16)
    flat_profile = profile.reshape(cell_count, probe_count, levels)
    targets = columns[0]
    live_slots = jnp.arange(slot_count, dtype=jnp.int32)[None, :] < counts[0][:, None]
    cell_ids = jnp.arange(cell_count, dtype=jnp.int32)
    selector = ((targets[:, :, None] == cell_ids[None, None, :]) & live_slots[:, :, None]).astype(
        jnp.bfloat16
    )
    outgoing = jnp.einsum(
        "tkn,npl->tkpl", selector, flat_profile, preferred_element_type=jnp.float32
    ).astype(jnp.bfloat16)
    own_offsets = lax.dynamic_index_in_dim(offsets, my_section, 0, keepdims=False)
    dense_map = band_matrix(jacobian[0], own_offsets)
    weights = lax.dynamic_index_in_dim(obs_weights, my_section, 0, keepdims=False)
    arrived = lax.all_to_all(outgoing, "tile", split_axis=0, concat_axis=0, tiled=True)
    sources, slot_here, probe_here, level_here = arrived.shape
    group_size = math.gcd(sources, 8)
    stacked = arrived.reshape(
        sources // group_size, group_size * slot_here * probe_here, level_here
    )

    def radiate(batch_rows):
        return respond(batch_rows, dense_map, weights)

    adjoint, energy = lax.map(radiate, stacked)
    energy = energy.reshape(sources, slot_here, probe_here).sum(axis=2)
    adjoints_here = adjoint.reshape(arrived.shape)
    returned = lax.all_to_all(adjoints_here, "tile", split_axis=0, concat_axis=0, tiled=True)
    section_part = jnp.sum(energy).reshape(1)
    totals = lax.psum(section_part, "lev")
    trace_share = totals * (1.0 / (PROBES * tile_count * slot_count * CH))
    gradient = jnp.einsum("tkn,tkpl->npl", selector, returned, preferred_element_type=jnp.float32)
    gradient = gradient.reshape(row_count, col_count, probe_count, levels)
    hessian = smooth(spread * gradient, diffusivity)
    return (hessian, trace_share)


def solution(mesh):
    placed = (
        P("tile", None, "lev", None),
        P("tile", None, None),
        P(),
        P("tile", None),
        P("tile", None, None),
        P("tile", None, None),
        P(),
        P(),
    )
    return jax.shard_map(
        body,
        mesh=mesh,
        in_specs=placed,
        out_specs=(P("tile", None, "lev", None), P("tile")),
        check_vma=False,
    )
```

profile of v0, /device:TPU:32, one launch (start us, length us, event | category | flops | bytes accessed | tf_op | source)
XLA Modules:
  0.0 203.5 jit_solution(3389362068707142357)
XLA Ops:
  0.7 0.8 fusion.54
  1.5 3.7 %collective-permute-start = (f32[1,32,2,128]{3,2,1,0:T(2,128)S(1)}, f32[1,32,2,128]{3,2,1,0:T(2,128)S(1)}, u32[]{:S(2)}, u32[]{:S(2)}) collective-permute-start(f32[1,32,2,128]{3,2,1,0:T(2,128)S(1)} %get-tuple-element.61), channel_id=1, source_target_pairs={{4,0},{8,4},{12,8},{16,12},{20,16},{24,20},{28,24},{32,28},{36,32}... | collective-permute-start | bytes 98312 | tf_op jit(solution)/shard_map/ppermute | solution.py:23
  5.1 1.9 collective-permute-start.1
  7.0 0.9 convert_element_type.23
  7.9 4.5 %collective-permute-done.1 = f32[1,32,2,128]{3,2,1,0:T(2,128)S(1)} collective-permute-done((f32[1,32,2,128]{3,2,1,0:T(2,128)S(1)}, f32[1,32,2,128]{3,2,1,0:T(2,128)S(1)}, u32[]{:S(2)}, u32[]{:S(2)}) %collective-permute-start.1) | collective-permute-done | bytes 32800 | tf_op jit(solution)/shard_map/ppermute | solution.py:21
  12.5 0.8 multiply_add_fusion.2
  13.3 1.9 collective-permute-start.2
  15.2 2.4 %collective-permute-start.3 = (f32[1,32,2,128]{3,2,1,0:T(2,128)S(1)}, f32[1,32,2,128]{3,2,1,0:T(2,128)S(1)}, u32[]{:S(2)}, u32[]{:S(2)}) collective-permute-start(f32[1,32,2,128]{3,2,1,0:T(2,128)S(1)} %get-tuple-element.58), channel_id=1, source_target_pairs={{0,4},{4,8},{8,12},{12,16},{16,20},{20,24},{24,28},{28,32},{32,36}... | collective-permute-start | bytes 98312 | tf_op jit(solution)/shard_map/ppermute | solution.py:21
  17.6 0.7 iota_compare_fusion.1
  18.3 4.3 %collective-permute-done.3 = f32[1,32,2,128]{3,2,1,0:T(2,128)S(1)} collective-permute-done((f32[1,32,2,128]{3,2,1,0:T(2,128)S(1)}, f32[1,32,2,128]{3,2,1,0:T(2,128)S(1)}, u32[]{:S(2)}, u32[]{:S(2)}) %collective-permute-start.3) | collective-permute-done | bytes 32800 | tf_op jit(solution)/shard_map/ppermute | solution.py:21
  22.6 1.0 multiply_convert_fusion.2
  23.6 0.5 convolution_convert_fusion.1
  24.1 2.1 %copy.22 = bf16[128,16,2,128]{3,2,1,0:T(2,128)(2,1)} copy(bf16[128,16,2,128]{3,0,2,1:T(8,128)(2,1)S(1)} %convolution_convert_fusion.1) | data formatting | bytes 2097152 | tf_op jit(solution)/shard_map/convert_element_type | solution.py:84
  26.2 19.1 %all-to-all-start = ((bf16[128,16,2,128]{3,2,1,0:T(2,128)(2,1)}), bf16[128,16,2,128]{3,2,1,0:T(2,128)(2,1)S(1)}, u32[]{:S(2)}, u32[]{:S(2)}) async-start(bf16[128,16,2,128]{3,2,1,0:T(2,128)(2,1)} %copy.22), calls=%async_computation | async-start | bytes 2097152 | tf_op jit(solution)/shard_map/all_to_all | solution.py:88
  46.0 0.1 maximum_select_fusion.1
  46.2 0.1 maximum_select_fusion.2
  46.6 0.7 constant_dynamic-slice_fusion.1
  47.7 53.0 %all-to-all-done = bf16[128,16,2,128]{3,2,1,0:T(2,128)(2,1)S(1)} async-done(((bf16[128,16,2,128]{3,2,1,0:T(2,128)(2,1)}), bf16[128,16,2,128]{3,2,1,0:T(2,128)(2,1)S(1)}, u32[]{:S(2)}, u32[]{:S(2)}) %all-to-all-start) | async-done | bytes 1048608 | tf_op jit(solution)/shard_map/all_to_all | solution.py:88
  100.7 9.9 %while.12 = (s32[]{:T(128)}, bf16[16,256,128]{2,1,0:T(8,128)(2,1)S(1)}, f32[16,256]{1,0:T(8,128)S(1)}, f32[256]{0:T(256)S(1)}, bf16[16,256,128]{2,1,0:T(8,128)(2...) while((s32[]{:T(128)}, bf16[16,256,128]{2,1,0:T(8,128)(2,1)S(1)}, f32[16,256]{1,0:T(8,128)S(1)}, ...), condition=%wide.region_2.3_spmd, body=%wide.region_0.2_spmd.sunk | while | flops 33914624 | bytes 791657 | solution.py:98
  100.7 0.2 fusion.63
  101.0 0.3 fusion.64
  101.3 0.2 fusion.63
  101.6 0.3 fusion.64
  102.0 0.2 fusion.63
  102.2 0.3 fusion.64
  102.6 0.2 fusion.63
  102.9 0.3 fusion.64
  103.2 0.2 fusion.63
  103.5 0.3 fusion.64
  103.8 0.2 fusion.63
  104.1 0.3 fusion.64
  104.4 0.2 fusion.63
  104.7 0.3 fusion.64
  105.1 0.2 fusion.63
  105.4 0.3 fusion.64
  105.7 0.2 fusion.63
  106.0 0.3 fusion.64
  106.3 0.2 fusion.63
  106.6 0.3 fusion.64
  106.9 0.2 fusion.63
  107.2 0.3 fusion.64
  107.6 0.2 fusion.63
  107.8 0.3 fusion.64
  108.2 0.2 fusion.63
  108.5 0.3 fusion.64
  108.8 0.2 fusion.63
  109.1 0.3 fusion.64
  109.4 0.2 fusion.63
  109.7 0.3 fusion.64
  110.1 0.2 fusion.63
  110.3 0.3 fusion.64
  110.7 0.2 copy.24
  110.9 61.9 %all_to_all.10 = bf16[128,16,2,128]{3,1,2,0:T(8,128)(2,1)S(1)} all-to-all(bf16[128,16,2,128]{3,1,2,0:T(8,128)(2,1)S(1)} %copy.24), channel_id=1, replica_groups=mesh['tile'=128,'lev'=4] {'tile'}, dimensions={0} | all-to-all | bytes 2097152 | tf_op jit(solution)/shard_map/all_to_all | solution.py:101
  172.7 0.8 fusion.8
  173.6 0.1 copy_multiply_fusion
  173.7 3.4 %collective-permute-start.4 = (f32[1,32,2,128]{3,2,1,0:T(2,128)S(1)}, f32[1,32,2,128]{3,2,1,0:T(2,128)S(1)}, u32[]{:S(2)}, u32[]{:S(2)}) collective-permute-start(f32[1,32,2,128]{3,2,1,0:T(2,128)S(1)} %get-tuple-element.55), channel_id=1, source_target_pairs={{4,0},{8,4},{12,8},{16,12},{20,16},{24,20},{28,24},{32,28},{36,32}... | collective-permute-start | bytes 98312 | tf_op jit(solution)/shard_map/ppermute | solution.py:23
  177.1 1.9 collective-permute-start.5
  179.1 5.4 %collective-permute-done.5 = f32[1,32,2,128]{3,2,1,0:T(2,128)S(1)} collective-permute-done((f32[1,32,2,128]{3,2,1,0:T(2,128)S(1)}, f32[1,32,2,128]{3,2,1,0:T(2,128)S(1)}, u32[]{:S(2)}, u32[]{:S(2)}) %collective-permute-start.5) | collective-permute-done | bytes 32800 | tf_op jit(solution)/shard_map/ppermute | solution.py:21
  184.5 0.1 multiply_add_fusion.1
  184.6 1.9 collective-permute-start.6
  186.6 2.4 %collective-permute-start.7 = (f32[1,32,2,128]{3,2,1,0:T(2,128)S(1)}, f32[1,32,2,128]{3,2,1,0:T(2,128)S(1)}, u32[]{:S(2)}, u32[]{:S(2)}) collective-permute-start(f32[1,32,2,128]{3,2,1,0:T(2,128)S(1)} %get-tuple-element.54), channel_id=1, source_target_pairs={{0,4},{4,8},{8,12},{12,16},{16,20},{20,24},{24,28},{28,32},{32,36}... | collective-permute-start | bytes 98312 | tf_op jit(solution)/shard_map/ppermute | solution.py:21
  189.0 0.6 reduce_sum.17
  189.6 11.3 %psum.7 = f32[1]{0:T(128)} all-reduce(f32[1]{0:T(128)} %bitcast.17), channel_id=1, replica_groups=mesh['tile'=128,'lev'=4] {'lev'}, use_global_device_ids=true, to_apply=%region_4.5 | all-reduce | flops 1 | bytes 8 | tf_op jit(solution)/shard_map/psum | solution.py:103
  201.6 0.8 multiply_add_fusion
  (52 shorter events, 2.1 us)
Async XLA Ops:
  0.6 44.8 %copy-start = (s32[128,256]{1,0:T(8,128)S(1)}, s32[128,256]{1,0:T(8,128)}, u32[]{:S(2)}) copy-start(s32[128,256]{1,0:T(8,128)} %param.16) | copy-start | bytes 393220
  0.6 23.0 %copy-start.3 = (s32[1,128,16]{1,2,0:T(8,128)S(1)}, s32[1,128,16]{1,2,0:T(8,128)}, u32[]{:S(2)}) copy-start(s32[1,128,16]{1,2,0:T(8,128)} %param.14) | copy-start | bytes 24580
  1.5 6.5 %collective-permute-start = (f32[1,32,2,128]{3,2,1,0:T(2,128)S(1)}, f32[1,32,2,128]{3,2,1,0:T(2,128)S(1)}, u32[]{:S(2)}, u32[]{:S(2)}) collective-permute-start(f32[1,32,2,128]{3,2,1,0:T(2,128)S(1)} %get-tuple-element.61), channel_id=1, source_target_pairs={{4,0},{8,4},{12,8},{16,12},{20,16},{24,20},{28,24},{32,28},{36,32}... | collective-permute-start | bytes 98312 | tf_op jit(solution)/shard_map/ppermute | solution.py:23
  5.1 7.3 %collective-permute-start.1 = (f32[1,32,2,128]{3,2,1,0:T(2,128)S(1)}, f32[1,32,2,128]{3,2,1,0:T(2,128)S(1)}, u32[]{:S(2)}, u32[]{:S(2)}) collective-permute-start(f32[1,32,2,128]{3,2,1,0:T(2,128)S(1)} %get-tuple-element.62), channel_id=1, source_target_pairs={{0,4},{4,8},{8,12},{12,16},{16,20},{20,24},{24,28},{28,32},{32,36}... | collective-permute-start | bytes 98312 | tf_op jit(solution)/shard_map/ppermute | solution.py:21
  13.3 5.0 %collective-permute-start.2 = (f32[1,32,2,128]{3,2,1,0:T(2,128)S(1)}, f32[1,32,2,128]{3,2,1,0:T(2,128)S(1)}, u32[]{:S(2)}, u32[]{:S(2)}) collective-permute-start(f32[1,32,2,128]{3,2,1,0:T(2,128)S(1)} %get-tuple-element.57), channel_id=1, source_target_pairs={{4,0},{8,4},{12,8},{16,12},{20,16},{24,20},{28,24},{32,28},{36,32}... | collective-permute-start | bytes 98312 | tf_op jit(solution)/shard_map/ppermute | solution.py:23
  15.2 7.3 %collective-permute-start.3 = (f32[1,32,2,128]{3,2,1,0:T(2,128)S(1)}, f32[1,32,2,128]{3,2,1,0:T(2,128)S(1)}, u32[]{:S(2)}, u32[]{:S(2)}) collective-permute-start(f32[1,32,2,128]{3,2,1,0:T(2,128)S(1)} %get-tuple-element.58), channel_id=1, source_target_pairs={{0,4},{4,8},{8,12},{12,16},{16,20},{20,24},{24,28},{28,32},{32,36}... | collective-permute-start | bytes 98312 | tf_op jit(solution)/shard_map/ppermute | solution.py:21
  26.2 19.1 %copy-start.2 = (bf16[1,256,32]{1,2,0:T(8,128)(2,1)S(1)}, bf16[1,256,32]{1,2,0:T(8,128)(2,1)}, u32[]{:S(2)}) copy-start(bf16[1,256,32]{1,2,0:T(8,128)(2,1)} %param.15) | copy-start | bytes 49156
  26.2 74.6 %all-to-all-start = ((bf16[128,16,2,128]{3,2,1,0:T(2,128)(2,1)}), bf16[128,16,2,128]{3,2,1,0:T(2,128)(2,1)S(1)}, u32[]{:S(2)}, u32[]{:S(2)}) async-start(bf16[128,16,2,128]{3,2,1,0:T(2,128)(2,1)} %copy.22), calls=%async_computation | async-start | bytes 2097152 | tf_op jit(solution)/shard_map/all_to_all | solution.py:88
  172.7 0.8 copy-start.1
  172.7 11.7 %copy-start.4 = (f32[128]{0:T(128)S(1)}, f32[128]{0:T(128)}, u32[]{:S(2)}) copy-start(f32[128]{0:T(128)} %param.12) | copy-start | bytes 1540
  173.7 5.3 %collective-permute-start.4 = (f32[1,32,2,128]{3,2,1,0:T(2,128)S(1)}, f32[1,32,2,128]{3,2,1,0:T(2,128)S(1)}, u32[]{:S(2)}, u32[]{:S(2)}) collective-permute-start(f32[1,32,2,128]{3,2,1,0:T(2,128)S(1)} %get-tuple-element.55), channel_id=1, source_target_pairs={{4,0},{8,4},{12,8},{16,12},{20,16},{24,20},{28,24},{32,28},{36,32}... | collective-permute-start | bytes 98312 | tf_op jit(solution)/shard_map/ppermute | solution.py:23
  177.1 7.3 %collective-permute-start.5 = (f32[1,32,2,128]{3,2,1,0:T(2,128)S(1)}, f32[1,32,2,128]{3,2,1,0:T(2,128)S(1)}, u32[]{:S(2)}, u32[]{:S(2)}) collective-permute-start(f32[1,32,2,128]{3,2,1,0:T(2,128)S(1)} %get-tuple-element.56), channel_id=1, source_target_pairs={{0,4},{4,8},{8,12},{12,16},{16,20},{20,24},{24,28},{28,32},{32,36}... | collective-permute-start | bytes 98312 | tf_op jit(solution)/shard_map/ppermute | solution.py:21
  184.6 17.0 %collective-permute-start.6 = (f32[1,32,2,128]{3,2,1,0:T(2,128)S(1)}, f32[1,32,2,128]{3,2,1,0:T(2,128)S(1)}, u32[]{:S(2)}, u32[]{:S(2)}) collective-permute-start(f32[1,32,2,128]{3,2,1,0:T(2,128)S(1)} %get-tuple-element.53), channel_id=1, source_target_pairs={{4,0},{8,4},{12,8},{16,12},{20,16},{24,20},{28,24},{32,28},{36,32}... | collective-permute-start | bytes 98312 | tf_op jit(solution)/shard_map/ppermute | solution.py:23
  186.6 15.0 %collective-permute-start.7 = (f32[1,32,2,128]{3,2,1,0:T(2,128)S(1)}, f32[1,32,2,128]{3,2,1,0:T(2,128)S(1)}, u32[]{:S(2)}, u32[]{:S(2)}) collective-permute-start(f32[1,32,2,128]{3,2,1,0:T(2,128)S(1)} %get-tuple-element.54), channel_id=1, source_target_pairs={{0,4},{4,8},{8,12},{12,16},{16,20},{20,24},{24,28},{28,32},{32,36}... | collective-permute-start | bytes 98312 | tf_op jit(solution)/shard_map/ppermute | solution.py:21
where the time goes:
time: 204 us
  blocking collectives  73.2 us (36%)
  waiting for transfers between devices  67.2 us (33%)
  starting transfers between devices  38.6 us (19%)
  matrix products  10.1 us (5%)
  other arithmetic  5.97 us (3%)
  local copies, waits for them, and re-layouts  5.19 us (3%)
  between operations  2.76 us (1%)
    all_to_all x1, blocking collectives, body(): lax.all_to_all(adjoints_here, 'tile', split_axis=0, concat_axis=0, tiled=...  61.9 us
    all_to_all x1, waiting for transfers between devices, body(): lax.all_to_all(outgoing, 'tile', split_axis=0, concat_axis=0, tiled=True)  53 us
    all_to_all x1, starting transfers between devices, body(): lax.all_to_all(outgoing, 'tile', split_axis=0, concat_axis=0, tiled=True)  19.1 us
    ppermute x4, waiting for transfers between devices, padded_2(): lax.ppermute(tail, axis, [(i, (i + 1) % count) for i in range(count)])  14.2 us
    psum x1, blocking collectives, body(): totals = lax.psum(section_part, 'lev')  11.3 us
    ppermute x4, starting transfers between devices, padded_2(): lax.ppermute(head, axis, [((i + 1) % count, i) for i in range(count)])  10.9 us
    ppermute x4, starting transfers between devices, padded_2(): lax.ppermute(tail, axis, [(i, (i + 1) % count) for i in range(count)])  8.65 us
    dot_general x16, matrix products, respond(): jnp.dot(weighted.astype(jnp.bfloat16), dense_map, preferred_element_type=...  5.18 us
  transfers between devices with their start and end apart: 9, of which 4 were waited for; matrix products, arithmetic and copies ran while one was open for 2% of the time, Pallas kernels for 0%

commit v1 on v0

v1 whole, which is shorter than its diff:
```python
import jax
import jax.numpy as jnp
from jax import lax
from jax.experimental import pallas as pl
from jax.experimental.pallas import tpu as pltpu
from jax.sharding import PartitionSpec as P

NSTEP = 2
ZS, XS, CS = 16, 4, 2
QS = XS * CS


def tile_groups(sizes, free):
    groups = {}
    for z in range(sizes[0]):
        for x in range(sizes[1]):
            for c in range(sizes[2]):
                key = tuple(v for i, v in enumerate((z, x, c)) if i not in free)
                groups.setdefault(key, []).append((z * sizes[1] + x) * sizes[2] + c)
    return list(groups.values())


def laplace_step(ext, diffusivity):
    middle = ext[:, 1:-1]
    padded = jnp.pad(middle, ((0, 0), (0, 0), (1, 1), (0, 0)))
    laplace = ext[:, 2:] + ext[:, :-2] + padded[:, :, 2:] + padded[:, :, :-2] - 4.0 * middle
    return middle + diffusivity * laplace


def halo(field, width):
    count = lax.axis_size("tile")
    before = lax.ppermute(field[:, -width:], "tile", [(i, (i + 1) % count) for i in range(count)])
    after = lax.ppermute(field[:, :width], "tile", [((i + 1) % count, i) for i in range(count)])
    return before, after


def smooth(field, diffusivity):
    before, after = halo(field, NSTEP)
    ext = jnp.concatenate([before, field, after], axis=1).astype(jnp.float32)
    for _ in range(NSTEP):
        ext = laplace_step(ext, diffusivity)
    return ext


def band_columns(jac, offsets):
    band, ch = jac.shape

    def zeros(n):
        return jnp.zeros((n, ch), jac.dtype)

    x = jnp.concatenate([jac, zeros(8)], axis=0)
    for shift in (1, 2, 4):
        x = jnp.where((offsets & shift) != 0, pltpu.roll(x, shift, 0), x)
    for shift in (8, 16, 32):
        down = jnp.concatenate([zeros(shift), x], axis=0)
        stay = jnp.concatenate([x, zeros(shift)], axis=0)
        x = jnp.where((offsets & shift) != 0, down, stay)
    far = (offsets & 64) != 0
    top = jnp.where(far, zeros(64), x[:64])
    low = jnp.where(far, x[:64], jnp.concatenate([x[64:96], zeros(32)], axis=0))
    return jnp.concatenate([top, low], axis=0)


def respond_kernel(me_ref, gathered, jac, off, wts, mine, other, energy, sel, rows, adj):
    tiles, cells_ext, width = gathered.shape
    cells = sel.shape[1]
    sections = jac.shape[0]
    lev = width // 2
    slot = rows.shape[1] // sections
    me = me_ref[0]
    cell_id = lax.broadcasted_iota(jnp.int32, (cells, rows.shape[1]), 0).astype(jnp.float32)
    pick = lax.broadcasted_iota(jnp.int32, (tiles, width), 0) == me
    for q in range(tiles):
        block = gathered[q, cells : cells + tiles, :].astype(jnp.float32)
        target = jnp.sum(jnp.where(pick, block, 0.0), axis=0, keepdims=True)
        chosen = jnp.where(cell_id == target, 1.0, 0.0).astype(jnp.bfloat16)
        sel[q] = chosen
        rows[q] = lax.dot_general(
            chosen,
            gathered[q, :cells, :],
            (((0,), (0,)), ((), ())),
            preferred_element_type=jnp.float32,
        ).astype(jnp.bfloat16)
    for s in range(sections):
        band = band_columns(jac[s].astype(jnp.float32), off[s : s + 1, :]).astype(jnp.bfloat16)
        here = slice(s * slot, (s + 1) * slot)
        weight = wts[s : s + 1, :]
        total = jnp.zeros((1, band.shape[1]), jnp.float32)
        for h in range(2):
            span = range(h * tiles // 2, (h + 1) * tiles // 2)
            mine_rows = jnp.concatenate(
                [rows[q, here, p * lev : (p + 1) * lev] for q in span for p in range(2)], axis=0
            )
            bright = jnp.dot(mine_rows, band, preferred_element_type=jnp.float32)
            weighted = weight * bright
            total = total + jnp.sum(bright * weighted, axis=0, keepdims=True)
            back = lax.dot_general(
                weighted.astype(jnp.bfloat16),
                band,
                (((1,), (1,)), ((), ())),
                preferred_element_type=jnp.float32,
            ).astype(jnp.bfloat16)
            at = 0
            for q in span:
                for p in range(2):
                    adj[q, here, p * lev : (p + 1) * lev] = back[at : at + slot]
                    at += slot
        energy[s : s + 1, :] = total
    for j in range(tiles // 2):
        for half, out in ((0, mine), (1, other)):
            q = 2 * j + jnp.where(half == 0, me % 2, 1 - me % 2)
            out[j] = jnp.dot(sel[q], adj[q], preferred_element_type=jnp.float32)


def respond_all(me, gathered, jac, off, wts):
    tiles, cells_ext, width = gathered.shape
    cells = cells_ext - tiles
    sections = jac.shape[0]
    part = jax.ShapeDtypeStruct((tiles // 2, cells, width), jnp.float32)
    vmem = pl.BlockSpec(memory_space=pltpu.VMEM)
    return pl.pallas_call(
        respond_kernel,
        out_shape=(part, part, jax.ShapeDtypeStruct((sections, wts.shape[1]), jnp.float32)),
        in_specs=[pl.BlockSpec(memory_space=pltpu.SMEM), vmem, vmem, vmem, vmem],
        out_specs=(vmem, vmem, vmem),
        scratch_shapes=[
            pltpu.VMEM((tiles, cells, 256), jnp.bfloat16),
            pltpu.VMEM((tiles, 256, width), jnp.bfloat16),
            pltpu.VMEM((tiles, 256, width), jnp.bfloat16),
        ],
        name="respond",
    )(me, gathered, jac, off, wts)


def body(probes, stddev, diffusivity, counts, columns, jacobian, offsets, obs_weights):
    tile_count = lax.axis_size("tile")
    row_count, col_count, probe_count, levels = probes.shape
    slot_count = columns.shape[2]
    channels = jacobian.shape[1]
    cell_count = row_count * col_count
    sizes = (ZS, XS, CS)
    along_z = tile_groups(sizes, (0,))
    along_x = tile_groups(sizes, (1,))
    plane = tile_groups(sizes, (1, 2))
    here = lax.axis_index("tile")
    me = here % QS
    own = jnp.swapaxes(jacobian, 1, 2)
    jac = lax.all_to_all(
        jnp.broadcast_to(own, (ZS,) + own.shape[1:]),
        "tile", 0, 0, axis_index_groups=along_z, tiled=True,
    )
    live = jnp.arange(slot_count, dtype=jnp.int32)[None, :] < counts[0][:, None]
    target = jnp.where(live, columns[0], -1).astype(jnp.bfloat16)
    target = target.reshape(ZS, QS, slot_count).swapaxes(0, 1).reshape(QS, ZS * slot_count)
    field = probes.transpose(2, 0, 1, 3)
    profile = (stddev[None] * smooth(field, diffusivity)).astype(jnp.bfloat16)
    profile = profile.transpose(1, 2, 0, 3).reshape(cell_count, probe_count * levels)
    gathered = lax.all_gather(
        jnp.concatenate([profile, target], axis=0)[None],
        "tile", axis=0, axis_index_groups=plane, tiled=True,
    )
    off = lax.dynamic_index_in_dim(offsets.reshape(ZS, QS, channels), me, 1, keepdims=False)
    wts = lax.dynamic_index_in_dim(obs_weights.reshape(ZS, QS, channels), me, 1, keepdims=False)
    mine, other, energy = respond_all(me.reshape(1), gathered, jac, off, wts)
    lev_count = lax.axis_size("lev")
    along_zy = [[t * lev_count + y for t in group for y in range(lev_count)] for group in along_z]
    spread = jnp.repeat(jnp.sum(energy, axis=1), lev_count)
    shares = lax.all_to_all(spread, ("tile", "lev"), 0, 0, axis_index_groups=along_zy, tiled=True)
    trace_share = (
        jnp.sum(shares) * (1.0 / (probe_count * lev_count * tile_count * slot_count * channels))
    ).reshape(1)
    summed = mine + lax.ppermute(other, "tile", [(i, i ^ 1) for i in range(tile_count)])
    parts = lax.all_to_all(summed, "tile", 0, 0, axis_index_groups=along_x, tiled=True)
    gradient = jnp.sum(parts, axis=0).reshape(row_count, col_count, probe_count, levels)
    hessian = smooth(stddev[None] * gradient.transpose(2, 0, 1, 3), diffusivity)
    return (hessian.transpose(1, 2, 0, 3), trace_share)


def solution(mesh):
    placed = (
        P("tile", None, "lev", None),
        P("tile", None, None),
        P(),
        P("tile", None),
        P("tile", None, None),
        P("tile", None, None),
        P(),
        P(),
    )
    return jax.shard_map(
        body,
        mesh=mesh,
        in_specs=placed,
        out_specs=(P("tile", None, "lev", None), P("tile")),
        check_vma=False,
    )
```

time: 204 us -> 112 us (0.55)
  the two profiles are of different devices: /device:TPU:32 before, /device:TPU:8 now
where the time goes in v1:
time: 112 us; the launch traced here: 111 us
  blocking collectives  56 us (50%)
  starting transfers between devices  35.2 us (31%)
  local copies, waits for them, and re-layouts  7.25 us (6%)
  other arithmetic  4.36 us (4%)
  Pallas kernels  4.05 us (4%)
  between operations  2.72 us (2%)
  waiting for transfers between devices  1.77 us (2%)
    all_to_all x1, blocking collectives, body(): lax.all_to_all(spread, ('tile', 'lev'), 0, 0, axis_index_groups=along_zy,...  29.1 us
    ppermute x2, starting transfers between devices, halo(): lax.ppermute(field[:, :width], 'tile', [((i + 1) % count, i) for i in ran...  20 us
    all_gather x1, blocking collectives, body(): lax.all_gather(jnp.concatenate([profile, target], axis=0)[None], 'tile',...  14.2 us
    all_to_all x1, blocking collectives, body(): lax.all_to_all(summed, 'tile', 0, 0, axis_index_groups=along_x, tiled=True)  12.7 us
    all_to_all x1, starting transfers between devices, body(): lax.all_to_all(jnp.broadcast_to(own, (ZS,) + own.shape[1:]), 'tile', 0, 0...  9.12 us
    unnamed x23, local copies, waits for them, and re-layouts  4.23 us
    pallas_call x1, Pallas kernels, respond_all(): pl.pallas_call(respond_kernel, out_shape=(part, part, jax.ShapeDtypeStruc...  4.05 us
    ppermute x2, starting transfers between devices, halo(): lax.ppermute(field[:, -width:], 'tile', [(i, (i + 1) % count) for i in ra...  3.84 us
  transfers between devices with their start and end apart: 6, of which 1 were waited for; matrix products, arithmetic and copies ran while one was open for 5% of the time, Pallas kernels for 0%

profile of v1, /device:TPU:8, one launch (start us, length us, event | category | flops | bytes accessed | tf_op | source)
XLA Modules:
  0.0 111.4 jit_solution(12950198284935569447)
XLA Ops:
  0.6 0.0 copy-start
  0.6 0.0 copy-start.4
  0.7 0.9 fusion.15
  1.5 1.9 %collective-permute-start = (bf16[2,2,32,128]{3,0,2,1:T(2,128)(2,1)S(1)}, bf16[2,2,32,128]{3,0,2,1:T(2,128)(2,1)S(1)}, u32[]{:S(2)}, u32[]{:S(2)}) collective-permute-start(bf16[2,2,32,128]{3,0,2,1:T(2,128)(2,1)S(1)} %get-tuple-element.10), channel_id=1, source_target_pairs={{0,4},{4,8},{8,12},{12,16},{16,20},{20,24},{24,28},{28,32},{32,36}... | collective-permute-start | bytes 98312 | tf_op jit(solution)/shard_map/ppermute | solution.py:32
  3.4 13.0 %collective-permute-start.1 = (bf16[2,2,32,128]{3,0,2,1:T(2,128)(2,1)S(1)}, bf16[2,2,32,128]{3,0,2,1:T(2,128)(2,1)S(1)}, u32[]{:S(2)}, u32[]{:S(2)}) collective-permute-start(bf16[2,2,32,128]{3,0,2,1:T(2,128)(2,1)S(1)} %get-tuple-element.11), channel_id=1, source_target_pairs={{4,0},{8,4},{12,8},{16,12},{20,16},{24,20},{28,24},{32,28},{36,32}... | collective-permute-start | bytes 98312 | tf_op jit(solution)/shard_map/ppermute | solution.py:33
  16.5 0.0 copy-done.4
  16.5 0.7 broadcast_in_dim.27
  17.2 9.1 %all-to-all-start = ((bf16[16,32,256]{2,1,0:T(8,128)(2,1)}), bf16[16,32,256]{2,1,0:T(8,128)(2,1)S(1)}, u32[]{:S(2)}, u32[]{:S(2)}) async-start(bf16[16,32,256]{2,1,0:T(8,128)(2,1)} %broadcast_in_dim.27), calls=%async_computation | async-start | bytes 524288 | tf_op jit(solution)/shard_map/all_to_all | solution.py:148
  26.4 0.0 copy-start.8
  26.4 0.0 copy-start.6
  26.4 0.5 broadcast.33
  26.9 0.1 copy-done.8
  27.0 0.7 reduce.4
  27.7 0.1 lt.30
  27.8 0.0 copy-done.6
  27.8 0.1 copy.20
  27.9 0.0 copy-done
  27.9 0.1 fusion.13
  28.0 0.9 constant_dynamic-slice_fusion
  28.9 0.6 copy.33
  29.6 0.0 copy-start.3
  29.6 0.6 copy.32
  30.2 0.1 reshape.44
  30.3 0.0 collective-permute-done
  30.3 0.0 collective-permute-done.1
  30.3 0.1 copy-done.3
  30.4 0.2 maximum_convert_fusion
  30.6 0.0 copy-start.7
  30.6 0.6 copy-done.7
  31.2 0.2 multiply_add_fusion.1
  31.4 0.0 copy-start.2
  31.4 0.8 copy-done.2
  32.2 0.2 multiply_convert_fusion
  32.4 14.2 %all-gather = bf16[1088,256]{1,0:T(8,128)(2,1)} all-gather(bf16[136,256]{1,0:T(8,128)(2,1)S(1)} %pad_maximum_fusion.2), channel_id=2, replica_groups={{0,4,8,12,16,20,24,28},{32,36,40,44,48,52,56,60},{64,68,72,76,80,84,88,..., dimensions={0}, use_global_device_ids=true | all-gather | bytes 626688 | tf_op jit(solution)/shard_map/all_gather | solution.py:158
  46.7 0.0 all-to-all-done.jac
  46.7 0.0 copy-start.1
  46.7 0.7 copy-done.1
  47.4 4.1 %respond.1 = (f32[4,128,256]{2,1,0:T(8,128)}, f32[4,128,256]{2,1,0:T(8,128)}, f32[16,256]{1,0:T(8,128)}) custom-call(s32[1]{0:T(128)} %bitcast.me_ref, bf16[8,136,256]{2,1,0:T(8,128)(2,1)} %bitcast.34, bf16[16,32,256]{2,1,0:T(8,128)(2,1)} %copy-done.1, s32[16,256]{1,0:T(8,128)} %bitcast.39, f32[16,256]{1,0:T(8,128)} %bitcast.40), custom_call_target="tpu_custom_call" | custom-call | tf_op jit(solution)/shard_map/respond/pallas_call | solution.py:121
  51.4 2.2 %collective-permute-start.2 = (f32[4,128,256]{2,1,0:T(8,128)}, f32[4,128,256]{2,1,0:T(8,128)S(1)}, u32[]{:S(2)}, u32[]{:S(2)}) collective-permute-start(f32[4,128,256]{2,1,0:T(8,128)} %get-tuple-element.6), channel_id=1, source_target_pairs={{0,4},{4,0},{8,12},{12,8},{16,20},{20,16},{24,28},{28,24},{32,36},... | collective-permute-start | bytes 1572872 | tf_op jit(solution)/shard_map/ppermute | solution.py:172
  53.7 1.8 %collective-permute-done.2 = f32[4,128,256]{2,1,0:T(8,128)S(1)} collective-permute-done((f32[4,128,256]{2,1,0:T(8,128)}, f32[4,128,256]{2,1,0:T(8,128)S(1)}, u32[]{:S(2)}, u32[]{:S(2)}) %collective-permute-start.2) | collective-permute-done | bytes 524320 | tf_op jit(solution)/shard_map/ppermute | solution.py:172
  55.4 1.1 add.79
  56.5 12.7 %all_to_all.20 = f32[4,128,256]{2,1,0:T(8,128)S(1)} all-to-all(f32[4,128,256]{2,1,0:T(8,128)S(1)} %add.79), channel_id=1, replica_groups={{0,8,16,24},{4,12,20,28},{32,40,48,56},{36,44,52,60},{64,72,80,88},{68,..., dimensions={0} | all-to-all | bytes 1048576 | tf_op jit(solution)/shard_map/all_to_all | solution.py:173
  69.2 0.1 reshape.47
  69.3 0.1 multiply_bitcast_fusion
  69.4 0.0 copy-start.5
  69.4 1.9 %collective-permute-start.3 = (f32[2,2,32,128]{3,0,2,1:T(2,128)S(1)}, f32[2,2,32,128]{3,0,2,1:T(2,128)S(1)}, u32[]{:S(2)}, u32[]{:S(2)}) collective-permute-start(f32[2,2,32,128]{3,0,2,1:T(2,128)S(1)} %get-tuple-element.8), channel_id=1, source_target_pairs={{0,4},{4,8},{8,12},{12,16},{16,20},{20,24},{24,28},{28,32},{32,36}... | collective-permute-start | bytes 196616 | tf_op jit(solution)/shard_map/ppermute | solution.py:32
  71.4 7.0 %collective-permute-start.4 = (f32[2,2,32,128]{3,0,2,1:T(2,128)S(1)}, f32[2,2,32,128]{3,0,2,1:T(2,128)S(1)}, u32[]{:S(2)}, u32[]{:S(2)}) collective-permute-start(f32[2,2,32,128]{3,0,2,1:T(2,128)S(1)} %get-tuple-element.9), channel_id=1, source_target_pairs={{4,0},{8,4},{12,8},{16,12},{20,16},{24,20},{28,24},{32,28},{36,32}... | collective-permute-start | bytes 196616 | tf_op jit(solution)/shard_map/ppermute | solution.py:33
  78.3 0.0 copy-done.5
  78.3 0.1 reduce_sum.28
  78.5 0.1 broadcast_in_dim.28
  78.5 0.1 all_to_all.16
  78.6 29.1 %all_to_all.21 = f32[64,1,1]{2,1,0:T(1,128)S(1)} all-to-all(f32[64,1,1]{2,1,0:T(1,128)S(1)} %all_to_all.16), channel_id=1, replica_groups={{0,1,2,3,32,33,34,35,64,65,66,67,96,97,98,99,128,129,130,131,160,161,16..., dimensions={0} | all-to-all | bytes 512 | tf_op jit(solution)/shard_map/all_to_all | solution.py:168
  107.8 0.7 reduce_sum.29
  109.1 0.0 collective-permute-done.3
  109.1 0.0 collective-permute-done.4
  109.1 0.1 pad_maximum_fusion
  109.2 0.2 multiply_add_fusion
  109.5 0.8 add_bitcast_fusion
  (9 shorter events, 0.1 us)
Async XLA Ops:
  0.6 27.3 %copy-start = (s32[128,256]{1,0:T(8,128)S(1)}, s32[128,256]{1,0:T(8,128)}, u32[]{:S(2)}) copy-start(s32[128,256]{1,0:T(8,128)} %param.14) | copy-start | bytes 393220
  0.6 15.9 %copy-start.4 = (bf16[1,256,32]{1,2,0:T(8,128)(2,1)S(1)}, bf16[1,256,32]{1,2,0:T(8,128)(2,1)}, u32[]{:S(2)}) copy-start(bf16[1,256,32]{1,2,0:T(8,128)(2,1)} %param.13) | copy-start | bytes 49156
  1.5 28.7 %collective-permute-start = (bf16[2,2,32,128]{3,0,2,1:T(2,128)(2,1)S(1)}, bf16[2,2,32,128]{3,0,2,1:T(2,128)(2,1)S(1)}, u32[]{:S(2)}, u32[]{:S(2)}) collective-permute-start(bf16[2,2,32,128]{3,0,2,1:T(2,128)(2,1)S(1)} %get-tuple-element.10), channel_id=1, source_target_pairs={{0,4},{4,8},{8,12},{12,16},{16,20},{20,24},{24,28},{28,32},{32,36}... | collective-permute-start | bytes 98312 | tf_op jit(solution)/shard_map/ppermute | solution.py:32
  3.4 26.8 %collective-permute-start.1 = (bf16[2,2,32,128]{3,0,2,1:T(2,128)(2,1)S(1)}, bf16[2,2,32,128]{3,0,2,1:T(2,128)(2,1)S(1)}, u32[]{:S(2)}, u32[]{:S(2)}) collective-permute-start(bf16[2,2,32,128]{3,0,2,1:T(2,128)(2,1)S(1)} %get-tuple-element.11), channel_id=1, source_target_pairs={{4,0},{8,4},{12,8},{16,12},{20,16},{24,20},{28,24},{32,28},{36,32}... | collective-permute-start | bytes 98312 | tf_op jit(solution)/shard_map/ppermute | solution.py:33
  17.2 29.4 %all-to-all-start = ((bf16[16,32,256]{2,1,0:T(8,128)(2,1)}), bf16[16,32,256]{2,1,0:T(8,128)(2,1)S(1)}, u32[]{:S(2)}, u32[]{:S(2)}) async-start(bf16[16,32,256]{2,1,0:T(8,128)(2,1)} %broadcast_in_dim.27), calls=%async_computation | async-start | bytes 524288 | tf_op jit(solution)/shard_map/all_to_all | solution.py:148
  26.4 0.7 copy-start.8
  26.4 1.4 %copy-start.6 = (s32[1,128,16]{1,2,0:T(8,128)S(1)}, s32[1,128,16]{1,2,0:T(8,128)}, u32[]{:S(2)}) copy-start(s32[1,128,16]{1,2,0:T(8,128)} %param.12) | copy-start | bytes 24580
  29.6 0.8 copy-start.3
  30.6 0.7 copy-start.7
  31.4 0.8 copy-start.2
  46.7 0.7 copy-start.1
  51.4 4.0 %collective-permute-start.2 = (f32[4,128,256]{2,1,0:T(8,128)}, f32[4,128,256]{2,1,0:T(8,128)S(1)}, u32[]{:S(2)}, u32[]{:S(2)}) collective-permute-start(f32[4,128,256]{2,1,0:T(8,128)} %get-tuple-element.6), channel_id=1, source_target_pairs={{0,4},{4,0},{8,12},{12,8},{16,20},{20,16},{24,28},{28,24},{32,36},... | collective-permute-start | bytes 1572872 | tf_op jit(solution)/shard_map/ppermute | solution.py:172
  69.4 8.9 %copy-start.5 = (f32[16,256]{1,0:T(8,128)S(1)}, f32[16,256]{1,0:T(8,128)}, u32[]{:S(2)}) copy-start(f32[16,256]{1,0:T(8,128)} %get-tuple-element.7) | copy-start | bytes 49156
  69.4 39.7 %collective-permute-start.3 = (f32[2,2,32,128]{3,0,2,1:T(2,128)S(1)}, f32[2,2,32,128]{3,0,2,1:T(2,128)S(1)}, u32[]{:S(2)}, u32[]{:S(2)}) collective-permute-start(f32[2,2,32,128]{3,0,2,1:T(2,128)S(1)} %get-tuple-element.8), channel_id=1, source_target_pairs={{0,4},{4,8},{8,12},{12,16},{16,20},{20,24},{24,28},{28,32},{32,36}... | collective-permute-start | bytes 196616 | tf_op jit(solution)/shard_map/ppermute | solution.py:32
  71.4 37.8 %collective-permute-start.4 = (f32[2,2,32,128]{3,0,2,1:T(2,128)S(1)}, f32[2,2,32,128]{3,0,2,1:T(2,128)S(1)}, u32[]{:S(2)}, u32[]{:S(2)}) collective-permute-start(f32[2,2,32,128]{3,0,2,1:T(2,128)S(1)} %get-tuple-element.9), channel_id=1, source_target_pairs={{4,0},{8,4},{12,8},{16,12},{20,16},{24,20},{28,24},{32,28},{36,32}... | collective-permute-start | bytes 196616 | tf_op jit(solution)/shard_map/ppermute | solution.py:33

commit v2 on v1

--- a/solution.py
+++ b/solution.py
@@ -29,9 +29,15 @@
 
 def halo(field, width):
     count = lax.axis_size("tile")
-    before = lax.ppermute(field[:, -width:], "tile", [(i, (i + 1) % count) for i in range(count)])
-    after = lax.ppermute(field[:, :width], "tile", [((i + 1) % count, i) for i in range(count)])
-    return before, after
+    even = (lax.axis_index("tile") & 1) == 0
+    top, bottom = field[:, :width], field[:, -width:]
+    cross = lax.ppermute(
+        jnp.where(even, top, bottom),
+        "tile",
+        [(i, (i - 1 if i % 2 == 0 else i + 1) % count) for i in range(count)],
+    )
+    near = lax.ppermute(jnp.where(even, bottom, top), "tile", [(i, i ^ 1) for i in range(count)])
+    return jnp.where(even, cross, near), jnp.where(even, near, cross)
 
 
 def smooth(field, diffusivity):
@@ -82,9 +88,10 @@
             preferred_element_type=jnp.float32,
         ).astype(jnp.bfloat16)
     for s in range(sections):
-        band = band_columns(jac[s].astype(jnp.float32), off[s : s + 1, :]).astype(jnp.bfloat16)
+        row = pl.ds(s * tiles + me, 1)
+        band = band_columns(jac[s].astype(jnp.float32), off[row, :]).astype(jnp.bfloat16)
         here = slice(s * slot, (s + 1) * slot)
-        weight = wts[s : s + 1, :]
+        weight = wts[row, :]
         total = jnp.zeros((1, band.shape[1]), jnp.float32)
         for h in range(2):
             span = range(h * tiles // 2, (h + 1) * tiles // 2)
@@ -105,14 +112,17 @@
                 for p in range(2):
                     adj[q, here, p * lev : (p + 1) * lev] = back[at : at + slot]
                     at += slot
-        energy[s : s + 1, :] = total
+        each = energy.shape[0] // sections
+        energy[s * each : (s + 1) * each] = jnp.broadcast_to(
+            jnp.sum(total, axis=1, keepdims=True)[None], (each,) + energy.shape[1:]
+        )
     for j in range(tiles // 2):
         for half, out in ((0, mine), (1, other)):
-            q = 2 * j + jnp.where(half == 0, me % 2, 1 - me % 2)
+            q = 2 * j + ((me & 1) if half == 0 else 1 - (me & 1))
             out[j] = jnp.dot(sel[q], adj[q], preferred_element_type=jnp.float32)
 
 
-def respond_all(me, gathered, jac, off, wts):
+def respond_all(me, gathered, jac, off, wts, copies):
     tiles, cells_ext, width = gathered.shape
     cells = cells_ext - tiles
     sections = jac.shape[0]
@@ -120,7 +130,7 @@
     vmem = pl.BlockSpec(memory_space=pltpu.VMEM)
     return pl.pallas_call(
         respond_kernel,
-        out_shape=(part, part, jax.ShapeDtypeStruct((sections, wts.shape[1]), jnp.float32)),
+        out_shape=(part, part, jax.ShapeDtypeStruct((sections * copies, 8, 128), jnp.float32)),
         in_specs=[pl.BlockSpec(memory_space=pltpu.SMEM), vmem, vmem, vmem, vmem],
         out_specs=(vmem, vmem, vmem),
         scratch_shapes=[
@@ -143,7 +153,7 @@
     along_x = tile_groups(sizes, (1,))
     plane = tile_groups(sizes, (1, 2))
     here = lax.axis_index("tile")
-    me = here % QS
+    me = here & (QS - 1)
     own = jnp.swapaxes(jacobian, 1, 2)
     jac = lax.all_to_all(
         jnp.broadcast_to(own, (ZS,) + own.shape[1:]),
@@ -159,19 +169,22 @@
         jnp.concatenate([profile, target], axis=0)[None],
         "tile", axis=0, axis_index_groups=plane, tiled=True,
     )
-    off = lax.dynamic_index_in_dim(offsets.reshape(ZS, QS, channels), me, 1, keepdims=False)
-    wts = lax.dynamic_index_in_dim(obs_weights.reshape(ZS, QS, channels), me, 1, keepdims=False)
-    mine, other, energy = respond_all(me.reshape(1), gathered, jac, off, wts)
     lev_count = lax.axis_size("lev")
+    mine, other, energy = respond_all(me.reshape(1), gathered, jac, offsets, obs_weights, lev_count)
     along_zy = [[t * lev_count + y for t in group for y in range(lev_count)] for group in along_z]
-    spread = jnp.repeat(jnp.sum(energy, axis=1), lev_count)
-    shares = lax.all_to_all(spread, ("tile", "lev"), 0, 0, axis_index_groups=along_zy, tiled=True)
+    shares = lax.all_to_all(energy, ("tile", "lev"), 0, 0, axis_index_groups=along_zy, tiled=True)
     trace_share = (
-        jnp.sum(shares) * (1.0 / (probe_count * lev_count * tile_count * slot_count * channels))
+        jnp.sum(shares[:, 0, 0])
+        * (1.0 / (probe_count * lev_count * tile_count * slot_count * channels))
     ).reshape(1)
     summed = mine + lax.ppermute(other, "tile", [(i, i ^ 1) for i in range(tile_count)])
-    parts = lax.all_to_all(summed, "tile", 0, 0, axis_index_groups=along_x, tiled=True)
-    gradient = jnp.sum(parts, axis=0).reshape(row_count, col_count, probe_count, levels)
+    x = (here >> 1) & (XS - 1)
+    gradient = lax.dynamic_index_in_dim(summed, x, 0, keepdims=False)
+    for step in range(1, XS):
+        ring = [(i, i // QS * QS + (i + step * CS) % QS) for i in range(tile_count)]
+        sent = lax.dynamic_index_in_dim(summed, (x + step) & (XS - 1), 0, keepdims=False)
+        gradient = gradient + lax.ppermute(sent, "tile", ring)
+    gradient = gradient.reshape(row_count, col_count, probe_count, levels)
     hessian = smooth(stddev[None] * gradient.transpose(2, 0, 1, 3), diffusivity)
     return (hessian.transpose(1, 2, 0, 3), trace_share)
 

time: 112 us -> 103 us (0.920)
  the two profiles are of different devices: /device:TPU:8 before, /device:TPU:2 now
where the time goes in v2:
time: 103 us; the launch traced here: 102 us
  starting transfers between devices  53.9 us (52%)
  waiting for transfers between devices  17.7 us (17%)
  blocking collectives  13.7 us (13%)
  other arithmetic  5.16 us (5%)
  local copies, waits for them, and re-layouts  4.79 us (5%)
  Pallas kernels  4.25 us (4%)
  between operations  2.73 us (3%)
    all_to_all x1, starting transfers between devices, body(): lax.all_to_all(energy, ('tile', 'lev'), 0, 0, axis_index_groups=along_zy,...  15.6 us
    all_to_all x1, starting transfers between devices, body(): lax.all_to_all(jnp.broadcast_to(own, (ZS,) + own.shape[1:]), 'tile', 0, 0...  15.3 us
    all_to_all x1, waiting for transfers between devices, body(): lax.all_to_all(energy, ('tile', 'lev'), 0, 0, axis_index_groups=along_zy,...  15 us
    all_gather x1, blocking collectives, body(): lax.all_gather(jnp.concatenate([profile, target], axis=0)[None], 'tile',...  13.7 us
    ppermute x3, starting transfers between devices, body(): gradient = gradient + lax.ppermute(sent, 'tile', ring)  10.4 us
    ppermute x2, starting transfers between devices, halo(): lax.ppermute(jnp.where(even, bottom, top), 'tile', [(i, i ^ 1) for i in r...  6.55 us
    pallas_call x1, Pallas kernels, respond_all(): pl.pallas_call(respond_kernel, out_shape=(part, part, jax.ShapeDtypeStruc...  4.25 us
    ppermute x2, starting transfers between devices, halo(): lax.ppermute(jnp.where(even, top, bottom), 'tile', [(i, (i - 1 if i % 2 =...  3.84 us
  transfers between devices with their start and end apart: 10, of which 4 were waited for; matrix products, arithmetic and copies ran while one was open for 4% of the time, Pallas kernels for 0%

profile of v2, /device:TPU:2, one launch (start us, length us, event | category | flops | bytes accessed | tf_op | source)
XLA Modules:
  0.0 102.3 jit_solution(6260637424188295641)
XLA Ops:
  0.6 0.0 copy-start.3
  0.6 0.8 broadcast_select_fusion.7
  1.5 1.9 %collective-permute-start = (bf16[2,2,32,128]{3,0,2,1:T(2,128)(2,1)S(1)}, bf16[2,2,32,128]{3,0,2,1:T(2,128)(2,1)S(1)}, u32[]{:S(2)}, u32[]{:S(2)}) collective-permute-start(bf16[2,2,32,128]{3,0,2,1:T(2,128)(2,1)S(1)} %get-tuple-element.17), channel_id=1, source_target_pairs={{0,508},{4,8},{8,4},{12,16},{16,12},{20,24},{24,20},{28,32},{32,28... | collective-permute-start | bytes 98312 | tf_op jit(solution)/shard_map/ppermute | solution.py:34
  3.4 3.5 %collective-permute-start.1 = (bf16[2,2,32,128]{3,0,2,1:T(2,128)(2,1)S(1)}, bf16[2,2,32,128]{3,0,2,1:T(2,128)(2,1)S(1)}, u32[]{:S(2)}, u32[]{:S(2)}) collective-permute-start(bf16[2,2,32,128]{3,0,2,1:T(2,128)(2,1)S(1)} %get-tuple-element.18), channel_id=1, source_target_pairs={{0,4},{4,0},{8,12},{12,8},{16,20},{20,16},{24,28},{28,24},{32,36},... | collective-permute-start | bytes 98312 | tf_op jit(solution)/shard_map/ppermute | solution.py:39
  6.9 0.0 copy-done.3
  6.9 0.7 broadcast_in_dim.24
  7.7 0.0 copy-start.4
  7.7 15.3 %all-to-all-start = ((bf16[16,32,256]{2,1,0:T(8,128)(2,1)}), bf16[16,32,256]{2,1,0:T(8,128)(2,1)S(1)}, u32[]{:S(2)}, u32[]{:S(2)}) async-start(bf16[16,32,256]{2,1,0:T(8,128)(2,1)} %broadcast_in_dim.24), calls=%async_computation | async-start | bytes 524288 | tf_op jit(solution)/shard_map/all_to_all | solution.py:158
  23.0 0.0 copy-done.4
  23.0 0.1 copy.12
  23.1 0.0 copy-start.6
  23.1 0.5 broadcast.32
  23.6 0.1 copy-done.6
  23.8 0.7 reduce.4
  24.4 0.1 lt.30
  24.5 0.1 fusion.15
  24.6 0.1 reshape.34
  24.7 0.0 collective-permute-done
  24.7 0.0 collective-permute-done.1
  24.8 0.0 copy-start.2
  24.8 0.8 copy-done.2
  25.6 0.2 maximum_convert_fusion
  25.8 0.0 copy-start.5
  25.8 0.6 copy-done.5
  26.4 0.2 multiply_add_fusion.1
  26.6 0.0 copy-start.1
  26.6 0.8 copy-done.1
  27.4 0.2 multiply_convert_fusion
  27.6 13.7 %all-gather = bf16[1088,256]{1,0:T(8,128)(2,1)} all-gather(bf16[136,256]{1,0:T(8,128)(2,1)S(1)} %pad_maximum_fusion.2), channel_id=2, replica_groups={{0,4,8,12,16,20,24,28},{32,36,40,44,48,52,56,60},{64,68,72,76,80,84,88,..., dimensions={0}, use_global_device_ids=true | all-gather | bytes 626688 | tf_op jit(solution)/shard_map/all_gather | solution.py:168
  41.4 0.0 all-to-all-done.jac
  41.4 0.0 copy-start
  41.4 0.7 copy-done
  42.1 4.3 %respond.1 = (f32[4,128,256]{2,1,0:T(8,128)}, f32[4,128,256]{2,1,0:T(8,128)}, f32[64,8,128]{2,1,0:T(8,128)}) custom-call(s32[1]{0:T(128)} %bitcast.me_ref, bf16[8,136,256]{2,1,0:T(8,128)(2,1)} %bitcast.45, bf16[16,32,256]{2,1,0:T(8,128)(2,1)} %copy-done, s32[128,256]{1,0:T(8,128)} %off.1, f32[128,256]{1,0:T(8,128)} %wts.1), custom_call_target="tpu_custom_call" | custom-call | tf_op jit(solution)/shard_map/respond/pallas_call | solution.py:131
  46.3 2.2 %collective-permute-start.2 = (f32[4,128,256]{2,1,0:T(8,128)}, f32[4,128,256]{2,1,0:T(8,128)S(1)}, u32[]{:S(2)}, u32[]{:S(2)}) collective-permute-start(f32[4,128,256]{2,1,0:T(8,128)} %get-tuple-element.6), channel_id=1, source_target_pairs={{0,4},{4,0},{8,12},{12,8},{16,20},{20,16},{24,28},{28,24},{32,36},... | collective-permute-start | bytes 1572872 | tf_op jit(solution)/shard_map/ppermute | solution.py:180
  48.6 1.8 %collective-permute-done.2 = f32[4,128,256]{2,1,0:T(8,128)S(1)} collective-permute-done((f32[4,128,256]{2,1,0:T(8,128)}, f32[4,128,256]{2,1,0:T(8,128)S(1)}, u32[]{:S(2)}, u32[]{:S(2)}) %collective-permute-start.2) | collective-permute-done | bytes 524320 | tf_op jit(solution)/shard_map/ppermute | solution.py:180
  50.3 1.1 %add.98 = f32[4,128,256]{2,1,0:T(8,128)S(1)} add(f32[4,128,256]{2,1,0:T(8,128)} %get-tuple-element.5, f32[4,128,256]{2,1,0:T(8,128)S(1)} %collective-permute-done.2) | non-fusion elementwise | flops 131072 | bytes 1572864 | tf_op jit(solution)/shard_map/add | solution.py:180
  51.5 3.1 %collective-permute-start.3 = (f32[128,256]{1,0:T(8,128)S(1)}, f32[128,256]{1,0:T(8,128)S(1)}, u32[]{:S(2)}, u32[]{:S(2)}) collective-permute-start(f32[128,256]{1,0:T(8,128)S(1)} %get-tuple-element.8), channel_id=1, source_target_pairs={{0,8},{4,12},{8,16},{12,20},{16,24},{20,28},{24,0},{28,4},{32,40},... | collective-permute-start | bytes 393224 | tf_op jit(solution)/shard_map/ppermute | solution.py:186
  54.6 4.4 %collective-permute-start.4 = (f32[128,256]{1,0:T(8,128)S(1)}, f32[128,256]{1,0:T(8,128)S(1)}, u32[]{:S(2)}, u32[]{:S(2)}) collective-permute-start(f32[128,256]{1,0:T(8,128)S(1)} %get-tuple-element.10), channel_id=1, source_target_pairs={{0,16},{4,20},{8,24},{12,28},{16,0},{20,4},{24,8},{28,12},{32,48},... | collective-permute-start | bytes 393224 | tf_op jit(solution)/shard_map/ppermute | solution.py:186
  59.0 2.9 %collective-permute-start.5 = (f32[128,256]{1,0:T(8,128)S(1)}, f32[128,256]{1,0:T(8,128)S(1)}, u32[]{:S(2)}, u32[]{:S(2)}) collective-permute-start(f32[128,256]{1,0:T(8,128)S(1)} %get-tuple-element.9), channel_id=1, source_target_pairs={{0,24},{4,28},{8,0},{12,4},{16,8},{20,12},{24,16},{28,20},{32,56},... | collective-permute-start | bytes 393224 | tf_op jit(solution)/shard_map/ppermute | solution.py:186
  61.9 15.6 %all-to-all-start.1 = ((f32[64,8,128]{2,1,0:T(8,128)}), f32[64,8,128]{2,1,0:T(8,128)S(1)}, u32[]{:S(2)}, u32[]{:S(2)}) async-start(f32[64,8,128]{2,1,0:T(8,128)} %get-tuple-element.7), calls=%async_computation.1 | async-start | bytes 524288 | tf_op jit(solution)/shard_map/all_to_all | solution.py:175
  77.5 0.0 collective-permute-done.3
  77.5 0.0 collective-permute-done.4
  77.5 0.0 collective-permute-done.5
  77.6 0.1 reshape.35
  77.7 0.1 multiply_bitcast_fusion
  77.8 1.9 %collective-permute-start.6 = (f32[2,2,32,128]{3,0,2,1:T(2,128)S(1)}, f32[2,2,32,128]{3,0,2,1:T(2,128)S(1)}, u32[]{:S(2)}, u32[]{:S(2)}) collective-permute-start(f32[2,2,32,128]{3,0,2,1:T(2,128)S(1)} %get-tuple-element.13), channel_id=1, source_target_pairs={{0,508},{4,8},{8,4},{12,16},{16,12},{20,24},{24,20},{28,32},{32,28... | collective-permute-start | bytes 196616 | tf_op jit(solution)/shard_map/ppermute | solution.py:34
  79.7 3.0 %collective-permute-start.7 = (f32[2,2,32,128]{3,0,2,1:T(2,128)S(1)}, f32[2,2,32,128]{3,0,2,1:T(2,128)S(1)}, u32[]{:S(2)}, u32[]{:S(2)}) collective-permute-start(f32[2,2,32,128]{3,0,2,1:T(2,128)S(1)} %get-tuple-element.14), channel_id=1, source_target_pairs={{0,4},{4,0},{8,12},{12,8},{16,20},{20,16},{24,28},{28,24},{32,36},... | collective-permute-start | bytes 196616 | tf_op jit(solution)/shard_map/ppermute | solution.py:39
  82.8 0.6 collective-permute-done.6
  83.4 0.3 collective-permute-done.7
  83.7 0.1 pad_maximum_fusion
  83.8 0.2 multiply_add_fusion
  84.0 0.8 add_bitcast_fusion
  84.8 15.0 %all-to-all-done.1 = f32[64,8,128]{2,1,0:T(8,128)S(1)} async-done(((f32[64,8,128]{2,1,0:T(8,128)}), f32[64,8,128]{2,1,0:T(8,128)S(1)}, u32[]{:S(2)}, u32[]{:S(2)}) %all-to-all-start.1) | async-done | bytes 262176 | tf_op jit(solution)/shard_map/all_to_all | solution.py:175
  99.8 0.7 slice_reduce_fusion
  (11 shorter events, 0.2 us)
Async XLA Ops:
  0.6 6.3 %copy-start.3 = (bf16[1,256,32]{1,2,0:T(8,128)(2,1)S(1)}, bf16[1,256,32]{1,2,0:T(8,128)(2,1)}, u32[]{:S(2)}) copy-start(bf16[1,256,32]{1,2,0:T(8,128)(2,1)} %param.13) | copy-start | bytes 49156
  1.5 23.3 %collective-permute-start = (bf16[2,2,32,128]{3,0,2,1:T(2,128)(2,1)S(1)}, bf16[2,2,32,128]{3,0,2,1:T(2,128)(2,1)S(1)}, u32[]{:S(2)}, u32[]{:S(2)}) collective-permute-start(bf16[2,2,32,128]{3,0,2,1:T(2,128)(2,1)S(1)} %get-tuple-element.17), channel_id=1, source_target_pairs={{0,508},{4,8},{8,4},{12,16},{16,12},{20,24},{24,20},{28,32},{32,28... | collective-permute-start | bytes 98312 | tf_op jit(solution)/shard_map/ppermute | solution.py:34
  3.4 21.3 %collective-permute-start.1 = (bf16[2,2,32,128]{3,0,2,1:T(2,128)(2,1)S(1)}, bf16[2,2,32,128]{3,0,2,1:T(2,128)(2,1)S(1)}, u32[]{:S(2)}, u32[]{:S(2)}) collective-permute-start(bf16[2,2,32,128]{3,0,2,1:T(2,128)(2,1)S(1)} %get-tuple-element.18), channel_id=1, source_target_pairs={{0,4},{4,0},{8,12},{12,8},{16,20},{20,16},{24,28},{28,24},{32,36},... | collective-permute-start | bytes 98312 | tf_op jit(solution)/shard_map/ppermute | solution.py:39
  7.7 15.3 %copy-start.4 = (s32[1,128,16]{1,2,0:T(8,128)S(1)}, s32[1,128,16]{1,2,0:T(8,128)}, u32[]{:S(2)}) copy-start(s32[1,128,16]{1,2,0:T(8,128)} %param.12) | copy-start | bytes 24580
  7.7 33.7 %all-to-all-start = ((bf16[16,32,256]{2,1,0:T(8,128)(2,1)}), bf16[16,32,256]{2,1,0:T(8,128)(2,1)S(1)}, u32[]{:S(2)}, u32[]{:S(2)}) async-start(bf16[16,32,256]{2,1,0:T(8,128)(2,1)} %broadcast_in_dim.24), calls=%async_computation | async-start | bytes 524288 | tf_op jit(solution)/shard_map/all_to_all | solution.py:158
  23.1 0.7 copy-start.6
  24.8 0.8 copy-start.2
  25.8 0.7 copy-start.5
  26.6 0.8 copy-start.1
  41.4 0.7 copy-start
  46.3 4.0 %collective-permute-start.2 = (f32[4,128,256]{2,1,0:T(8,128)}, f32[4,128,256]{2,1,0:T(8,128)S(1)}, u32[]{:S(2)}, u32[]{:S(2)}) collective-permute-start(f32[4,128,256]{2,1,0:T(8,128)} %get-tuple-element.6), channel_id=1, source_target_pairs={{0,4},{4,0},{8,12},{12,8},{16,20},{20,16},{24,28},{28,24},{32,36},... | collective-permute-start | bytes 1572872 | tf_op jit(solution)/shard_map/ppermute | solution.py:180
  51.5 26.0 %collective-permute-start.3 = (f32[128,256]{1,0:T(8,128)S(1)}, f32[128,256]{1,0:T(8,128)S(1)}, u32[]{:S(2)}, u32[]{:S(2)}) collective-permute-start(f32[128,256]{1,0:T(8,128)S(1)} %get-tuple-element.8), channel_id=1, source_target_pairs={{0,8},{4,12},{8,16},{12,20},{16,24},{20,28},{24,0},{28,4},{32,40},... | collective-permute-start | bytes 393224 | tf_op jit(solution)/shard_map/ppermute | solution.py:186
  54.6 22.9 %collective-permute-start.4 = (f32[128,256]{1,0:T(8,128)S(1)}, f32[128,256]{1,0:T(8,128)S(1)}, u32[]{:S(2)}, u32[]{:S(2)}) collective-permute-start(f32[128,256]{1,0:T(8,128)S(1)} %get-tuple-element.10), channel_id=1, source_target_pairs={{0,16},{4,20},{8,24},{12,28},{16,0},{20,4},{24,8},{28,12},{32,48},... | collective-permute-start | bytes 393224 | tf_op jit(solution)/shard_map/ppermute | solution.py:186
  59.0 18.5 %collective-permute-start.5 = (f32[128,256]{1,0:T(8,128)S(1)}, f32[128,256]{1,0:T(8,128)S(1)}, u32[]{:S(2)}, u32[]{:S(2)}) collective-permute-start(f32[128,256]{1,0:T(8,128)S(1)} %get-tuple-element.9), channel_id=1, source_target_pairs={{0,24},{4,28},{8,0},{12,4},{16,8},{20,12},{24,16},{28,20},{32,56},... | collective-permute-start | bytes 393224 | tf_op jit(solution)/shard_map/ppermute | solution.py:186
  61.9 37.9 %all-to-all-start.1 = ((f32[64,8,128]{2,1,0:T(8,128)}), f32[64,8,128]{2,1,0:T(8,128)S(1)}, u32[]{:S(2)}, u32[]{:S(2)}) async-start(f32[64,8,128]{2,1,0:T(8,128)} %get-tuple-element.7), calls=%async_computation.1 | async-start | bytes 524288 | tf_op jit(solution)/shard_map/all_to_all | solution.py:175
  77.8 5.6 %collective-permute-start.6 = (f32[2,2,32,128]{3,0,2,1:T(2,128)S(1)}, f32[2,2,32,128]{3,0,2,1:T(2,128)S(1)}, u32[]{:S(2)}, u32[]{:S(2)}) collective-permute-start(f32[2,2,32,128]{3,0,2,1:T(2,128)S(1)} %get-tuple-element.13), channel_id=1, source_target_pairs={{0,508},{4,8},{8,4},{12,16},{16,12},{20,24},{24,20},{28,32},{32,28... | collective-permute-start | bytes 196616 | tf_op jit(solution)/shard_map/ppermute | solution.py:34
  79.7 3.9 %collective-permute-start.7 = (f32[2,2,32,128]{3,0,2,1:T(2,128)S(1)}, f32[2,2,32,128]{3,0,2,1:T(2,128)S(1)}, u32[]{:S(2)}, u32[]{:S(2)}) collective-permute-start(f32[2,2,32,128]{3,0,2,1:T(2,128)S(1)} %get-tuple-element.14), channel_id=1, source_target_pairs={{0,4},{4,0},{8,12},{12,8},{16,20},{20,16},{24,28},{28,24},{32,36},... | collective-permute-start | bytes 196616 | tf_op jit(solution)/shard_map/ppermute | solution.py:39

commit v3 on v2

--- a/solution.py
+++ b/solution.py
@@ -21,31 +21,102 @@
 
 
 def laplace_step(ext, diffusivity):
-    middle = ext[:, 1:-1]
-    padded = jnp.pad(middle, ((0, 0), (0, 0), (1, 1), (0, 0)))
-    laplace = ext[:, 2:] + ext[:, :-2] + padded[:, :, 2:] + padded[:, :, :-2] - 4.0 * middle
+    middle = ext[1:-1]
+    padded = jnp.pad(middle, ((0, 0), (1, 1), (0, 0), (0, 0)))
+    laplace = ext[2:] + ext[:-2] + padded[:, 2:] + padded[:, :-2] - 4.0 * middle
     return middle + diffusivity * laplace
 
 
-def halo(field, width):
+def edge_rows(field, width):
+    even = (lax.axis_index("tile") & 1) == 0
+    top, bottom = field[:width], field[-width:]
+    return jnp.where(even, top, bottom), jnp.where(even, bottom, top)
+
+
+def swap_edges(to_cross, to_near):
     count = lax.axis_size("tile")
+    across = [(i, (i - 1 if i % 2 == 0 else i + 1) % count) for i in range(count)]
+    cross = lax.ppermute(to_cross, "tile", across)
+    near = lax.ppermute(to_near, "tile", [(i, i ^ 1) for i in range(count)])
+    return cross, near
+
+
+def smooth(field, diffusivity):
+    cross, near = swap_edges(*edge_rows(field, NSTEP))
     even = (lax.axis_index("tile") & 1) == 0
-    top, bottom = field[:, :width], field[:, -width:]
-    cross = lax.ppermute(
-        jnp.where(even, top, bottom),
-        "tile",
-        [(i, (i - 1 if i % 2 == 0 else i + 1) % count) for i in range(count)],
-    )
-    near = lax.ppermute(jnp.where(even, bottom, top), "tile", [(i, i ^ 1) for i in range(count)])
-    return jnp.where(even, cross, near), jnp.where(even, near, cross)
-
-
-def smooth(field, diffusivity):
-    before, after = halo(field, NSTEP)
-    ext = jnp.concatenate([before, field, after], axis=1).astype(jnp.float32)
+    ext = jnp.concatenate(
+        [jnp.where(even, cross, near), field, jnp.where(even, near, cross)], axis=0
+    )
     for _ in range(NSTEP):
         ext = laplace_step(ext, diffusivity)
     return ext
+
+
+def profile_kernel(me_ref, field, cross, near, stddev, diffusivity, columns, counts, out):
+    tile_rows, cols, lev = stddev.shape
+    wide = 2 * cols
+    edge = cross.shape[0]
+    even = (me_ref[0] & 1) == 0
+    before = jnp.where(even, cross[...], near[...])
+    after = jnp.where(even, near[...], cross[...])
+    own = field[...]
+    left = lax.broadcasted_iota(jnp.int32, (wide, wide), 0)
+    right = lax.broadcasted_iota(jnp.int32, (wide, wide), 1)
+    split = jnp.where(
+        right == jnp.where(left < cols, 2 * left, 2 * (left - cols) + 1), 1.0, 0.0
+    ).astype(jnp.bfloat16)
+    grid = []
+    for block, count in ((before, edge // wide), (own, tile_rows), (after, edge // wide)):
+        for i in range(count):
+            grid.append(
+                jnp.dot(split, block[i * wide : (i + 1) * wide], preferred_element_type=jnp.float32)
+            )
+    place = lax.broadcasted_iota(jnp.int32, (wide, lev), 0) & (cols - 1)
+    rate = diffusivity[...]
+    for _ in range(NSTEP):
+        new = []
+        for i in range(1, len(grid) - 1):
+            middle = grid[i]
+            following = jnp.where(place == cols - 1, 0.0, pltpu.roll(middle, wide - 1, 0))
+            leading = jnp.where(place == 0, 0.0, pltpu.roll(middle, 1, 0))
+            laplace = grid[i + 1] + grid[i - 1] + following + leading - 4.0 * middle
+            new.append(middle + rate * laplace)
+        grid = new
+    for i in range(tile_rows):
+        for p in range(2):
+            out[i * cols : (i + 1) * cols, p * lev : (p + 1) * lev] = (
+                stddev[i] * grid[i][p * cols : (p + 1) * cols]
+            ).astype(jnp.bfloat16)
+    slots, sections = columns.shape
+    width = out.shape[1]
+    live = lax.broadcasted_iota(jnp.int32, (slots, sections), 0) < counts[...]
+    target = jnp.where(live, columns[...], -1).astype(jnp.float32).astype(jnp.bfloat16)
+    lane = lax.broadcasted_iota(jnp.int32, (sections, width), 1)
+    apart = lax.broadcasted_iota(jnp.int32, (sections, width), 0) - (lane >> 4) * QS
+    slot = lax.broadcasted_iota(jnp.int32, (slots, width), 0)
+    mine = slot == (lax.broadcasted_iota(jnp.int32, (slots, width), 1) & (slots - 1))
+    lines = []
+    for q in range(QS):
+        choose = jnp.where(apart == q, 1.0, 0.0).astype(jnp.bfloat16)
+        spread = jnp.dot(target, choose, preferred_element_type=jnp.float32)
+        lines.append(jnp.sum(jnp.where(mine, spread, 0.0), axis=0, keepdims=True))
+    out[tile_rows * cols :, :] = jnp.concatenate(lines, axis=0).astype(jnp.bfloat16)
+
+
+def in_vmem(*arrays):
+    return [pltpu.with_memory_space_constraint(a, pltpu.VMEM) for a in arrays]
+
+
+def profile_block(me, field, cross, near, stddev, diffusivity, columns, counts):
+    tile_rows, cols, lev = stddev.shape
+    vmem = pl.BlockSpec(memory_space=pltpu.VMEM)
+    return pl.pallas_call(
+        profile_kernel,
+        out_shape=pltpu.VMEM((tile_rows * cols + QS, 2 * lev), jnp.bfloat16),
+        in_specs=[pl.BlockSpec(memory_space=pltpu.SMEM)] + [vmem] * 7,
+        out_specs=vmem,
+        name="profile",
+    )(me, *in_vmem(field, cross, near, stddev, diffusivity, columns, counts))
 
 
 def band_columns(jac, offsets):
@@ -118,7 +189,7 @@
         )
     for j in range(tiles // 2):
         for half, out in ((0, mine), (1, other)):
-            q = 2 * j + ((me & 1) if half == 0 else 1 - (me & 1))
+            q = ((me + 2 * j) & (tiles - 1)) if half == 0 else (((me ^ 1) + 2 * j) & (tiles - 1))
             out[j] = jnp.dot(sel[q], adj[q], preferred_element_type=jnp.float32)
 
 
@@ -126,11 +197,11 @@
     tiles, cells_ext, width = gathered.shape
     cells = cells_ext - tiles
     sections = jac.shape[0]
-    part = jax.ShapeDtypeStruct((tiles // 2, cells, width), jnp.float32)
+    part = pltpu.VMEM((tiles // 2, cells, width), jnp.float32)
     vmem = pl.BlockSpec(memory_space=pltpu.VMEM)
     return pl.pallas_call(
         respond_kernel,
-        out_shape=(part, part, jax.ShapeDtypeStruct((sections * copies, 8, 128), jnp.float32)),
+        out_shape=(part, part, pltpu.VMEM((sections * copies, 4, 128), jnp.float32)),
         in_specs=[pl.BlockSpec(memory_space=pltpu.SMEM), vmem, vmem, vmem, vmem],
         out_specs=(vmem, vmem, vmem),
         scratch_shapes=[
@@ -139,7 +210,7 @@
             pltpu.VMEM((tiles, 256, width), jnp.bfloat16),
         ],
         name="respond",
-    )(me, gathered, jac, off, wts)
+    )(me, *in_vmem(gathered, jac, off, wts))
 
 
 def body(probes, stddev, diffusivity, counts, columns, jacobian, offsets, obs_weights):
@@ -154,39 +225,44 @@
     plane = tile_groups(sizes, (1, 2))
     here = lax.axis_index("tile")
     me = here & (QS - 1)
-    own = jnp.swapaxes(jacobian, 1, 2)
+    cross, near = swap_edges(*edge_rows(probes, NSTEP))
+    own = jnp.broadcast_to(jnp.swapaxes(jacobian, 1, 2), (ZS, jacobian.shape[2], channels))
+    own, cross, near = lax.optimization_barrier((own, cross, near))
     jac = lax.all_to_all(
-        jnp.broadcast_to(own, (ZS,) + own.shape[1:]),
+        own,
         "tile", 0, 0, axis_index_groups=along_z, tiled=True,
     )
-    live = jnp.arange(slot_count, dtype=jnp.int32)[None, :] < counts[0][:, None]
-    target = jnp.where(live, columns[0], -1).astype(jnp.bfloat16)
-    target = target.reshape(ZS, QS, slot_count).swapaxes(0, 1).reshape(QS, ZS * slot_count)
-    field = probes.transpose(2, 0, 1, 3)
-    profile = (stddev[None] * smooth(field, diffusivity)).astype(jnp.bfloat16)
-    profile = profile.transpose(1, 2, 0, 3).reshape(cell_count, probe_count * levels)
+    block = profile_block(
+        me.reshape(1),
+        probes.reshape(-1, levels),
+        cross.reshape(-1, levels),
+        near.reshape(-1, levels),
+        stddev,
+        diffusivity[None],
+        columns[0].T,
+        counts,
+    )
     gathered = lax.all_gather(
-        jnp.concatenate([profile, target], axis=0)[None],
+        block[None],
         "tile", axis=0, axis_index_groups=plane, tiled=True,
     )
     lev_count = lax.axis_size("lev")
     mine, other, energy = respond_all(me.reshape(1), gathered, jac, offsets, obs_weights, lev_count)
     along_zy = [[t * lev_count + y for t in group for y in range(lev_count)] for group in along_z]
     shares = lax.all_to_all(energy, ("tile", "lev"), 0, 0, axis_index_groups=along_zy, tiled=True)
+    summed = mine + lax.ppermute(other, "tile", [(i, i ^ 1) for i in range(tile_count)])
+    gradient = summed[0]
+    for step in range(1, XS):
+        ring = [(i, i // QS * QS + (i + step * CS) % QS) for i in range(tile_count)]
+        gradient = gradient + lax.ppermute(summed[step], "tile", ring)
+    gradient = gradient.reshape(row_count, col_count, probe_count, levels)
+    gradient, shares = lax.optimization_barrier((gradient, shares))
     trace_share = (
         jnp.sum(shares[:, 0, 0])
         * (1.0 / (probe_count * lev_count * tile_count * slot_count * channels))
     ).reshape(1)
-    summed = mine + lax.ppermute(other, "tile", [(i, i ^ 1) for i in range(tile_count)])
-    x = (here >> 1) & (XS - 1)
-    gradient = lax.dynamic_index_in_dim(summed, x, 0, keepdims=False)
-    for step in range(1, XS):
-        ring = [(i, i // QS * QS + (i + step * CS) % QS) for i in range(tile_count)]
-        sent = lax.dynamic_index_in_dim(summed, (x + step) & (XS - 1), 0, keepdims=False)
-        gradient = gradient + lax.ppermute(sent, "tile", ring)
-    gradient = gradient.reshape(row_count, col_count, probe_count, levels)
-    hessian = smooth(stddev[None] * gradient.transpose(2, 0, 1, 3), diffusivity)
-    return (hessian.transpose(1, 2, 0, 3), trace_share)
+    hessian = smooth(stddev[:, :, None, :] * gradient, diffusivity)
+    return (hessian, trace_share)
 
 
 def solution(mesh):

time: 103 us -> 91.6 us (0.89)
  the two profiles are of different devices: /device:TPU:2 before, /device:TPU:8 now
where the time goes in v3:
time: 91.6 us; the launch traced here: 91 us
  starting transfers between devices  52.9 us (58%)
  waiting for transfers between devices  15 us (16%)
  blocking collectives  13.3 us (15%)
  other arithmetic  2.84 us (3%)
  Pallas kernels  2.84 us (3%)
  between operations  2.67 us (3%)
  local copies, waits for them, and re-layouts  1.51 us (2%)
    ppermute x2, starting transfers between devices, swap_edges(): cross = lax.ppermute(to_cross, 'tile', across)  15.6 us
    all_to_all x1, starting transfers between devices, body(): lax.all_to_all(energy, ('tile', 'lev'), 0, 0, axis_index_groups=along_zy,...  13.7 us
    all_gather x1, blocking collectives, body(): lax.all_gather(block[None], 'tile', axis=0, axis_index_groups=plane, tile...  13.3 us
    ppermute x3, starting transfers between devices, body(): gradient = gradient + lax.ppermute(summed[step], 'tile', ring)  9.21 us
    all_to_all x1, starting transfers between devices, body(): lax.all_to_all(own, 'tile', 0, 0, axis_index_groups=along_z, tiled=True)  8.59 us
    ppermute x3, waiting for transfers between devices, body(): gradient = gradient + lax.ppermute(summed[step], 'tile', ring)  6.19 us
    ppermute x2, waiting for transfers between devices, swap_edges(): cross = lax.ppermute(to_cross, 'tile', across)  5.3 us
    ppermute x2, starting transfers between devices, swap_edges(): near = lax.ppermute(to_near, 'tile', [(i, i ^ 1) for i in range(count)])  3.84 us
  transfers between devices with their start and end apart: 10, of which 6 were waited for; matrix products, arithmetic and copies ran while one was open for 1% of the time, Pallas kernels for 0%

profile of v3, /device:TPU:8, one launch (start us, length us, event | category | flops | bytes accessed | tf_op | source)
XLA Modules:
  0.0 91.0 jit_solution(520039742265003125)
XLA Ops:
  0.6 0.0 copy-start.7
  0.6 0.8 broadcast_select_fusion.4
  1.5 1.9 %collective-permute-start.1 = (bf16[2,32,2,128]{3,2,1,0:T(2,128)(2,1)S(1)}, bf16[2,32,2,128]{3,2,1,0:T(2,128)(2,1)S(1)}, u32[]{:S(2)}, u32[]{:S(2)}) collective-permute-start(bf16[2,32,2,128]{3,2,1,0:T(2,128)(2,1)S(1)} %get-tuple-element.25), channel_id=1, source_target_pairs={{0,4},{4,0},{8,12},{12,8},{16,20},{20,16},{24,28},{28,24},{32,36},... | collective-permute-start | bytes 98312 | tf_op jit(solution)/shard_map/ppermute | solution.py:40
  3.4 13.7 %collective-permute-start = (bf16[2,32,2,128]{3,2,1,0:T(2,128)(2,1)S(1)}, bf16[2,32,2,128]{3,2,1,0:T(2,128)(2,1)S(1)}, u32[]{:S(2)}, u32[]{:S(2)}) collective-permute-start(bf16[2,32,2,128]{3,2,1,0:T(2,128)(2,1)S(1)} %get-tuple-element.26), channel_id=1, source_target_pairs={{0,508},{4,8},{8,4},{12,16},{16,12},{20,24},{24,20},{28,32},{32,28... | collective-permute-start | bytes 98312 | tf_op jit(solution)/shard_map/ppermute | solution.py:39
  17.1 0.0 collective-permute-done.1
  17.1 1.6 %collective-permute-done = bf16[2,32,2,128]{3,2,1,0:T(2,128)(2,1)S(1)} collective-permute-done((bf16[2,32,2,128]{3,2,1,0:T(2,128)(2,1)S(1)}, bf16[2,32,2,128]{3,2,1,0:T(2,128)(2,1)S(1)}, u32[]{:S(2)}, u32[]{:S(2)}) %collective-permute-start) | collective-permute-done | bytes 32800 | tf_op jit(solution)/shard_map/ppermute | solution.py:39
  18.7 0.0 copy-done.7
  18.7 0.7 broadcast_in_dim.17
  19.4 0.0 copy-start
  19.4 0.0 copy-start.1
  19.4 8.6 %all-to-all-start = ((bf16[16,32,256]{2,1,0:T(8,128)(2,1)}), bf16[16,32,256]{2,1,0:T(8,128)(2,1)S(1)}, u32[]{:S(2)}, u32[]{:S(2)}) async-start(bf16[16,32,256]{2,1,0:T(8,128)(2,1)} %broadcast_in_dim.17), calls=%async_computation | async-start | bytes 524288 | tf_op jit(solution)/shard_map/all_to_all | solution.py:231
  28.0 0.0 copy-start.4
  28.1 0.0 copy-start.5
  28.1 0.0 copy-start.6
  28.1 0.0 copy-done
  28.1 0.0 copy-done.1
  28.1 0.6 copy-done.4
  28.7 0.0 copy-done.5
  28.7 0.0 copy-done.6
  28.7 0.3 profile.1
  29.1 0.0 copy-start.2
  29.1 0.0 copy-start.3
  29.1 13.3 %all-gather = bf16[1088,256]{1,0:T(8,128)(2,1)S(1)} all-gather(bf16[136,256]{1,0:T(8,128)(2,1)S(1)} %profile.1), channel_id=2, replica_groups={{0,4,8,12,16,20,24,28},{32,36,40,44,48,52,56,60},{64,68,72,76,80,84,88,..., dimensions={0}, use_global_device_ids=true | all-gather | bytes 626688 | tf_op jit(solution)/shard_map/all_gather | solution.py:245
  42.4 2.2 %all-to-all-done.jac = bf16[16,32,256]{2,1,0:T(8,128)(2,1)S(1)} async-done(((bf16[16,32,256]{2,1,0:T(8,128)(2,1)}), bf16[16,32,256]{2,1,0:T(8,128)(2,1)S(1)}, u32[]{:S(2)}, u32[]{:S(2)}) %all-to-all-start) | async-done | bytes 262176 | tf_op jit(solution)/shard_map/all_to_all | solution.py:231
  44.6 0.0 copy-done.2
  44.6 0.0 copy-done.3
  44.6 2.5 %respond.1 = (f32[4,128,256]{2,1,0:T(8,128)S(1)}, f32[4,128,256]{2,1,0:T(8,128)S(1)}, f32[64,4,128]{2,1,0:T(4,128)}) custom-call(s32[1]{0:T(128)} %bitcast.me_ref, bf16[8,136,256]{2,1,0:T(8,128)(2,1)S(1)} %bitcast.31, bf16[16,32,256]{2,1,0:T(8,128)(2,1)S(1)} %all-to-all-done.jac, s32[128,256]{1,0:T(8,128)S(1)} %copy-done.2, f32[128,256]{1,0:T(8,128)S(1)} %copy-done.3), custom_call_target="tpu_custom_call" | custom-call | tf_op jit(solution)/shard_map/respond/pallas_call | solution.py:202
  47.1 1.9 %collective-permute-start.2 = (f32[4,128,256]{2,1,0:T(8,128)S(1)}, f32[4,128,256]{2,1,0:T(8,128)S(1)}, u32[]{:S(2)}, u32[]{:S(2)}) collective-permute-start(f32[4,128,256]{2,1,0:T(8,128)S(1)} %get-tuple-element.14), channel_id=1, source_target_pairs={{0,4},{4,0},{8,12},{12,8},{16,20},{20,16},{24,28},{28,24},{32,36},... | collective-permute-start | bytes 1572872 | tf_op jit(solution)/shard_map/ppermute | solution.py:253
  49.0 13.7 %all-to-all-start.1 = ((f32[64,4,128]{2,1,0:T(4,128)}), f32[64,4,128]{2,1,0:T(4,128)S(1)}, u32[]{:S(2)}, u32[]{:S(2)}) async-start(f32[64,4,128]{2,1,0:T(4,128)} %get-tuple-element.15), calls=%async_computation.1 | async-start | bytes 262144 | tf_op jit(solution)/shard_map/all_to_all | solution.py:252
  62.7 0.0 collective-permute-done.2
  62.7 0.1 add.40
  62.8 1.9 %collective-permute-start.3 = (f32[128,256]{1,0:T(8,128)S(1)}, f32[128,256]{1,0:T(8,128)S(1)}, u32[]{:S(2)}, u32[]{:S(2)}) collective-permute-start(f32[128,256]{1,0:T(8,128)S(1)} %get-tuple-element.18), channel_id=1, source_target_pairs={{0,8},{4,12},{8,16},{12,20},{16,24},{20,28},{24,0},{28,4},{32,40},... | collective-permute-start | bytes 393224 | tf_op jit(solution)/shard_map/ppermute | solution.py:257
  64.8 5.1 %collective-permute-start.5 = (f32[128,256]{1,0:T(8,128)S(1)}, f32[128,256]{1,0:T(8,128)S(1)}, u32[]{:S(2)}, u32[]{:S(2)}) collective-permute-start(f32[128,256]{1,0:T(8,128)S(1)} %get-tuple-element.19), channel_id=1, source_target_pairs={{0,24},{4,28},{8,0},{12,4},{16,8},{20,12},{24,16},{28,20},{32,56},... | collective-permute-start | bytes 393224 | tf_op jit(solution)/shard_map/ppermute | solution.py:257
  69.9 2.2 %collective-permute-start.4 = (f32[128,256]{1,0:T(8,128)S(1)}, f32[128,256]{1,0:T(8,128)S(1)}, u32[]{:S(2)}, u32[]{:S(2)}) collective-permute-start(f32[128,256]{1,0:T(8,128)S(1)} %get-tuple-element.20), channel_id=1, source_target_pairs={{0,16},{4,20},{8,24},{12,28},{16,0},{20,4},{24,8},{28,12},{32,48},... | collective-permute-start | bytes 393224 | tf_op jit(solution)/shard_map/ppermute | solution.py:257
  72.1 0.0 collective-permute-done.3
  72.1 3.1 %collective-permute-done.5 = f32[128,256]{1,0:T(8,128)S(1)} collective-permute-done((f32[128,256]{1,0:T(8,128)S(1)}, f32[128,256]{1,0:T(8,128)S(1)}, u32[]{:S(2)}, u32[]{:S(2)}) %collective-permute-start.5) | collective-permute-done | bytes 131104 | tf_op jit(solution)/shard_map/ppermute | solution.py:257
  75.2 3.1 %collective-permute-done.4 = f32[128,256]{1,0:T(8,128)S(1)} collective-permute-done((f32[128,256]{1,0:T(8,128)S(1)}, f32[128,256]{1,0:T(8,128)S(1)}, u32[]{:S(2)}, u32[]{:S(2)}) %collective-permute-start.4) | collective-permute-done | bytes 131104 | tf_op jit(solution)/shard_map/ppermute | solution.py:257
  78.3 0.1 reshape.29
  78.4 1.3 %all-to-all-done.1 = f32[64,4,128]{2,1,0:T(4,128)S(1)} async-done(((f32[64,4,128]{2,1,0:T(4,128)}), f32[64,4,128]{2,1,0:T(4,128)S(1)}, u32[]{:S(2)}, u32[]{:S(2)}) %all-to-all-start.1) | async-done | bytes 131104 | tf_op jit(solution)/shard_map/all_to_all | solution.py:252
  79.7 0.1 broadcast_multiply_fusion
  79.8 1.9 %collective-permute-start.6 = (f32[2,32,2,128]{3,2,1,0:T(2,128)S(1)}, f32[2,32,2,128]{3,2,1,0:T(2,128)S(1)}, u32[]{:S(2)}, u32[]{:S(2)}) collective-permute-start(f32[2,32,2,128]{3,2,1,0:T(2,128)S(1)} %get-tuple-element.23), channel_id=1, source_target_pairs={{0,508},{4,8},{8,4},{12,16},{16,12},{20,24},{24,20},{28,32},{32,28... | collective-permute-start | bytes 196616 | tf_op jit(solution)/shard_map/ppermute | solution.py:39
  81.7 1.9 %collective-permute-start.7 = (f32[2,32,2,128]{3,2,1,0:T(2,128)S(1)}, f32[2,32,2,128]{3,2,1,0:T(2,128)S(1)}, u32[]{:S(2)}, u32[]{:S(2)}) collective-permute-start(f32[2,32,2,128]{3,2,1,0:T(2,128)S(1)} %get-tuple-element.24), channel_id=1, source_target_pairs={{0,4},{4,0},{8,12},{12,8},{16,20},{20,16},{24,28},{28,24},{32,36},... | collective-permute-start | bytes 196616 | tf_op jit(solution)/shard_map/ppermute | solution.py:40
  83.7 0.7 slice_reduce_fusion
  85.0 3.7 %collective-permute-done.6 = f32[2,32,2,128]{3,2,1,0:T(2,128)S(1)} collective-permute-done((f32[2,32,2,128]{3,2,1,0:T(2,128)S(1)}, f32[2,32,2,128]{3,2,1,0:T(2,128)S(1)}, u32[]{:S(2)}, u32[]{:S(2)}) %collective-permute-start.6) | collective-permute-done | bytes 65568 | tf_op jit(solution)/shard_map/ppermute | solution.py:39
  88.7 0.0 collective-permute-done.7
  88.7 0.1 pad_maximum_fusion
  88.8 0.2 multiply_add_fusion
  89.1 0.8 multiply_add_fusion.1
  (5 shorter events, 0.1 us)
Async XLA Ops:
  0.6 18.1 %copy-start.7 = (bf16[1,256,32]{1,2,0:T(8,128)(2,1)S(1)}, bf16[1,256,32]{1,2,0:T(8,128)(2,1)}, u32[]{:S(2)}) copy-start(bf16[1,256,32]{1,2,0:T(8,128)(2,1)} %param.13) | copy-start | bytes 49156
  1.5 15.6 %collective-permute-start.1 = (bf16[2,32,2,128]{3,2,1,0:T(2,128)(2,1)S(1)}, bf16[2,32,2,128]{3,2,1,0:T(2,128)(2,1)S(1)}, u32[]{:S(2)}, u32[]{:S(2)}) collective-permute-start(bf16[2,32,2,128]{3,2,1,0:T(2,128)(2,1)S(1)} %get-tuple-element.25), channel_id=1, source_target_pairs={{0,4},{4,0},{8,12},{12,8},{16,20},{20,16},{24,28},{28,24},{32,36},... | collective-permute-start | bytes 98312 | tf_op jit(solution)/shard_map/ppermute | solution.py:40
  3.4 15.3 %collective-permute-start = (bf16[2,32,2,128]{3,2,1,0:T(2,128)(2,1)S(1)}, bf16[2,32,2,128]{3,2,1,0:T(2,128)(2,1)S(1)}, u32[]{:S(2)}, u32[]{:S(2)}) collective-permute-start(bf16[2,32,2,128]{3,2,1,0:T(2,128)(2,1)S(1)} %get-tuple-element.26), channel_id=1, source_target_pairs={{0,508},{4,8},{8,4},{12,16},{16,12},{20,24},{24,20},{28,32},{32,28... | collective-permute-start | bytes 98312 | tf_op jit(solution)/shard_map/ppermute | solution.py:39
  19.4 8.6 %copy-start = (f32[4,32,128]{2,1,0:T(8,128)S(1)}, f32[4,32,128]{2,1,0:T(8,128)}, u32[]{:S(2)}) copy-start(f32[4,32,128]{2,1,0:T(8,128)} %stddev.1) | copy-start | bytes 196612
  19.4 8.7 %copy-start.1 = (bf16[4,32,2,128]{3,2,1,0:T(2,128)(2,1)S(1)}, bf16[4,32,2,128]{3,2,1,0:T(2,128)(2,1)}, u32[]{:S(2)}) copy-start(bf16[4,32,2,128]{3,2,1,0:T(2,128)(2,1)} %param.8) | copy-start | bytes 196612
  19.4 25.2 %all-to-all-start = ((bf16[16,32,256]{2,1,0:T(8,128)(2,1)}), bf16[16,32,256]{2,1,0:T(8,128)(2,1)S(1)}, u32[]{:S(2)}, u32[]{:S(2)}) async-start(bf16[16,32,256]{2,1,0:T(8,128)(2,1)} %broadcast_in_dim.17), calls=%async_computation | async-start | bytes 524288 | tf_op jit(solution)/shard_map/all_to_all | solution.py:231
  28.0 0.7 copy-start.4
  28.1 0.7 copy-start.5
  28.1 0.7 copy-start.6
  29.1 15.5 %copy-start.2 = (s32[128,256]{1,0:T(8,128)S(1)}, s32[128,256]{1,0:T(8,128)}, u32[]{:S(2)}) copy-start(s32[128,256]{1,0:T(8,128)} %off.1) | copy-start | bytes 393220
  29.1 15.5 %copy-start.3 = (f32[128,256]{1,0:T(8,128)S(1)}, f32[128,256]{1,0:T(8,128)}, u32[]{:S(2)}) copy-start(f32[128,256]{1,0:T(8,128)} %wts.1) | copy-start | bytes 393220
  47.1 15.6 %collective-permute-start.2 = (f32[4,128,256]{2,1,0:T(8,128)S(1)}, f32[4,128,256]{2,1,0:T(8,128)S(1)}, u32[]{:S(2)}, u32[]{:S(2)}) collective-permute-start(f32[4,128,256]{2,1,0:T(8,128)S(1)} %get-tuple-element.14), channel_id=1, source_target_pairs={{0,4},{4,0},{8,12},{12,8},{16,20},{20,16},{24,28},{28,24},{32,36},... | collective-permute-start | bytes 1572872 | tf_op jit(solution)/shard_map/ppermute | solution.py:253
  49.0 30.6 %all-to-all-start.1 = ((f32[64,4,128]{2,1,0:T(4,128)}), f32[64,4,128]{2,1,0:T(4,128)S(1)}, u32[]{:S(2)}, u32[]{:S(2)}) async-start(f32[64,4,128]{2,1,0:T(4,128)} %get-tuple-element.15), calls=%async_computation.1 | async-start | bytes 262144 | tf_op jit(solution)/shard_map/all_to_all | solution.py:252
  62.8 9.2 %collective-permute-start.3 = (f32[128,256]{1,0:T(8,128)S(1)}, f32[128,256]{1,0:T(8,128)S(1)}, u32[]{:S(2)}, u32[]{:S(2)}) collective-permute-start(f32[128,256]{1,0:T(8,128)S(1)} %get-tuple-element.18), channel_id=1, source_target_pairs={{0,8},{4,12},{8,16},{12,20},{16,24},{20,28},{24,0},{28,4},{32,40},... | collective-permute-start | bytes 393224 | tf_op jit(solution)/shard_map/ppermute | solution.py:257
  64.8 10.4 %collective-permute-start.5 = (f32[128,256]{1,0:T(8,128)S(1)}, f32[128,256]{1,0:T(8,128)S(1)}, u32[]{:S(2)}, u32[]{:S(2)}) collective-permute-start(f32[128,256]{1,0:T(8,128)S(1)} %get-tuple-element.19), channel_id=1, source_target_pairs={{0,24},{4,28},{8,0},{12,4},{16,8},{20,12},{24,16},{28,20},{32,56},... | collective-permute-start | bytes 393224 | tf_op jit(solution)/shard_map/ppermute | solution.py:257
  69.9 8.4 %collective-permute-start.4 = (f32[128,256]{1,0:T(8,128)S(1)}, f32[128,256]{1,0:T(8,128)S(1)}, u32[]{:S(2)}, u32[]{:S(2)}) collective-permute-start(f32[128,256]{1,0:T(8,128)S(1)} %get-tuple-element.20), channel_id=1, source_target_pairs={{0,16},{4,20},{8,24},{12,28},{16,0},{20,4},{24,8},{28,12},{32,48},... | collective-permute-start | bytes 393224 | tf_op jit(solution)/shard_map/ppermute | solution.py:257
  79.8 8.9 %collective-permute-start.6 = (f32[2,32,2,128]{3,2,1,0:T(2,128)S(1)}, f32[2,32,2,128]{3,2,1,0:T(2,128)S(1)}, u32[]{:S(2)}, u32[]{:S(2)}) collective-permute-start(f32[2,32,2,128]{3,2,1,0:T(2,128)S(1)} %get-tuple-element.23), channel_id=1, source_target_pairs={{0,508},{4,8},{8,4},{12,16},{16,12},{20,24},{24,20},{28,32},{32,28... | collective-permute-start | bytes 196616 | tf_op jit(solution)/shard_map/ppermute | solution.py:39
  81.7 7.0 %collective-permute-start.7 = (f32[2,32,2,128]{3,2,1,0:T(2,128)S(1)}, f32[2,32,2,128]{3,2,1,0:T(2,128)S(1)}, u32[]{:S(2)}, u32[]{:S(2)}) collective-permute-start(f32[2,32,2,128]{3,2,1,0:T(2,128)S(1)} %get-tuple-element.24), channel_id=1, source_target_pairs={{0,4},{4,0},{8,12},{12,8},{16,20},{20,16},{24,28},{28,24},{32,36},... | collective-permute-start | bytes 196616 | tf_op jit(solution)/shard_map/ppermute | solution.py:40

commit v4 on v3

--- a/solution.py
+++ b/solution.py
@@ -8,6 +8,7 @@
 NSTEP = 2
 ZS, XS, CS = 16, 4, 2
 QS = XS * CS
+HALVING = (0, 3, 1, 2)
 
 
 def tile_groups(sizes, free):
@@ -41,8 +42,8 @@
     return cross, near
 
 
-def smooth(field, diffusivity):
-    cross, near = swap_edges(*edge_rows(field, NSTEP))
+def smooth(field, edges, diffusivity):
+    cross, near = edges
     even = (lax.axis_index("tile") & 1) == 0
     ext = jnp.concatenate(
         [jnp.where(even, cross, near), field, jnp.where(even, near, cross)], axis=0
@@ -52,41 +53,9 @@
     return ext
 
 
-def profile_kernel(me_ref, field, cross, near, stddev, diffusivity, columns, counts, out):
-    tile_rows, cols, lev = stddev.shape
-    wide = 2 * cols
-    edge = cross.shape[0]
-    even = (me_ref[0] & 1) == 0
-    before = jnp.where(even, cross[...], near[...])
-    after = jnp.where(even, near[...], cross[...])
-    own = field[...]
-    left = lax.broadcasted_iota(jnp.int32, (wide, wide), 0)
-    right = lax.broadcasted_iota(jnp.int32, (wide, wide), 1)
-    split = jnp.where(
-        right == jnp.where(left < cols, 2 * left, 2 * (left - cols) + 1), 1.0, 0.0
-    ).astype(jnp.bfloat16)
-    grid = []
-    for block, count in ((before, edge // wide), (own, tile_rows), (after, edge // wide)):
-        for i in range(count):
-            grid.append(
-                jnp.dot(split, block[i * wide : (i + 1) * wide], preferred_element_type=jnp.float32)
-            )
-    place = lax.broadcasted_iota(jnp.int32, (wide, lev), 0) & (cols - 1)
-    rate = diffusivity[...]
-    for _ in range(NSTEP):
-        new = []
-        for i in range(1, len(grid) - 1):
-            middle = grid[i]
-            following = jnp.where(place == cols - 1, 0.0, pltpu.roll(middle, wide - 1, 0))
-            leading = jnp.where(place == 0, 0.0, pltpu.roll(middle, 1, 0))
-            laplace = grid[i + 1] + grid[i - 1] + following + leading - 4.0 * middle
-            new.append(middle + rate * laplace)
-        grid = new
-    for i in range(tile_rows):
-        for p in range(2):
-            out[i * cols : (i + 1) * cols, p * lev : (p + 1) * lev] = (
-                stddev[i] * grid[i][p * cols : (p + 1) * cols]
-            ).astype(jnp.bfloat16)
+def target_kernel(columns, counts, probes, stddev, out, field, spread):
+    field[...] = probes[...].astype(jnp.float32)
+    spread[...] = stddev[...]
     slots, sections = columns.shape
     width = out.shape[1]
     live = lax.broadcasted_iota(jnp.int32, (slots, sections), 0) < counts[...]
@@ -100,23 +69,26 @@
         choose = jnp.where(apart == q, 1.0, 0.0).astype(jnp.bfloat16)
         spread = jnp.dot(target, choose, preferred_element_type=jnp.float32)
         lines.append(jnp.sum(jnp.where(mine, spread, 0.0), axis=0, keepdims=True))
-    out[tile_rows * cols :, :] = jnp.concatenate(lines, axis=0).astype(jnp.bfloat16)
+    out[...] = jnp.concatenate(lines, axis=0).astype(jnp.bfloat16)
 
 
 def in_vmem(*arrays):
     return [pltpu.with_memory_space_constraint(a, pltpu.VMEM) for a in arrays]
 
 
-def profile_block(me, field, cross, near, stddev, diffusivity, columns, counts):
-    tile_rows, cols, lev = stddev.shape
+def slot_targets(columns, counts, probes, stddev):
     vmem = pl.BlockSpec(memory_space=pltpu.VMEM)
     return pl.pallas_call(
-        profile_kernel,
-        out_shape=pltpu.VMEM((tile_rows * cols + QS, 2 * lev), jnp.bfloat16),
-        in_specs=[pl.BlockSpec(memory_space=pltpu.SMEM)] + [vmem] * 7,
-        out_specs=vmem,
-        name="profile",
-    )(me, *in_vmem(field, cross, near, stddev, diffusivity, columns, counts))
+        target_kernel,
+        out_shape=(
+            pltpu.VMEM((QS, columns.size // QS), jnp.bfloat16),
+            pltpu.VMEM(probes.shape, jnp.float32),
+            pltpu.VMEM(stddev.shape, jnp.float32),
+        ),
+        in_specs=[vmem] * 4,
+        out_specs=(vmem, vmem, vmem),
+        name="targets",
+    )(*in_vmem(columns, counts, probes, stddev))
 
 
 def band_columns(jac, offsets):
@@ -187,9 +159,9 @@
         energy[s * each : (s + 1) * each] = jnp.broadcast_to(
             jnp.sum(total, axis=1, keepdims=True)[None], (each,) + energy.shape[1:]
         )
-    for j in range(tiles // 2):
+    for j, away in enumerate(HALVING):
         for half, out in ((0, mine), (1, other)):
-            q = ((me + 2 * j) & (tiles - 1)) if half == 0 else (((me ^ 1) + 2 * j) & (tiles - 1))
+            q = me ^ (CS * away + half)
             out[j] = jnp.dot(sel[q], adj[q], preferred_element_type=jnp.float32)
 
 
@@ -201,7 +173,7 @@
     vmem = pl.BlockSpec(memory_space=pltpu.VMEM)
     return pl.pallas_call(
         respond_kernel,
-        out_shape=(part, part, pltpu.VMEM((sections * copies, 4, 128), jnp.float32)),
+        out_shape=(part, part, pltpu.VMEM((sections * copies, 1, 128), jnp.float32)),
         in_specs=[pl.BlockSpec(memory_space=pltpu.SMEM), vmem, vmem, vmem, vmem],
         out_specs=(vmem, vmem, vmem),
         scratch_shapes=[
@@ -225,23 +197,28 @@
     plane = tile_groups(sizes, (1, 2))
     here = lax.axis_index("tile")
     me = here & (QS - 1)
-    cross, near = swap_edges(*edge_rows(probes, NSTEP))
-    own = jnp.broadcast_to(jnp.swapaxes(jacobian, 1, 2), (ZS, jacobian.shape[2], channels))
-    own, cross, near = lax.optimization_barrier((own, cross, near))
+    starts, own = lax.optimization_barrier((edge_rows(probes, NSTEP), jnp.swapaxes(jacobian, 1, 2)))
     jac = lax.all_to_all(
-        own,
+        jnp.broadcast_to(own, (ZS,) + own.shape[1:]),
         "tile", 0, 0, axis_index_groups=along_z, tiled=True,
     )
-    block = profile_block(
-        me.reshape(1),
-        probes.reshape(-1, levels),
-        cross.reshape(-1, levels),
-        near.reshape(-1, levels),
-        stddev,
-        diffusivity[None],
-        columns[0].T,
-        counts,
-    )
+    cross, near = swap_edges(*starts)
+    targets, field, spread = slot_targets(
+        columns[0].T, counts, probes.reshape(-1, levels), stddev
+    )
+    even = (me & 1) == 0
+    ext = jnp.concatenate(
+        [
+            jnp.where(even, cross, near).astype(jnp.float32),
+            field.reshape(probes.shape),
+            jnp.where(even, near, cross).astype(jnp.float32),
+        ],
+        axis=0,
+    )
+    for _ in range(NSTEP):
+        ext = laplace_step(ext, diffusivity)
+    profile = (spread[:, :, None, :] * ext).astype(jnp.bfloat16)
+    block = jnp.concatenate([profile.reshape(cell_count, -1), targets], axis=0)
     gathered = lax.all_gather(
         block[None],
         "tile", axis=0, axis_index_groups=plane, tiled=True,
@@ -251,17 +228,22 @@
     along_zy = [[t * lev_count + y for t in group for y in range(lev_count)] for group in along_z]
     shares = lax.all_to_all(energy, ("tile", "lev"), 0, 0, axis_index_groups=along_zy, tiled=True)
     summed = mine + lax.ppermute(other, "tile", [(i, i ^ 1) for i in range(tile_count)])
-    gradient = summed[0]
-    for step in range(1, XS):
-        ring = [(i, i // QS * QS + (i + step * CS) % QS) for i in range(tile_count)]
-        gradient = gradient + lax.ppermute(summed[step], "tile", ring)
+    x = here >> 1
+    pairs = [[t, t + CS] for t in range(tile_count) if (t >> 1) & 1 == 0]
+    sent = lax.all_gather(summed[2:], "tile", axis=0, axis_index_groups=pairs)
+    halves = summed[:2] + lax.dynamic_index_in_dim(sent, 1 - (x & 1), 0, keepdims=False)
+    pairs = [[t, t ^ (3 * CS)] for t in range(tile_count) if (t >> 1) & 2 == 0]
+    sent = lax.all_gather(halves[1], "tile", axis=0, axis_index_groups=pairs)
+    gradient = halves[0] + lax.dynamic_index_in_dim(sent, 1 - ((x >> 1) & 1), 0, keepdims=False)
     gradient = gradient.reshape(row_count, col_count, probe_count, levels)
-    gradient, shares = lax.optimization_barrier((gradient, shares))
+    scaled = stddev[:, :, None, :] * gradient
+    edges = swap_edges(*edge_rows(scaled, NSTEP))
     trace_share = (
         jnp.sum(shares[:, 0, 0])
         * (1.0 / (probe_count * lev_count * tile_count * slot_count * channels))
     ).reshape(1)
-    hessian = smooth(stddev[:, :, None, :] * gradient, diffusivity)
+    edges, trace_share = lax.optimization_barrier((edges, trace_share))
+    hessian = smooth(scaled, edges, diffusivity)
     return (hessian, trace_share)
 
 

time: 91.6 us -> 86.7 us (0.947)
  blocking collectives: 13.3 us -> 28.6 us
  starting transfers between devices: 52.9 us -> 40.7 us
  waiting for transfers between devices: 15 us -> 6.07 us
    all_gather x0 -> x2, blocking collectives: none -> 15.3 us  [the longest x1 8.49 us: body(): sent = lax.all_gather(summed[2:], 'tile', axis=0, axis_index_groups=pairs)]
    ppermute x3 -> x0, starting transfers between devices: 9.21 us -> none  [body(): gradient = gradient + lax.ppermute(summed[step], 'tile', ring)]
    ppermute x3 -> x0, waiting for transfers between devices: 6.19 us -> none  [body(): gradient = gradient + lax.ppermute(summed[step], 'tile', ring)]
    ppermute x2, waiting for transfers between devices: 5.3 us -> 2.58 us  [swap_edges(): cross = lax.ppermute(to_cross, 'tile', across)]
    all_to_all x1, starting transfers between devices: 8.59 us -> 6.4 us  [body(): lax.all_to_all(jnp.broadcast_to(own, (ZS,) + own.shape[1:]), 'tile', 0, 0...]
    all_to_all x1, waiting for transfers between devices: 1.26 us -> 0.01 us  [body(): lax.all_to_all(energy, ('tile', 'lev'), 0, 0, axis_index_groups=along_zy,...]
    all_to_all x1, waiting for transfers between devices: 2.22 us -> 3.48 us  [body(): lax.all_to_all(jnp.broadcast_to(own, (ZS,) + own.shape[1:]), 'tile', 0, 0...]
    all_to_all x1, starting transfers between devices: 13.7 us -> 12.4 us  [body(): lax.all_to_all(energy, ('tile', 'lev'), 0, 0, axis_index_groups=along_zy,...]
  transfers between devices with their start and end apart: 10 -> 7, of which waited for: 6 -> 2; matrix products, arithmetic and copies ran while one was open for 1% -> 3% of each run, Pallas kernels for 0% -> 0%
where the time goes in v4:
time: 86.7 us; the launch traced here: 86.1 us
  starting transfers between devices  40.7 us (47%)
  blocking collectives  28.6 us (33%)
  waiting for transfers between devices  6.07 us (7%)
  other arithmetic  3.39 us (4%)
  between operations  2.73 us (3%)
  Pallas kernels  2.55 us (3%)
  local copies, waits for them, and re-layouts  2.09 us (2%)
    ppermute x2, starting transfers between devices, swap_edges(): cross = lax.ppermute(to_cross, 'tile', across)  16.1 us
    all_gather x1, blocking collectives, body(): lax.all_gather(block[None], 'tile', axis=0, axis_index_groups=plane, tile...  13.3 us
    all_to_all x1, starting transfers between devices, body(): lax.all_to_all(energy, ('tile', 'lev'), 0, 0, axis_index_groups=along_zy,...  12.4 us
    all_gather x1, blocking collectives, body(): sent = lax.all_gather(summed[2:], 'tile', axis=0, axis_index_groups=pairs)  8.49 us
    all_gather x1, blocking collectives, body(): sent = lax.all_gather(halves[1], 'tile', axis=0, axis_index_groups=pairs)  6.86 us
    all_to_all x1, starting transfers between devices, body(): lax.all_to_all(jnp.broadcast_to(own, (ZS,) + own.shape[1:]), 'tile', 0, 0...  6.4 us
    ppermute x2, starting transfers between devices, swap_edges(): near = lax.ppermute(to_near, 'tile', [(i, i ^ 1) for i in range(count)])  3.84 us
    all_to_all x1, waiting for transfers between devices, body(): lax.all_to_all(jnp.broadcast_to(own, (ZS,) + own.shape[1:]), 'tile', 0, 0...  3.48 us
  transfers between devices with their start and end apart: 7, of which 2 were waited for; matrix products, arithmetic and copies ran while one was open for 3% of the time, Pallas kernels for 0%

profile of v4, /device:TPU:8, one launch (start us, length us, event | category | flops | bytes accessed | tf_op | source)
XLA Modules:
  0.0 86.1 jit_solution(2229820391254013362)
XLA Ops:
  0.6 0.0 copy-start.6
  0.6 0.8 broadcast_select_fusion.6
  1.5 13.0 %collective-permute-start = (bf16[2,32,2,128]{3,2,1,0:T(2,128)(2,1)S(1)}, bf16[2,32,2,128]{3,2,1,0:T(2,128)(2,1)S(1)}, u32[]{:S(2)}, u32[]{:S(2)}) collective-permute-start(bf16[2,32,2,128]{3,2,1,0:T(2,128)(2,1)S(1)} %get-tuple-element.15), channel_id=1, source_target_pairs={{0,508},{4,8},{8,4},{12,16},{16,12},{20,24},{24,20},{28,32},{32,28... | collective-permute-start | bytes 98312 | tf_op jit(solution)/shard_map/ppermute | solution.py:40
  14.5 1.9 %collective-permute-start.1 = (bf16[2,32,2,128]{3,2,1,0:T(2,128)(2,1)S(1)}, bf16[2,32,2,128]{3,2,1,0:T(2,128)(2,1)S(1)}, u32[]{:S(2)}, u32[]{:S(2)}) collective-permute-start(bf16[2,32,2,128]{3,2,1,0:T(2,128)(2,1)S(1)} %get-tuple-element.16), channel_id=1, source_target_pairs={{0,4},{4,0},{8,12},{12,8},{16,20},{20,16},{24,28},{28,24},{32,36},... | collective-permute-start | bytes 98312 | tf_op jit(solution)/shard_map/ppermute | solution.py:41
  16.5 0.0 copy-done.6
  16.5 0.7 broadcast_in_dim.8
  17.2 0.0 copy-start
  17.2 0.0 copy-start.1
  17.2 6.4 %all-to-all-start = ((bf16[16,32,256]{2,1,0:T(8,128)(2,1)}), bf16[16,32,256]{2,1,0:T(8,128)(2,1)S(1)}, u32[]{:S(2)}, u32[]{:S(2)}) async-start(bf16[16,32,256]{2,1,0:T(8,128)(2,1)} %broadcast_in_dim.8), calls=%async_computation | async-start | bytes 524288 | tf_op jit(solution)/shard_map/all_to_all | solution.py:201
  23.6 0.0 copy-start.4
  23.6 0.0 copy-start.5
  23.6 0.0 copy-done
  23.6 0.0 copy-done.1
  23.7 0.6 copy-done.4
  24.3 0.0 copy-done.5
  24.3 0.2 targets.1
  24.5 0.0 collective-permute-done
  24.5 0.0 collective-permute-done.1
  24.6 0.0 copy-start.7
  24.6 0.1 pad_maximum_fusion.2
  24.7 0.5 copy-done.7
  25.3 0.2 multiply_add_fusion.1
  25.5 0.2 multiply_convert_fusion
  25.7 0.0 copy-start.2
  25.7 0.0 copy-start.3
  25.7 13.3 %all-gather = bf16[1088,256]{1,0:T(8,128)(2,1)S(1)} all-gather(bf16[136,256]{1,0:T(8,128)(2,1)S(1)} %pad_maximum_fusion.4), channel_id=2, replica_groups={{0,4,8,12,16,20,24,28},{32,36,40,44,48,52,56,60},{64,68,72,76,80,84,88,..., dimensions={0}, use_global_device_ids=true | all-gather | bytes 626688 | tf_op jit(solution)/shard_map/all_gather | solution.py:222
  39.0 3.5 %all-to-all-done.jac = bf16[16,32,256]{2,1,0:T(8,128)(2,1)S(1)} async-done(((bf16[16,32,256]{2,1,0:T(8,128)(2,1)}), bf16[16,32,256]{2,1,0:T(8,128)(2,1)S(1)}, u32[]{:S(2)}, u32[]{:S(2)}) %all-to-all-start) | async-done | bytes 262176 | tf_op jit(solution)/shard_map/all_to_all | solution.py:201
  42.5 0.0 copy-done.2
  42.5 0.0 copy-done.3
  42.5 2.3 %respond.1 = (f32[4,128,256]{2,1,0:T(8,128)S(1)}, f32[4,128,256]{2,1,0:T(8,128)S(1)}, f32[64,1,128]{2,1,0:T(1,128)}) custom-call(s32[1]{0:T(128)} %bitcast.me_ref, bf16[8,136,256]{2,1,0:T(8,128)(2,1)S(1)} %bitcast.22, bf16[16,32,256]{2,1,0:T(8,128)(2,1)S(1)} %all-to-all-done.jac, s32[128,256]{1,0:T(8,128)S(1)} %copy-done.2, f32[128,256]{1,0:T(8,128)S(1)} %copy-done.3), custom_call_target="tpu_custom_call" | custom-call | tf_op jit(solution)/shard_map/respond/pallas_call | solution.py:174
  44.8 1.9 %collective-permute-start.2 = (f32[4,128,256]{2,1,0:T(8,128)S(1)}, f32[4,128,256]{2,1,0:T(8,128)S(1)}, u32[]{:S(2)}, u32[]{:S(2)}) collective-permute-start(f32[4,128,256]{2,1,0:T(8,128)S(1)} %get-tuple-element.21), channel_id=1, source_target_pairs={{0,4},{4,0},{8,12},{12,8},{16,20},{20,16},{24,28},{28,24},{32,36},... | collective-permute-start | bytes 1572872 | tf_op jit(solution)/shard_map/ppermute | solution.py:230
  46.8 12.4 %all-to-all-start.1 = ((f32[64,1,128]{2,1,0:T(1,128)}), f32[64,1,128]{2,1,0:T(1,128)S(1)}, u32[]{:S(2)}, u32[]{:S(2)}) async-start(f32[64,1,128]{2,1,0:T(1,128)} %get-tuple-element.22), calls=%async_computation.1 | async-start | bytes 65536 | tf_op jit(solution)/shard_map/all_to_all | solution.py:229
  59.2 0.0 collective-permute-done.2
  59.2 0.1 add.87
  59.3 8.5 %all-gather.1 = f32[4,128,256]{2,1,0:T(8,128)S(1)} all-gather(f32[2,128,256]{2,1,0:T(8,128)S(1)} %slice.112), channel_id=3, replica_groups={{0,8},{4,12},{16,24},{20,28},{32,40},{36,44},{48,56},{52,60},{64,72},{6..., dimensions={0}, use_global_device_ids=true | all-gather | bytes 786432 | tf_op jit(solution)/shard_map/all_gather | solution.py:233
  67.9 6.9 %all_gather.15 = f32[2,128,256]{2,1,0:T(8,128)S(1)} all-gather(f32[1,128,256]{2,1,0:T(8,128)S(1)} %slice.114), channel_id=1, replica_groups={{0,24},{4,28},{8,16},{12,20},{32,56},{36,60},{40,48},{44,52},{64,88},{6..., dimensions={0}, use_global_device_ids=true | all-gather | bytes 393216 | tf_op jit(solution)/shard_map/all_gather | solution.py:236
  74.7 0.1 add.92
  74.8 0.1 broadcast_multiply_fusion
  74.9 3.1 %collective-permute-start.3 = (f32[2,32,2,128]{3,2,1,0:T(2,128)S(1)}, f32[2,32,2,128]{3,2,1,0:T(2,128)S(1)}, u32[]{:S(2)}, u32[]{:S(2)}) collective-permute-start(f32[2,32,2,128]{3,2,1,0:T(2,128)S(1)} %get-tuple-element.29), channel_id=1, source_target_pairs={{0,508},{4,8},{8,4},{12,16},{16,12},{20,24},{24,20},{28,32},{32,28... | collective-permute-start | bytes 196616 | tf_op jit(solution)/shard_map/ppermute | solution.py:40
  78.0 1.9 %collective-permute-start.4 = (f32[2,32,2,128]{3,2,1,0:T(2,128)S(1)}, f32[2,32,2,128]{3,2,1,0:T(2,128)S(1)}, u32[]{:S(2)}, u32[]{:S(2)}) collective-permute-start(f32[2,32,2,128]{3,2,1,0:T(2,128)S(1)} %get-tuple-element.28), channel_id=1, source_target_pairs={{0,4},{4,0},{8,12},{12,8},{16,20},{20,16},{24,28},{28,24},{32,36},... | collective-permute-start | bytes 196616 | tf_op jit(solution)/shard_map/ppermute | solution.py:41
  79.9 0.0 all-to-all-done.1
  79.9 0.7 slice_reduce_fusion
  81.3 2.6 %collective-permute-done.3 = f32[2,32,2,128]{3,2,1,0:T(2,128)S(1)} collective-permute-done((f32[2,32,2,128]{3,2,1,0:T(2,128)S(1)}, f32[2,32,2,128]{3,2,1,0:T(2,128)S(1)}, u32[]{:S(2)}, u32[]{:S(2)}) %collective-permute-start.3) | collective-permute-done | bytes 65568 | tf_op jit(solution)/shard_map/ppermute | solution.py:40
  83.8 0.0 collective-permute-done.4
  83.9 0.1 pad_maximum_fusion
  84.0 0.2 multiply_add_fusion
  84.2 0.8 multiply_add_fusion.2
  (11 shorter events, 0.2 us)
Async XLA Ops:
  0.6 15.8 %copy-start.6 = (bf16[1,256,32]{1,2,0:T(8,128)(2,1)S(1)}, bf16[1,256,32]{1,2,0:T(8,128)(2,1)}, u32[]{:S(2)}) copy-start(bf16[1,256,32]{1,2,0:T(8,128)(2,1)} %param.13) | copy-start | bytes 49156
  1.5 23.0 %collective-permute-start = (bf16[2,32,2,128]{3,2,1,0:T(2,128)(2,1)S(1)}, bf16[2,32,2,128]{3,2,1,0:T(2,128)(2,1)S(1)}, u32[]{:S(2)}, u32[]{:S(2)}) collective-permute-start(bf16[2,32,2,128]{3,2,1,0:T(2,128)(2,1)S(1)} %get-tuple-element.15), channel_id=1, source_target_pairs={{0,508},{4,8},{8,4},{12,16},{16,12},{20,24},{24,20},{28,32},{32,28... | collective-permute-start | bytes 98312 | tf_op jit(solution)/shard_map/ppermute | solution.py:40
  14.5 10.0 %collective-permute-start.1 = (bf16[2,32,2,128]{3,2,1,0:T(2,128)(2,1)S(1)}, bf16[2,32,2,128]{3,2,1,0:T(2,128)(2,1)S(1)}, u32[]{:S(2)}, u32[]{:S(2)}) collective-permute-start(bf16[2,32,2,128]{3,2,1,0:T(2,128)(2,1)S(1)} %get-tuple-element.16), channel_id=1, source_target_pairs={{0,4},{4,0},{8,12},{12,8},{16,20},{20,16},{24,28},{28,24},{32,36},... | collective-permute-start | bytes 98312 | tf_op jit(solution)/shard_map/ppermute | solution.py:41
  17.2 6.4 %copy-start = (f32[4,32,128]{2,1,0:T(8,128)S(1)}, f32[4,32,128]{2,1,0:T(8,128)}, u32[]{:S(2)}) copy-start(f32[4,32,128]{2,1,0:T(8,128)} %stddev.1) | copy-start | bytes 196612
  17.2 6.4 %copy-start.1 = (bf16[4,32,2,128]{3,2,1,0:T(2,128)(2,1)S(1)}, bf16[4,32,2,128]{3,2,1,0:T(2,128)(2,1)}, u32[]{:S(2)}) copy-start(bf16[4,32,2,128]{3,2,1,0:T(2,128)(2,1)} %param.8) | copy-start | bytes 196612
  17.2 25.3 %all-to-all-start = ((bf16[16,32,256]{2,1,0:T(8,128)(2,1)}), bf16[16,32,256]{2,1,0:T(8,128)(2,1)S(1)}, u32[]{:S(2)}, u32[]{:S(2)}) async-start(bf16[16,32,256]{2,1,0:T(8,128)(2,1)} %broadcast_in_dim.8), calls=%async_computation | async-start | bytes 524288 | tf_op jit(solution)/shard_map/all_to_all | solution.py:201
  23.6 0.7 copy-start.4
  23.6 0.7 copy-start.5
  24.6 0.7 copy-start.7
  25.7 16.8 %copy-start.2 = (s32[128,256]{1,0:T(8,128)S(1)}, s32[128,256]{1,0:T(8,128)}, u32[]{:S(2)}) copy-start(s32[128,256]{1,0:T(8,128)} %off.1) | copy-start | bytes 393220
  25.7 16.8 %copy-start.3 = (f32[128,256]{1,0:T(8,128)S(1)}, f32[128,256]{1,0:T(8,128)}, u32[]{:S(2)}) copy-start(f32[128,256]{1,0:T(8,128)} %wts.1) | copy-start | bytes 393220
  44.8 14.4 %collective-permute-start.2 = (f32[4,128,256]{2,1,0:T(8,128)S(1)}, f32[4,128,256]{2,1,0:T(8,128)S(1)}, u32[]{:S(2)}, u32[]{:S(2)}) collective-permute-start(f32[4,128,256]{2,1,0:T(8,128)S(1)} %get-tuple-element.21), channel_id=1, source_target_pairs={{0,4},{4,0},{8,12},{12,8},{16,20},{20,16},{24,28},{28,24},{32,36},... | collective-permute-start | bytes 1572872 | tf_op jit(solution)/shard_map/ppermute | solution.py:230
  46.8 33.2 %all-to-all-start.1 = ((f32[64,1,128]{2,1,0:T(1,128)}), f32[64,1,128]{2,1,0:T(1,128)S(1)}, u32[]{:S(2)}, u32[]{:S(2)}) async-start(f32[64,1,128]{2,1,0:T(1,128)} %get-tuple-element.22), calls=%async_computation.1 | async-start | bytes 65536 | tf_op jit(solution)/shard_map/all_to_all | solution.py:229
  74.9 8.9 %collective-permute-start.3 = (f32[2,32,2,128]{3,2,1,0:T(2,128)S(1)}, f32[2,32,2,128]{3,2,1,0:T(2,128)S(1)}, u32[]{:S(2)}, u32[]{:S(2)}) collective-permute-start(f32[2,32,2,128]{3,2,1,0:T(2,128)S(1)} %get-tuple-element.29), channel_id=1, source_target_pairs={{0,508},{4,8},{8,4},{12,16},{16,12},{20,24},{24,20},{28,32},{32,28... | collective-permute-start | bytes 196616 | tf_op jit(solution)/shard_map/ppermute | solution.py:40
  78.0 5.8 %collective-permute-start.4 = (f32[2,32,2,128]{3,2,1,0:T(2,128)S(1)}, f32[2,32,2,128]{3,2,1,0:T(2,128)S(1)}, u32[]{:S(2)}, u32[]{:S(2)}) collective-permute-start(f32[2,32,2,128]{3,2,1,0:T(2,128)S(1)} %get-tuple-element.28), channel_id=1, source_target_pairs={{0,4},{4,0},{8,12},{12,8},{16,20},{20,16},{24,28},{28,24},{32,36},... | collective-permute-start | bytes 196616 | tf_op jit(solution)/shard_map/ppermute | solution.py:41

commit v5 on v4

--- a/solution.py
+++ b/solution.py
@@ -34,10 +34,13 @@
     return jnp.where(even, top, bottom), jnp.where(even, bottom, top)
 
 
+def cross_pairs(count):
+    return [(i, (i - 1 if i % 2 == 0 else i + 1) % count) for i in range(count)]
+
+
 def swap_edges(to_cross, to_near):
     count = lax.axis_size("tile")
-    across = [(i, (i - 1 if i % 2 == 0 else i + 1) % count) for i in range(count)]
-    cross = lax.ppermute(to_cross, "tile", across)
+    cross = lax.ppermute(to_cross, "tile", cross_pairs(count))
     near = lax.ppermute(to_near, "tile", [(i, i ^ 1) for i in range(count)])
     return cross, near
 
@@ -53,9 +56,24 @@
     return ext
 
 
-def target_kernel(columns, counts, probes, stddev, out, field, spread):
+def in_vmem(*arrays):
+    return [pltpu.with_memory_space_constraint(a, pltpu.VMEM) for a in arrays]
+
+
+def stage_kernel(
+    me_ref, probes, jac, stddev, diffusivity, columns, counts,
+    to_cross, to_near, copies, field, spread, rate, out,
+):
+    edge = to_cross.shape[0]
+    even = (me_ref[0] & 1) == 0
+    top, bottom = probes[:edge], probes[-edge:]
+    to_cross[...] = jnp.where(even, top, bottom)
+    to_near[...] = jnp.where(even, bottom, top)
+    for z in range(copies.shape[0]):
+        copies[z] = jac[...]
     field[...] = probes[...].astype(jnp.float32)
     spread[...] = stddev[...]
+    rate[...] = diffusivity[...]
     slots, sections = columns.shape
     width = out.shape[1]
     live = lax.broadcasted_iota(jnp.int32, (slots, sections), 0) < counts[...]
@@ -72,23 +90,24 @@
     out[...] = jnp.concatenate(lines, axis=0).astype(jnp.bfloat16)
 
 
-def in_vmem(*arrays):
-    return [pltpu.with_memory_space_constraint(a, pltpu.VMEM) for a in arrays]
-
-
-def slot_targets(columns, counts, probes, stddev):
+def stage(me, probes, jac, stddev, diffusivity, columns, counts, edge):
     vmem = pl.BlockSpec(memory_space=pltpu.VMEM)
+    rows = pltpu.VMEM((edge, probes.shape[1]), probes.dtype)
     return pl.pallas_call(
-        target_kernel,
+        stage_kernel,
         out_shape=(
-            pltpu.VMEM((QS, columns.size // QS), jnp.bfloat16),
+            rows,
+            rows,
+            jax.ShapeDtypeStruct((ZS,) + jac.shape, jac.dtype),
             pltpu.VMEM(probes.shape, jnp.float32),
             pltpu.VMEM(stddev.shape, jnp.float32),
+            pltpu.VMEM(diffusivity.shape, jnp.float32),
+            pltpu.VMEM((QS, columns.size // QS), jnp.bfloat16),
         ),
-        in_specs=[vmem] * 4,
-        out_specs=(vmem, vmem, vmem),
-        name="targets",
-    )(*in_vmem(columns, counts, probes, stddev))
+        in_specs=[pl.BlockSpec(memory_space=pltpu.SMEM)] + [vmem] * 6,
+        out_specs=(vmem,) * 7,
+        name="stage",
+    )(me, probes, jac, stddev, diffusivity, columns, counts)
 
 
 def band_columns(jac, offsets):
@@ -197,15 +216,19 @@
     plane = tile_groups(sizes, (1, 2))
     here = lax.axis_index("tile")
     me = here & (QS - 1)
-    starts, own = lax.optimization_barrier((edge_rows(probes, NSTEP), jnp.swapaxes(jacobian, 1, 2)))
-    jac = lax.all_to_all(
-        jnp.broadcast_to(own, (ZS,) + own.shape[1:]),
-        "tile", 0, 0, axis_index_groups=along_z, tiled=True,
-    )
-    cross, near = swap_edges(*starts)
-    targets, field, spread = slot_targets(
-        columns[0].T, counts, probes.reshape(-1, levels), stddev
-    )
+    to_cross, to_near, copies, field, spread, rate, targets = stage(
+        me.reshape(1), probes.reshape(-1, levels), jacobian[0].T, stddev, diffusivity[None],
+        columns[0].T, counts, NSTEP * col_count * probe_count,
+    )
+    jac = lax.all_to_all(copies, "tile", 0, 0, axis_index_groups=along_z, tiled=True)
+    rows = (NSTEP, col_count, probe_count, levels)
+    cross = lax.ppermute(to_cross, "tile", cross_pairs(tile_count))
+    to_near, cross = lax.optimization_barrier((to_near, cross))
+    near = lax.all_gather(
+        to_near, "tile", axis=0, axis_index_groups=tile_groups(sizes, (2,)),
+    )
+    near = lax.dynamic_index_in_dim(near, 1 - (me & 1), 0, keepdims=False)
+    cross, near = cross.reshape(rows), near.reshape(rows)
     even = (me & 1) == 0
     ext = jnp.concatenate(
         [
@@ -216,7 +239,7 @@
         axis=0,
     )
     for _ in range(NSTEP):
-        ext = laplace_step(ext, diffusivity)
+        ext = laplace_step(ext, rate[0])
     profile = (spread[:, :, None, :] * ext).astype(jnp.bfloat16)
     block = jnp.concatenate([profile.reshape(cell_count, -1), targets], axis=0)
     gathered = lax.all_gather(
@@ -236,14 +259,14 @@
     sent = lax.all_gather(halves[1], "tile", axis=0, axis_index_groups=pairs)
     gradient = halves[0] + lax.dynamic_index_in_dim(sent, 1 - ((x >> 1) & 1), 0, keepdims=False)
     gradient = gradient.reshape(row_count, col_count, probe_count, levels)
-    scaled = stddev[:, :, None, :] * gradient
+    scaled = spread[:, :, None, :] * gradient
     edges = swap_edges(*edge_rows(scaled, NSTEP))
     trace_share = (
         jnp.sum(shares[:, 0, 0])
         * (1.0 / (probe_count * lev_count * tile_count * slot_count * channels))
     ).reshape(1)
     edges, trace_share = lax.optimization_barrier((edges, trace_share))
-    hessian = smooth(scaled, edges, diffusivity)
+    hessian = smooth(scaled, edges, rate[0])
     return (hessian, trace_share)
 
 

time: 86.7 us -> 85 us (0.980)
  local copies, waits for them, and re-layouts: 2.09 us -> 0.15 us
  blocking collectives: 28.6 us -> 30.5 us
  starting transfers between devices: 40.7 us -> 38.9 us
  Pallas kernels: 2.55 us -> 4.06 us
    ppermute x2 -> x1, starting transfers between devices: 3.84 us -> 1.92 us  [swap_edges(): near = lax.ppermute(to_near, 'tile', [(i, i ^ 1) for i in range(count)])]
    all_gather x0 -> x1, blocking collectives: none -> 1.85 us  [body(): lax.all_gather(to_near, 'tile', axis=0, axis_index_groups=tile_groups(siz...]
    pallas_call x1, Pallas kernels: 0.21 us -> 1.72 us  [stage(): pl.pallas_call(stage_kernel, out_shape=(rows, rows, jax.ShapeDtypeStruct(...]
    unnamed x17 -> x5, local copies, waits for them, and re-layouts: 1.24 us -> 0.02 us
    all_to_all x1, waiting for transfers between devices: 3.48 us -> 2.44 us  [body(): lax.all_to_all(copies, 'tile', 0, 0, axis_index_groups=along_z, tiled=True)]
    all_to_all x1, starting transfers between devices: 12.4 us -> 13.5 us  [body(): lax.all_to_all(energy, ('tile', 'lev'), 0, 0, axis_index_groups=along_zy,...]
  transfers between devices with their start and end apart: 7 -> 6, of which waited for: 2 -> 2; matrix products, arithmetic and copies ran while one was open for 3% -> 2% of each run, Pallas kernels for 0% -> 0%
where the time goes in v5:
time: 85 us; the launch traced here: 84.6 us
  starting transfers between devices  38.9 us (46%)
  blocking collectives  30.5 us (36%)
  waiting for transfers between devices  5.79 us (7%)
  Pallas kernels  4.06 us (5%)
  between operations  2.66 us (3%)
  other arithmetic  2.55 us (3%)
    all_to_all x1, starting transfers between devices, body(): lax.all_to_all(energy, ('tile', 'lev'), 0, 0, axis_index_groups=along_zy,...  13.5 us
    all_gather x1, blocking collectives, body(): lax.all_gather(block[None], 'tile', axis=0, axis_index_groups=plane, tile...  13.3 us
    ppermute x1, starting transfers between devices, body(): cross = lax.ppermute(to_cross, 'tile', cross_pairs(tile_count))  13 us
    all_gather x1, blocking collectives, body(): sent = lax.all_gather(summed[2:], 'tile', axis=0, axis_index_groups=pairs)  8.48 us
    all_gather x1, blocking collectives, body(): sent = lax.all_gather(halves[1], 'tile', axis=0, axis_index_groups=pairs)  6.86 us
    all_to_all x1, starting transfers between devices, body(): lax.all_to_all(copies, 'tile', 0, 0, axis_index_groups=along_z, tiled=True)  6.28 us
    ppermute x1, waiting for transfers between devices, swap_edges(): cross = lax.ppermute(to_cross, 'tile', cross_pairs(count))  3.34 us
    all_to_all x1, waiting for transfers between devices, body(): lax.all_to_all(copies, 'tile', 0, 0, axis_index_groups=along_z, tiled=True)  2.44 us
  transfers between devices with their start and end apart: 6, of which 2 were waited for; matrix products, arithmetic and copies ran while one was open for 2% of the time, Pallas kernels for 0%

profile of v5, /device:TPU:8, one launch (start us, length us, event | category | flops | bytes accessed | tf_op | source)
XLA Modules:
  0.0 84.6 jit_solution(2823095532176927685)
XLA Ops:
  0.6 1.7 %stage.1 = (bf16[128,128]{1,0:T(8,128)(2,1)S(1)}, bf16[128,128]{1,0:T(8,128)(2,1)S(1)}, bf16[16,32,256]{2,1,0:T(8,128)(2,1)}, f32[256,128]{1,0:T(8,128)S(1)}, f3...) custom-call(s32[1]{0:T(128)} %bitcast.me_ref, bf16[256,128]{1,0:T(8,128)(2,1)} %bitcast.44, ...), custom_call_target="tpu_custom_call" | custom-call | tf_op jit(solution)/shard_map/stage/pallas_call | solution.py:96
  2.4 13.0 %collective-permute-start = (bf16[128,128]{1,0:T(8,128)(2,1)S(1)}, bf16[128,128]{1,0:T(8,128)(2,1)S(1)}, u32[]{:S(2)}, u32[]{:S(2)}) collective-permute-start(bf16[128,128]{1,0:T(8,128)(2,1)S(1)} %get-tuple-element.19), channel_id=1, source_target_pairs={{0,508},{4,8},{8,4},{12,16},{16,12},{20,24},{24,20},{28,32},{32,28... | collective-permute-start | bytes 98312 | tf_op jit(solution)/shard_map/ppermute | solution.py:225
  15.4 6.3 %all-to-all-start = ((bf16[16,32,256]{2,1,0:T(8,128)(2,1)}), bf16[16,32,256]{2,1,0:T(8,128)(2,1)S(1)}, u32[]{:S(2)}, u32[]{:S(2)}) async-start(bf16[16,32,256]{2,1,0:T(8,128)(2,1)} %get-tuple-element.25), calls=%async_computation | async-start | bytes 524288 | tf_op jit(solution)/shard_map/all_to_all | solution.py:223
  21.7 0.0 collective-permute-done
  21.7 1.9 %all-gather = bf16[256,128]{1,0:T(8,128)(2,1)S(1)} all-gather(bf16[128,128]{1,0:T(8,128)(2,1)S(1)} %get-tuple-element.21), channel_id=2, replica_groups={{0,4},{8,12},{16,20},{24,28},{32,36},{40,44},{48,52},{56,60},{64,68},{7..., dimensions={0}, use_global_device_ids=true | all-gather | bytes 98304 | tf_op jit(solution)/shard_map/all_gather | solution.py:227
  23.6 0.1 pad_maximum_fusion.2
  23.7 0.2 multiply_add_fusion.1
  23.9 0.2 multiply_convert_fusion
  24.1 0.0 copy-start
  24.2 0.0 copy-start.1
  24.2 13.3 %all-gather.1 = bf16[1088,256]{1,0:T(8,128)(2,1)S(1)} all-gather(bf16[136,256]{1,0:T(8,128)(2,1)S(1)} %pad_maximum_fusion.4), channel_id=3, replica_groups={{0,4,8,12,16,20,24,28},{32,36,40,44,48,52,56,60},{64,68,72,76,80,84,88,..., dimensions={0}, use_global_device_ids=true | all-gather | bytes 626688 | tf_op jit(solution)/shard_map/all_gather | solution.py:245
  37.5 2.4 %all-to-all-done.jac = bf16[16,32,256]{2,1,0:T(8,128)(2,1)S(1)} async-done(((bf16[16,32,256]{2,1,0:T(8,128)(2,1)}), bf16[16,32,256]{2,1,0:T(8,128)(2,1)S(1)}, u32[]{:S(2)}, u32[]{:S(2)}) %all-to-all-start) | async-done | bytes 262176 | tf_op jit(solution)/shard_map/all_to_all | solution.py:223
  39.9 0.0 copy-done
  39.9 0.0 copy-done.1
  39.9 2.3 %respond.1 = (f32[4,128,256]{2,1,0:T(8,128)S(1)}, f32[4,128,256]{2,1,0:T(8,128)S(1)}, f32[64,1,128]{2,1,0:T(1,128)}) custom-call(s32[1]{0:T(128)} %bitcast.me_ref, bf16[8,136,256]{2,1,0:T(8,128)(2,1)S(1)} %bitcast.28, bf16[16,32,256]{2,1,0:T(8,128)(2,1)S(1)} %all-to-all-done.jac, s32[128,256]{1,0:T(8,128)S(1)} %copy-done, f32[128,256]{1,0:T(8,128)S(1)} %copy-done.1), custom_call_target="tpu_custom_call" | custom-call | tf_op jit(solution)/shard_map/respond/pallas_call | solution.py:193
  42.2 1.9 %collective-permute-start.1 = (f32[4,128,256]{2,1,0:T(8,128)S(1)}, f32[4,128,256]{2,1,0:T(8,128)S(1)}, u32[]{:S(2)}, u32[]{:S(2)}) collective-permute-start(f32[4,128,256]{2,1,0:T(8,128)S(1)} %get-tuple-element.27), channel_id=1, source_target_pairs={{0,4},{4,0},{8,12},{12,8},{16,20},{20,16},{24,28},{28,24},{32,36},... | collective-permute-start | bytes 1572872 | tf_op jit(solution)/shard_map/ppermute | solution.py:253
  44.2 13.5 %all-to-all-start.1 = ((f32[64,1,128]{2,1,0:T(1,128)}), f32[64,1,128]{2,1,0:T(1,128)S(1)}, u32[]{:S(2)}, u32[]{:S(2)}) async-start(f32[64,1,128]{2,1,0:T(1,128)} %get-tuple-element.28), calls=%async_computation.1 | async-start | bytes 65536 | tf_op jit(solution)/shard_map/all_to_all | solution.py:252
  57.6 0.0 collective-permute-done.1
  57.6 0.1 add.93
  57.8 8.5 %all-gather.2 = f32[4,128,256]{2,1,0:T(8,128)S(1)} all-gather(f32[2,128,256]{2,1,0:T(8,128)S(1)} %slice.104), channel_id=4, replica_groups={{0,8},{4,12},{16,24},{20,28},{32,40},{36,44},{48,56},{52,60},{64,72},{6..., dimensions={0}, use_global_device_ids=true | all-gather | bytes 786432 | tf_op jit(solution)/shard_map/all_gather | solution.py:256
  66.3 6.9 %all_gather.23 = f32[2,128,256]{2,1,0:T(8,128)S(1)} all-gather(f32[1,128,256]{2,1,0:T(8,128)S(1)} %slice.106), channel_id=1, replica_groups={{0,24},{4,28},{8,16},{12,20},{32,56},{36,60},{40,48},{44,52},{64,88},{6..., dimensions={0}, use_global_device_ids=true | all-gather | bytes 393216 | tf_op jit(solution)/shard_map/all_gather | solution.py:259
  73.2 0.1 add.98
  73.2 0.1 broadcast_multiply_fusion
  73.4 2.3 %collective-permute-start.2 = (f32[2,32,2,128]{3,2,1,0:T(2,128)S(1)}, f32[2,32,2,128]{3,2,1,0:T(2,128)S(1)}, u32[]{:S(2)}, u32[]{:S(2)}) collective-permute-start(f32[2,32,2,128]{3,2,1,0:T(2,128)S(1)} %get-tuple-element.35), channel_id=1, source_target_pairs={{0,508},{4,8},{8,4},{12,16},{16,12},{20,24},{24,20},{28,32},{32,28... | collective-permute-start | bytes 196616 | tf_op jit(solution)/shard_map/ppermute | solution.py:43
  75.7 1.9 %collective-permute-start.3 = (f32[2,32,2,128]{3,2,1,0:T(2,128)S(1)}, f32[2,32,2,128]{3,2,1,0:T(2,128)S(1)}, u32[]{:S(2)}, u32[]{:S(2)}) collective-permute-start(f32[2,32,2,128]{3,2,1,0:T(2,128)S(1)} %get-tuple-element.34), channel_id=1, source_target_pairs={{0,4},{4,0},{8,12},{12,8},{16,20},{20,16},{24,28},{28,24},{32,36},... | collective-permute-start | bytes 196616 | tf_op jit(solution)/shard_map/ppermute | solution.py:44
  77.6 0.0 all-to-all-done.1
  77.6 0.7 slice_reduce_fusion
  78.9 3.3 %collective-permute-done.2 = f32[2,32,2,128]{3,2,1,0:T(2,128)S(1)} collective-permute-done((f32[2,32,2,128]{3,2,1,0:T(2,128)S(1)}, f32[2,32,2,128]{3,2,1,0:T(2,128)S(1)}, u32[]{:S(2)}, u32[]{:S(2)}) %collective-permute-start.2) | collective-permute-done | bytes 65568 | tf_op jit(solution)/shard_map/ppermute | solution.py:43
  82.3 0.0 collective-permute-done.3
  82.3 0.1 pad_maximum_fusion
  82.4 0.2 multiply_add_fusion
  82.7 0.8 multiply_add_fusion.2
  (12 shorter events, 0.2 us)
Async XLA Ops:
  2.4 19.3 %collective-permute-start = (bf16[128,128]{1,0:T(8,128)(2,1)S(1)}, bf16[128,128]{1,0:T(8,128)(2,1)S(1)}, u32[]{:S(2)}, u32[]{:S(2)}) collective-permute-start(bf16[128,128]{1,0:T(8,128)(2,1)S(1)} %get-tuple-element.19), channel_id=1, source_target_pairs={{0,508},{4,8},{8,4},{12,16},{16,12},{20,24},{24,20},{28,32},{32,28... | collective-permute-start | bytes 98312 | tf_op jit(solution)/shard_map/ppermute | solution.py:225
  15.4 24.5 %all-to-all-start = ((bf16[16,32,256]{2,1,0:T(8,128)(2,1)}), bf16[16,32,256]{2,1,0:T(8,128)(2,1)S(1)}, u32[]{:S(2)}, u32[]{:S(2)}) async-start(bf16[16,32,256]{2,1,0:T(8,128)(2,1)} %get-tuple-element.25), calls=%async_computation | async-start | bytes 524288 | tf_op jit(solution)/shard_map/all_to_all | solution.py:223
  24.1 15.8 %copy-start = (s32[128,256]{1,0:T(8,128)S(1)}, s32[128,256]{1,0:T(8,128)}, u32[]{:S(2)}) copy-start(s32[128,256]{1,0:T(8,128)} %off.1) | copy-start | bytes 393220
  24.2 15.7 %copy-start.1 = (f32[128,256]{1,0:T(8,128)S(1)}, f32[128,256]{1,0:T(8,128)}, u32[]{:S(2)}) copy-start(f32[128,256]{1,0:T(8,128)} %wts.1) | copy-start | bytes 393220
  42.2 15.4 %collective-permute-start.1 = (f32[4,128,256]{2,1,0:T(8,128)S(1)}, f32[4,128,256]{2,1,0:T(8,128)S(1)}, u32[]{:S(2)}, u32[]{:S(2)}) collective-permute-start(f32[4,128,256]{2,1,0:T(8,128)S(1)} %get-tuple-element.27), channel_id=1, source_target_pairs={{0,4},{4,0},{8,12},{12,8},{16,20},{20,16},{24,28},{28,24},{32,36},... | collective-permute-start | bytes 1572872 | tf_op jit(solution)/shard_map/ppermute | solution.py:253
  44.2 33.5 %all-to-all-start.1 = ((f32[64,1,128]{2,1,0:T(1,128)}), f32[64,1,128]{2,1,0:T(1,128)S(1)}, u32[]{:S(2)}, u32[]{:S(2)}) async-start(f32[64,1,128]{2,1,0:T(1,128)} %get-tuple-element.28), calls=%async_computation.1 | async-start | bytes 65536 | tf_op jit(solution)/shard_map/all_to_all | solution.py:252
  73.4 8.9 %collective-permute-start.2 = (f32[2,32,2,128]{3,2,1,0:T(2,128)S(1)}, f32[2,32,2,128]{3,2,1,0:T(2,128)S(1)}, u32[]{:S(2)}, u32[]{:S(2)}) collective-permute-start(f32[2,32,2,128]{3,2,1,0:T(2,128)S(1)} %get-tuple-element.35), channel_id=1, source_target_pairs={{0,508},{4,8},{8,4},{12,16},{16,12},{20,24},{24,20},{28,32},{32,28... | collective-permute-start | bytes 196616 | tf_op jit(solution)/shard_map/ppermute | solution.py:43
  75.7 6.6 %collective-permute-start.3 = (f32[2,32,2,128]{3,2,1,0:T(2,128)S(1)}, f32[2,32,2,128]{3,2,1,0:T(2,128)S(1)}, u32[]{:S(2)}, u32[]{:S(2)}) collective-permute-start(f32[2,32,2,128]{3,2,1,0:T(2,128)S(1)} %get-tuple-element.34), channel_id=1, source_target_pairs={{0,4},{4,0},{8,12},{12,8},{16,20},{20,16},{24,28},{28,24},{32,36},... | collective-permute-start | bytes 196616 | tf_op jit(solution)/shard_map/ppermute | solution.py:44

commit v6 on v5

--- a/solution.py
+++ b/solution.py
@@ -43,17 +43,6 @@
     cross = lax.ppermute(to_cross, "tile", cross_pairs(count))
     near = lax.ppermute(to_near, "tile", [(i, i ^ 1) for i in range(count)])
     return cross, near
-
-
-def smooth(field, edges, diffusivity):
-    cross, near = edges
-    even = (lax.axis_index("tile") & 1) == 0
-    ext = jnp.concatenate(
-        [jnp.where(even, cross, near), field, jnp.where(even, near, cross)], axis=0
-    )
-    for _ in range(NSTEP):
-        ext = laplace_step(ext, diffusivity)
-    return ext
 
 
 def in_vmem(*arrays):
@@ -108,6 +97,39 @@
         out_specs=(vmem,) * 7,
         name="stage",
     )(me, probes, jac, stddev, diffusivity, columns, counts)
+
+
+def spread_kernel(me_ref, scaled, cross, near, rate, out):
+    wide = cross.shape[0] // NSTEP
+    even = (me_ref[0] & 1) == 0
+    before = jnp.where(even, cross[...], near[...])
+    after = jnp.where(even, near[...], cross[...])
+    tile = scaled[...]
+    grid = [b[i : i + wide] for b in (before, tile, after) for i in range(0, b.shape[0], wide)]
+    place = lax.broadcasted_iota(jnp.int32, (wide, scaled.shape[1]), 0)
+    speed = rate[...]
+    for _ in range(NSTEP):
+        new = []
+        for i in range(1, len(grid) - 1):
+            middle = grid[i]
+            following = jnp.where(place >= wide - 2, 0.0, pltpu.roll(middle, wide - 2, 0))
+            leading = jnp.where(place < 2, 0.0, pltpu.roll(middle, 2, 0))
+            laplace = grid[i + 1] + grid[i - 1] + following + leading - 4.0 * middle
+            new.append(middle + speed * laplace)
+        grid = new
+    for i, row in enumerate(grid):
+        out[i * wide : (i + 1) * wide] = row
+
+
+def spread_tile(me, scaled, cross, near, rate):
+    vmem = pl.BlockSpec(memory_space=pltpu.VMEM)
+    return pl.pallas_call(
+        spread_kernel,
+        out_shape=jax.ShapeDtypeStruct(scaled.shape, jnp.float32),
+        in_specs=[pl.BlockSpec(memory_space=pltpu.SMEM)] + [vmem] * 4,
+        out_specs=vmem,
+        name="diffuse",
+    )(me, *in_vmem(scaled, cross, near, rate))
 
 
 def band_columns(jac, offsets):
@@ -266,7 +288,9 @@
         * (1.0 / (probe_count * lev_count * tile_count * slot_count * channels))
     ).reshape(1)
     edges, trace_share = lax.optimization_barrier((edges, trace_share))
-    hessian = smooth(scaled, edges, rate[0])
+    hessian = spread_tile(
+        me.reshape(1), scaled.reshape(-1, levels), *(e.reshape(-1, levels) for e in edges), rate
+    ).reshape(scaled.shape)
     return (hessian, trace_share)
 
 

time: 85 us -> 84.7 us (level)
  other arithmetic: 2.55 us -> 1.46 us
    add x3 -> x1, other arithmetic: 1.22 us -> 0.22 us  [laplace_step(): return middle + diffusivity * laplace]
where the time goes in v6:
time: 84.7 us; the launch traced here: 84.2 us
  starting transfers between devices  38.9 us (46%)
  blocking collectives  30.5 us (36%)
  waiting for transfers between devices  5.7 us (7%)
  Pallas kernels  4.86 us (6%)
  between operations  2.65 us (3%)
  other arithmetic  1.46 us (2%)
    all_to_all x1, starting transfers between devices, body(): lax.all_to_all(energy, ('tile', 'lev'), 0, 0, axis_index_groups=along_zy,...  13.5 us
    all_gather x1, blocking collectives, body(): lax.all_gather(block[None], 'tile', axis=0, axis_index_groups=plane, tile...  13.3 us
    ppermute x1, starting transfers between devices, body(): cross = lax.ppermute(to_cross, 'tile', cross_pairs(tile_count))  13 us
    all_gather x1, blocking collectives, body(): sent = lax.all_gather(summed[2:], 'tile', axis=0, axis_index_groups=pairs)  8.49 us
    all_gather x1, blocking collectives, body(): sent = lax.all_gather(halves[1], 'tile', axis=0, axis_index_groups=pairs)  6.86 us
    all_to_all x1, starting transfers between devices, body(): lax.all_to_all(copies, 'tile', 0, 0, axis_index_groups=along_z, tiled=True)  6.28 us
    ppermute x1, waiting for transfers between devices, swap_edges(): cross = lax.ppermute(to_cross, 'tile', cross_pairs(count))  3.25 us
    all_to_all x1, waiting for transfers between devices, body(): lax.all_to_all(copies, 'tile', 0, 0, axis_index_groups=along_z, tiled=True)  2.44 us
  transfers between devices with their start and end apart: 6, of which 2 were waited for; matrix products, arithmetic and copies ran while one was open for 2% of the time, Pallas kernels for 0%

profile of v6, /device:TPU:8, one launch (start us, length us, event | category | flops | bytes accessed | tf_op | source)
XLA Modules:
  0.0 84.2 jit_solution(15833965806800477181)
XLA Ops:
  0.6 1.7 %stage.1 = (bf16[128,128]{1,0:T(8,128)(2,1)S(1)}, bf16[128,128]{1,0:T(8,128)(2,1)S(1)}, bf16[16,32,256]{2,1,0:T(8,128)(2,1)}, f32[256,128]{1,0:T(8,128)S(1)}, f3...) custom-call(s32[1]{0:T(128)} %bitcast.me_ref, bf16[256,128]{1,0:T(8,128)(2,1)} %bitcast.42, ...), custom_call_target="tpu_custom_call" | custom-call | tf_op jit(solution)/shard_map/stage/pallas_call | solution.py:85
  2.4 13.0 %collective-permute-start = (bf16[128,128]{1,0:T(8,128)(2,1)S(1)}, bf16[128,128]{1,0:T(8,128)(2,1)S(1)}, u32[]{:S(2)}, u32[]{:S(2)}) collective-permute-start(bf16[128,128]{1,0:T(8,128)(2,1)S(1)} %get-tuple-element.19), channel_id=1, source_target_pairs={{0,508},{4,8},{8,4},{12,16},{16,12},{20,24},{24,20},{28,32},{32,28... | collective-permute-start | bytes 98312 | tf_op jit(solution)/shard_map/ppermute | solution.py:247
  15.4 6.3 %all-to-all-start = ((bf16[16,32,256]{2,1,0:T(8,128)(2,1)}), bf16[16,32,256]{2,1,0:T(8,128)(2,1)S(1)}, u32[]{:S(2)}, u32[]{:S(2)}) async-start(bf16[16,32,256]{2,1,0:T(8,128)(2,1)} %get-tuple-element.25), calls=%async_computation | async-start | bytes 524288 | tf_op jit(solution)/shard_map/all_to_all | solution.py:245
  21.7 0.0 collective-permute-done
  21.7 1.9 %all-gather = bf16[256,128]{1,0:T(8,128)(2,1)S(1)} all-gather(bf16[128,128]{1,0:T(8,128)(2,1)S(1)} %get-tuple-element.21), channel_id=2, replica_groups={{0,4},{8,12},{16,20},{24,28},{32,36},{40,44},{48,52},{56,60},{64,68},{7..., dimensions={0}, use_global_device_ids=true | all-gather | bytes 98304 | tf_op jit(solution)/shard_map/all_gather | solution.py:249
  23.6 0.1 pad_maximum_fusion
  23.7 0.2 multiply_add_fusion
  23.9 0.2 multiply_convert_fusion
  24.1 0.0 copy-start
  24.2 0.0 copy-start.1
  24.2 13.3 %all-gather.1 = bf16[1088,256]{1,0:T(8,128)(2,1)S(1)} all-gather(bf16[136,256]{1,0:T(8,128)(2,1)S(1)} %pad_maximum_fusion.2), channel_id=3, replica_groups={{0,4,8,12,16,20,24,28},{32,36,40,44,48,52,56,60},{64,68,72,76,80,84,88,..., dimensions={0}, use_global_device_ids=true | all-gather | bytes 626688 | tf_op jit(solution)/shard_map/all_gather | solution.py:267
  37.5 2.4 %all-to-all-done.jac = bf16[16,32,256]{2,1,0:T(8,128)(2,1)S(1)} async-done(((bf16[16,32,256]{2,1,0:T(8,128)(2,1)}), bf16[16,32,256]{2,1,0:T(8,128)(2,1)S(1)}, u32[]{:S(2)}, u32[]{:S(2)}) %all-to-all-start) | async-done | bytes 262176 | tf_op jit(solution)/shard_map/all_to_all | solution.py:245
  39.9 0.0 copy-done
  39.9 0.0 copy-done.1
  39.9 2.3 %respond.1 = (f32[4,128,256]{2,1,0:T(8,128)S(1)}, f32[4,128,256]{2,1,0:T(8,128)S(1)}, f32[64,1,128]{2,1,0:T(1,128)}) custom-call(s32[1]{0:T(128)} %bitcast.me_ref, bf16[8,136,256]{2,1,0:T(8,128)(2,1)S(1)} %bitcast.28, bf16[16,32,256]{2,1,0:T(8,128)(2,1)S(1)} %all-to-all-done.jac, s32[128,256]{1,0:T(8,128)S(1)} %copy-done, f32[128,256]{1,0:T(8,128)S(1)} %copy-done.1), custom_call_target="tpu_custom_call" | custom-call | tf_op jit(solution)/shard_map/respond/pallas_call | solution.py:215
  42.3 1.9 %collective-permute-start.1 = (f32[4,128,256]{2,1,0:T(8,128)S(1)}, f32[4,128,256]{2,1,0:T(8,128)S(1)}, u32[]{:S(2)}, u32[]{:S(2)}) collective-permute-start(f32[4,128,256]{2,1,0:T(8,128)S(1)} %get-tuple-element.27), channel_id=1, source_target_pairs={{0,4},{4,0},{8,12},{12,8},{16,20},{20,16},{24,28},{28,24},{32,36},... | collective-permute-start | bytes 1572872 | tf_op jit(solution)/shard_map/ppermute | solution.py:275
  44.2 13.5 %all-to-all-start.1 = ((f32[64,1,128]{2,1,0:T(1,128)}), f32[64,1,128]{2,1,0:T(1,128)S(1)}, u32[]{:S(2)}, u32[]{:S(2)}) async-start(f32[64,1,128]{2,1,0:T(1,128)} %get-tuple-element.28), calls=%async_computation.1 | async-start | bytes 65536 | tf_op jit(solution)/shard_map/all_to_all | solution.py:274
  57.6 0.0 collective-permute-done.1
  57.6 0.1 add.69
  57.8 8.5 %all-gather.2 = f32[4,128,256]{2,1,0:T(8,128)S(1)} all-gather(f32[2,128,256]{2,1,0:T(8,128)S(1)} %slice.68), channel_id=4, replica_groups={{0,8},{4,12},{16,24},{20,28},{32,40},{36,44},{48,56},{52,60},{64,72},{6..., dimensions={0}, use_global_device_ids=true | all-gather | bytes 786432 | tf_op jit(solution)/shard_map/all_gather | solution.py:278
  66.3 6.9 %all_gather.23 = f32[2,128,256]{2,1,0:T(8,128)S(1)} all-gather(f32[1,128,256]{2,1,0:T(8,128)S(1)} %slice.70), channel_id=1, replica_groups={{0,24},{4,28},{8,16},{12,20},{32,56},{36,60},{40,48},{44,52},{64,88},{6..., dimensions={0}, use_global_device_ids=true | all-gather | bytes 393216 | tf_op jit(solution)/shard_map/all_gather | solution.py:281
  73.2 0.1 add.75
  73.2 0.1 broadcast_multiply_fusion
  73.3 0.1 broadcast_select_fusion
  73.4 2.3 %collective-permute-start.2 = (f32[2,32,2,128]{3,2,1,0:T(2,128)S(1)}, f32[2,32,2,128]{3,2,1,0:T(2,128)S(1)}, u32[]{:S(2)}, u32[]{:S(2)}) collective-permute-start(f32[2,32,2,128]{3,2,1,0:T(2,128)S(1)} %get-tuple-element.33), channel_id=1, source_target_pairs={{0,508},{4,8},{8,4},{12,16},{16,12},{20,24},{24,20},{28,32},{32,28... | collective-permute-start | bytes 196616 | tf_op jit(solution)/shard_map/ppermute | solution.py:43
  75.7 1.9 %collective-permute-start.3 = (f32[2,32,2,128]{3,2,1,0:T(2,128)S(1)}, f32[2,32,2,128]{3,2,1,0:T(2,128)S(1)}, u32[]{:S(2)}, u32[]{:S(2)}) collective-permute-start(f32[2,32,2,128]{3,2,1,0:T(2,128)S(1)} %get-tuple-element.32), channel_id=1, source_target_pairs={{0,4},{4,0},{8,12},{12,8},{16,20},{20,16},{24,28},{28,24},{32,36},... | collective-permute-start | bytes 196616 | tf_op jit(solution)/shard_map/ppermute | solution.py:44
  77.6 0.0 all-to-all-done.1
  77.6 0.7 slice_reduce_fusion
  79.0 3.2 %collective-permute-done.2 = f32[2,32,2,128]{3,2,1,0:T(2,128)S(1)} collective-permute-done((f32[2,32,2,128]{3,2,1,0:T(2,128)S(1)}, f32[2,32,2,128]{3,2,1,0:T(2,128)S(1)}, u32[]{:S(2)}, u32[]{:S(2)}) %collective-permute-start.2) | collective-permute-done | bytes 65568 | tf_op jit(solution)/shard_map/ppermute | solution.py:43
  82.3 0.0 collective-permute-done.3
  82.3 0.8 diffuse.1
  (12 shorter events, 0.2 us)
Async XLA Ops:
  2.4 19.3 %collective-permute-start = (bf16[128,128]{1,0:T(8,128)(2,1)S(1)}, bf16[128,128]{1,0:T(8,128)(2,1)S(1)}, u32[]{:S(2)}, u32[]{:S(2)}) collective-permute-start(bf16[128,128]{1,0:T(8,128)(2,1)S(1)} %get-tuple-element.19), channel_id=1, source_target_pairs={{0,508},{4,8},{8,4},{12,16},{16,12},{20,24},{24,20},{28,32},{32,28... | collective-permute-start | bytes 98312 | tf_op jit(solution)/shard_map/ppermute | solution.py:247
  15.4 24.5 %all-to-all-start = ((bf16[16,32,256]{2,1,0:T(8,128)(2,1)}), bf16[16,32,256]{2,1,0:T(8,128)(2,1)S(1)}, u32[]{:S(2)}, u32[]{:S(2)}) async-start(bf16[16,32,256]{2,1,0:T(8,128)(2,1)} %get-tuple-element.25), calls=%async_computation | async-start | bytes 524288 | tf_op jit(solution)/shard_map/all_to_all | solution.py:245
  24.1 15.8 %copy-start = (s32[128,256]{1,0:T(8,128)S(1)}, s32[128,256]{1,0:T(8,128)}, u32[]{:S(2)}) copy-start(s32[128,256]{1,0:T(8,128)} %off.1) | copy-start | bytes 393220
  24.2 15.7 %copy-start.1 = (f32[128,256]{1,0:T(8,128)S(1)}, f32[128,256]{1,0:T(8,128)}, u32[]{:S(2)}) copy-start(f32[128,256]{1,0:T(8,128)} %wts.1) | copy-start | bytes 393220
  42.3 15.4 %collective-permute-start.1 = (f32[4,128,256]{2,1,0:T(8,128)S(1)}, f32[4,128,256]{2,1,0:T(8,128)S(1)}, u32[]{:S(2)}, u32[]{:S(2)}) collective-permute-start(f32[4,128,256]{2,1,0:T(8,128)S(1)} %get-tuple-element.27), channel_id=1, source_target_pairs={{0,4},{4,0},{8,12},{12,8},{16,20},{20,16},{24,28},{28,24},{32,36},... | collective-permute-start | bytes 1572872 | tf_op jit(solution)/shard_map/ppermute | solution.py:275
  44.2 33.4 %all-to-all-start.1 = ((f32[64,1,128]{2,1,0:T(1,128)}), f32[64,1,128]{2,1,0:T(1,128)S(1)}, u32[]{:S(2)}, u32[]{:S(2)}) async-start(f32[64,1,128]{2,1,0:T(1,128)} %get-tuple-element.28), calls=%async_computation.1 | async-start | bytes 65536 | tf_op jit(solution)/shard_map/all_to_all | solution.py:274
  73.4 8.9 %collective-permute-start.2 = (f32[2,32,2,128]{3,2,1,0:T(2,128)S(1)}, f32[2,32,2,128]{3,2,1,0:T(2,128)S(1)}, u32[]{:S(2)}, u32[]{:S(2)}) collective-permute-start(f32[2,32,2,128]{3,2,1,0:T(2,128)S(1)} %get-tuple-element.33), channel_id=1, source_target_pairs={{0,508},{4,8},{8,4},{12,16},{16,12},{20,24},{24,20},{28,32},{32,28... | collective-permute-start | bytes 196616 | tf_op jit(solution)/shard_map/ppermute | solution.py:43
  75.7 6.6 %collective-permute-start.3 = (f32[2,32,2,128]{3,2,1,0:T(2,128)S(1)}, f32[2,32,2,128]{3,2,1,0:T(2,128)S(1)}, u32[]{:S(2)}, u32[]{:S(2)}) collective-permute-start(f32[2,32,2,128]{3,2,1,0:T(2,128)S(1)} %get-tuple-element.32), channel_id=1, source_target_pairs={{0,4},{4,0},{8,12},{12,8},{16,20},{20,16},{24,28},{28,24},{32,36},... | collective-permute-start | bytes 196616 | tf_op jit(solution)/shard_map/ppermute | solution.py:44

commit v7 on v6

--- a/solution.py
+++ b/solution.py
@@ -8,7 +8,6 @@
 NSTEP = 2
 ZS, XS, CS = 16, 4, 2
 QS = XS * CS
-HALVING = (0, 3, 1, 2)
 
 
 def tile_groups(sizes, free):
@@ -200,8 +199,9 @@
         energy[s * each : (s + 1) * each] = jnp.broadcast_to(
             jnp.sum(total, axis=1, keepdims=True)[None], (each,) + energy.shape[1:]
         )
-    for j, away in enumerate(HALVING):
-        for half, out in ((0, mine), (1, other)):
+    for half, out in ((0, mine), (1, other)):
+        late = 3 - 2 * ((me ^ half) & 1)
+        for j, away in enumerate((0, late, 4 - late, 2)):
             q = me ^ (CS * away + half)
             out[j] = jnp.dot(sel[q], adj[q], preferred_element_type=jnp.float32)
 
@@ -273,13 +273,19 @@
     along_zy = [[t * lev_count + y for t in group for y in range(lev_count)] for group in along_z]
     shares = lax.all_to_all(energy, ("tile", "lev"), 0, 0, axis_index_groups=along_zy, tiled=True)
     summed = mine + lax.ppermute(other, "tile", [(i, i ^ 1) for i in range(tile_count)])
-    x = here >> 1
-    pairs = [[t, t + CS] for t in range(tile_count) if (t >> 1) & 1 == 0]
-    sent = lax.all_gather(summed[2:], "tile", axis=0, axis_index_groups=pairs)
-    halves = summed[:2] + lax.dynamic_index_in_dim(sent, 1 - (x & 1), 0, keepdims=False)
-    pairs = [[t, t ^ (3 * CS)] for t in range(tile_count) if (t >> 1) & 2 == 0]
-    sent = lax.all_gather(halves[1], "tile", axis=0, axis_index_groups=pairs)
-    gradient = halves[0] + lax.dynamic_index_in_dim(sent, 1 - ((x >> 1) & 1), 0, keepdims=False)
+    x = (here >> 1) & (XS - 1)
+    even = (here & 1) == 0
+    low, high = x & 1, x >> 1
+    steps = [
+        [[t, t ^ (CS * k[t & 1])] for t in range(tile_count) if t < t ^ (CS * k[t & 1])]
+        for k in ((1, 3), (3, 1))
+    ]
+    sent = lax.all_gather(summed[2:], "tile", axis=0, axis_index_groups=steps[0])
+    part = 1 - jnp.where(even, low, high)
+    halves = summed[:2] + lax.dynamic_index_in_dim(sent, part, 0, keepdims=False)
+    sent = lax.all_gather(halves[1], "tile", axis=0, axis_index_groups=steps[1])
+    part = 1 - jnp.where(even, high, low)
+    gradient = halves[0] + lax.dynamic_index_in_dim(sent, part, 0, keepdims=False)
     gradient = gradient.reshape(row_count, col_count, probe_count, levels)
     scaled = spread[:, :, None, :] * gradient
     edges = swap_edges(*edge_rows(scaled, NSTEP))

time: 84.7 us -> 83.4 us (0.985)
  blocking collectives: 30.5 us -> 29 us
    all_gather x2, blocking collectives: 15.3 us -> 13.9 us  [the longest x1 7.05 us: body(): lax.all_gather(summed[2:], 'tile', axis=0, axis_index_groups=steps[0])]
where the time goes in v7:
time: 83.4 us; the launch traced here: 82.9 us
  starting transfers between devices  38.9 us (47%)
  blocking collectives  29 us (35%)
  waiting for transfers between devices  5.65 us (7%)
  Pallas kernels  4.98 us (6%)
  between operations  2.66 us (3%)
  other arithmetic  1.46 us (2%)
    all_to_all x1, starting transfers between devices, body(): lax.all_to_all(energy, ('tile', 'lev'), 0, 0, axis_index_groups=along_zy,...  13.5 us
    all_gather x1, blocking collectives, body(): lax.all_gather(block[None], 'tile', axis=0, axis_index_groups=plane, tile...  13.3 us
    ppermute x1, starting transfers between devices, body(): cross = lax.ppermute(to_cross, 'tile', cross_pairs(tile_count))  13 us
    all_gather x1, blocking collectives, body(): lax.all_gather(summed[2:], 'tile', axis=0, axis_index_groups=steps[0])  7.05 us
    all_gather x1, blocking collectives, body(): sent = lax.all_gather(halves[1], 'tile', axis=0, axis_index_groups=steps[1])  6.86 us
    all_to_all x1, starting transfers between devices, body(): lax.all_to_all(copies, 'tile', 0, 0, axis_index_groups=along_z, tiled=True)  6.28 us
    ppermute x1, waiting for transfers between devices, swap_edges(): cross = lax.ppermute(to_cross, 'tile', cross_pairs(count))  3.2 us
    pallas_call x1, Pallas kernels, respond_all(): pl.pallas_call(respond_kernel, out_shape=(part, part, pltpu.VMEM((section...  2.47 us
  transfers between devices with their start and end apart: 6, of which 2 were waited for; matrix products, arithmetic and copies ran while one was open for 2% of the time, Pallas kernels for 0%

profile of v7, /device:TPU:8, one launch (start us, length us, event | category | flops | bytes accessed | tf_op | source)
XLA Modules:
  0.0 82.9 jit_solution(4906154174773788494)
XLA Ops:
  0.6 1.7 %stage.1 = (bf16[128,128]{1,0:T(8,128)(2,1)S(1)}, bf16[128,128]{1,0:T(8,128)(2,1)S(1)}, bf16[16,32,256]{2,1,0:T(8,128)(2,1)}, f32[256,128]{1,0:T(8,128)S(1)}, f3...) custom-call(s32[1]{0:T(128)} %bitcast.me_ref, bf16[256,128]{1,0:T(8,128)(2,1)} %bitcast.42, ...), custom_call_target="tpu_custom_call" | custom-call | tf_op jit(solution)/shard_map/stage/pallas_call | solution.py:84
  2.4 13.0 %collective-permute-start = (bf16[128,128]{1,0:T(8,128)(2,1)S(1)}, bf16[128,128]{1,0:T(8,128)(2,1)S(1)}, u32[]{:S(2)}, u32[]{:S(2)}) collective-permute-start(bf16[128,128]{1,0:T(8,128)(2,1)S(1)} %get-tuple-element.19), channel_id=1, source_target_pairs={{0,508},{4,8},{8,4},{12,16},{16,12},{20,24},{24,20},{28,32},{32,28... | collective-permute-start | bytes 98312 | tf_op jit(solution)/shard_map/ppermute | solution.py:247
  15.4 6.3 %all-to-all-start = ((bf16[16,32,256]{2,1,0:T(8,128)(2,1)}), bf16[16,32,256]{2,1,0:T(8,128)(2,1)S(1)}, u32[]{:S(2)}, u32[]{:S(2)}) async-start(bf16[16,32,256]{2,1,0:T(8,128)(2,1)} %get-tuple-element.25), calls=%async_computation | async-start | bytes 524288 | tf_op jit(solution)/shard_map/all_to_all | solution.py:245
  21.7 0.0 collective-permute-done
  21.7 1.9 %all-gather = bf16[256,128]{1,0:T(8,128)(2,1)S(1)} all-gather(bf16[128,128]{1,0:T(8,128)(2,1)S(1)} %get-tuple-element.21), channel_id=2, replica_groups={{0,4},{8,12},{16,20},{24,28},{32,36},{40,44},{48,52},{56,60},{64,68},{7..., dimensions={0}, use_global_device_ids=true | all-gather | bytes 98304 | tf_op jit(solution)/shard_map/all_gather | solution.py:249
  23.6 0.1 pad_maximum_fusion
  23.7 0.2 multiply_add_fusion
  23.9 0.2 multiply_convert_fusion
  24.1 0.0 copy-start
  24.2 0.0 copy-start.1
  24.2 13.3 %all-gather.1 = bf16[1088,256]{1,0:T(8,128)(2,1)S(1)} all-gather(bf16[136,256]{1,0:T(8,128)(2,1)S(1)} %pad_maximum_fusion.2), channel_id=3, replica_groups={{0,4,8,12,16,20,24,28},{32,36,40,44,48,52,56,60},{64,68,72,76,80,84,88,..., dimensions={0}, use_global_device_ids=true | all-gather | bytes 626688 | tf_op jit(solution)/shard_map/all_gather | solution.py:267
  37.5 2.4 %all-to-all-done.jac = bf16[16,32,256]{2,1,0:T(8,128)(2,1)S(1)} async-done(((bf16[16,32,256]{2,1,0:T(8,128)(2,1)}), bf16[16,32,256]{2,1,0:T(8,128)(2,1)S(1)}, u32[]{:S(2)}, u32[]{:S(2)}) %all-to-all-start) | async-done | bytes 262176 | tf_op jit(solution)/shard_map/all_to_all | solution.py:245
  39.9 0.0 copy-done
  39.9 0.0 copy-done.1
  39.9 2.5 %respond.1 = (f32[4,128,256]{2,1,0:T(8,128)S(1)}, f32[4,128,256]{2,1,0:T(8,128)S(1)}, f32[64,1,128]{2,1,0:T(1,128)}) custom-call(s32[1]{0:T(128)} %bitcast.me_ref, bf16[8,136,256]{2,1,0:T(8,128)(2,1)S(1)} %bitcast.28, bf16[16,32,256]{2,1,0:T(8,128)(2,1)S(1)} %all-to-all-done.jac, s32[128,256]{1,0:T(8,128)S(1)} %copy-done, f32[128,256]{1,0:T(8,128)S(1)} %copy-done.1), custom_call_target="tpu_custom_call" | custom-call | tf_op jit(solution)/shard_map/respond/pallas_call | solution.py:215
  42.4 1.9 %collective-permute-start.1 = (f32[4,128,256]{2,1,0:T(8,128)S(1)}, f32[4,128,256]{2,1,0:T(8,128)S(1)}, u32[]{:S(2)}, u32[]{:S(2)}) collective-permute-start(f32[4,128,256]{2,1,0:T(8,128)S(1)} %get-tuple-element.27), channel_id=1, source_target_pairs={{0,4},{4,0},{8,12},{12,8},{16,20},{20,16},{24,28},{28,24},{32,36},... | collective-permute-start | bytes 1572872 | tf_op jit(solution)/shard_map/ppermute | solution.py:275
  44.3 13.5 %all-to-all-start.1 = ((f32[64,1,128]{2,1,0:T(1,128)}), f32[64,1,128]{2,1,0:T(1,128)S(1)}, u32[]{:S(2)}, u32[]{:S(2)}) async-start(f32[64,1,128]{2,1,0:T(1,128)} %get-tuple-element.28), calls=%async_computation.1 | async-start | bytes 65536 | tf_op jit(solution)/shard_map/all_to_all | solution.py:274
  57.8 0.0 collective-permute-done.1
  57.8 0.1 add.69
  57.9 7.0 %all-gather.2 = f32[4,128,256]{2,1,0:T(8,128)S(1)} all-gather(f32[2,128,256]{2,1,0:T(8,128)S(1)} %slice.68), channel_id=4, replica_groups={{0,8},{4,28},{12,20},{16,24},{32,40},{36,60},{44,52},{48,56},{64,72},{6..., dimensions={0}, use_global_device_ids=true | all-gather | bytes 786432 | tf_op jit(solution)/shard_map/all_gather | solution.py:283
  65.0 6.9 %all_gather.23 = f32[2,128,256]{2,1,0:T(8,128)S(1)} all-gather(f32[1,128,256]{2,1,0:T(8,128)S(1)} %slice.70), channel_id=1, replica_groups={{0,24},{4,12},{8,16},{20,28},{32,56},{36,44},{40,48},{52,60},{64,88},{6..., dimensions={0}, use_global_device_ids=true | all-gather | bytes 393216 | tf_op jit(solution)/shard_map/all_gather | solution.py:286
  71.9 0.1 add.75
  71.9 0.1 broadcast_multiply_fusion
  72.1 2.3 %collective-permute-start.2 = (f32[2,32,2,128]{3,2,1,0:T(2,128)S(1)}, f32[2,32,2,128]{3,2,1,0:T(2,128)S(1)}, u32[]{:S(2)}, u32[]{:S(2)}) collective-permute-start(f32[2,32,2,128]{3,2,1,0:T(2,128)S(1)} %get-tuple-element.33), channel_id=1, source_target_pairs={{0,508},{4,8},{8,4},{12,16},{16,12},{20,24},{24,20},{28,32},{32,28... | collective-permute-start | bytes 196616 | tf_op jit(solution)/shard_map/ppermute | solution.py:42
  74.4 1.9 %collective-permute-start.3 = (f32[2,32,2,128]{3,2,1,0:T(2,128)S(1)}, f32[2,32,2,128]{3,2,1,0:T(2,128)S(1)}, u32[]{:S(2)}, u32[]{:S(2)}) collective-permute-start(f32[2,32,2,128]{3,2,1,0:T(2,128)S(1)} %get-tuple-element.32), channel_id=1, source_target_pairs={{0,4},{4,0},{8,12},{12,8},{16,20},{20,16},{24,28},{28,24},{32,36},... | collective-permute-start | bytes 196616 | tf_op jit(solution)/shard_map/ppermute | solution.py:43
  76.4 0.0 all-to-all-done.1
  76.4 0.7 slice_reduce_fusion
  77.8 3.2 %collective-permute-done.2 = f32[2,32,2,128]{3,2,1,0:T(2,128)S(1)} collective-permute-done((f32[2,32,2,128]{3,2,1,0:T(2,128)S(1)}, f32[2,32,2,128]{3,2,1,0:T(2,128)S(1)}, u32[]{:S(2)}, u32[]{:S(2)}) %collective-permute-start.2) | collective-permute-done | bytes 65568 | tf_op jit(solution)/shard_map/ppermute | solution.py:42
  81.0 0.0 collective-permute-done.3
  81.0 0.8 diffuse.1
  (13 shorter events, 0.3 us)
Async XLA Ops:
  2.4 19.3 %collective-permute-start = (bf16[128,128]{1,0:T(8,128)(2,1)S(1)}, bf16[128,128]{1,0:T(8,128)(2,1)S(1)}, u32[]{:S(2)}, u32[]{:S(2)}) collective-permute-start(bf16[128,128]{1,0:T(8,128)(2,1)S(1)} %get-tuple-element.19), channel_id=1, source_target_pairs={{0,508},{4,8},{8,4},{12,16},{16,12},{20,24},{24,20},{28,32},{32,28... | collective-permute-start | bytes 98312 | tf_op jit(solution)/shard_map/ppermute | solution.py:247
  15.4 24.5 %all-to-all-start = ((bf16[16,32,256]{2,1,0:T(8,128)(2,1)}), bf16[16,32,256]{2,1,0:T(8,128)(2,1)S(1)}, u32[]{:S(2)}, u32[]{:S(2)}) async-start(bf16[16,32,256]{2,1,0:T(8,128)(2,1)} %get-tuple-element.25), calls=%async_computation | async-start | bytes 524288 | tf_op jit(solution)/shard_map/all_to_all | solution.py:245
  24.1 15.8 %copy-start = (s32[128,256]{1,0:T(8,128)S(1)}, s32[128,256]{1,0:T(8,128)}, u32[]{:S(2)}) copy-start(s32[128,256]{1,0:T(8,128)} %off.1) | copy-start | bytes 393220
  24.2 15.7 %copy-start.1 = (f32[128,256]{1,0:T(8,128)S(1)}, f32[128,256]{1,0:T(8,128)}, u32[]{:S(2)}) copy-start(f32[128,256]{1,0:T(8,128)} %wts.1) | copy-start | bytes 393220
  42.4 15.4 %collective-permute-start.1 = (f32[4,128,256]{2,1,0:T(8,128)S(1)}, f32[4,128,256]{2,1,0:T(8,128)S(1)}, u32[]{:S(2)}, u32[]{:S(2)}) collective-permute-start(f32[4,128,256]{2,1,0:T(8,128)S(1)} %get-tuple-element.27), channel_id=1, source_target_pairs={{0,4},{4,0},{8,12},{12,8},{16,20},{20,16},{24,28},{28,24},{32,36},... | collective-permute-start | bytes 1572872 | tf_op jit(solution)/shard_map/ppermute | solution.py:275
  44.3 32.0 %all-to-all-start.1 = ((f32[64,1,128]{2,1,0:T(1,128)}), f32[64,1,128]{2,1,0:T(1,128)S(1)}, u32[]{:S(2)}, u32[]{:S(2)}) async-start(f32[64,1,128]{2,1,0:T(1,128)} %get-tuple-element.28), calls=%async_computation.1 | async-start | bytes 65536 | tf_op jit(solution)/shard_map/all_to_all | solution.py:274
  72.1 8.9 %collective-permute-start.2 = (f32[2,32,2,128]{3,2,1,0:T(2,128)S(1)}, f32[2,32,2,128]{3,2,1,0:T(2,128)S(1)}, u32[]{:S(2)}, u32[]{:S(2)}) collective-permute-start(f32[2,32,2,128]{3,2,1,0:T(2,128)S(1)} %get-tuple-element.33), channel_id=1, source_target_pairs={{0,508},{4,8},{8,4},{12,16},{16,12},{20,24},{24,20},{28,32},{32,28... | collective-permute-start | bytes 196616 | tf_op jit(solution)/shard_map/ppermute | solution.py:42
  74.4 6.6 %collective-permute-start.3 = (f32[2,32,2,128]{3,2,1,0:T(2,128)S(1)}, f32[2,32,2,128]{3,2,1,0:T(2,128)S(1)}, u32[]{:S(2)}, u32[]{:S(2)}) collective-permute-start(f32[2,32,2,128]{3,2,1,0:T(2,128)S(1)} %get-tuple-element.32), channel_id=1, source_target_pairs={{0,4},{4,0},{8,12},{12,8},{16,20},{20,16},{24,28},{28,24},{32,36},... | collective-permute-start | bytes 196616 | tf_op jit(solution)/shard_map/ppermute | solution.py:43

commit v8 on v7

--- a/solution.py
+++ b/solution.py
@@ -86,7 +86,7 @@
         out_shape=(
             rows,
             rows,
-            jax.ShapeDtypeStruct((ZS,) + jac.shape, jac.dtype),
+            pltpu.VMEM((ZS,) + jac.shape, jac.dtype),
             pltpu.VMEM(probes.shape, jnp.float32),
             pltpu.VMEM(stddev.shape, jnp.float32),
             pltpu.VMEM(diffusivity.shape, jnp.float32),

time: 83.4 us -> 83.4 us (level)
  no operation moved by 1% of the time
where the time goes in v8:
time: 83.4 us; the launch traced here: 82.9 us
  starting transfers between devices  38.9 us (47%)
  blocking collectives  29 us (35%)
  waiting for transfers between devices  5.65 us (7%)
  Pallas kernels  4.98 us (6%)
  between operations  2.65 us (3%)
  other arithmetic  1.46 us (2%)
    all_to_all x1, starting transfers between devices, body(): lax.all_to_all(energy, ('tile', 'lev'), 0, 0, axis_index_groups=along_zy,...  13.5 us
    all_gather x1, blocking collectives, body(): lax.all_gather(block[None], 'tile', axis=0, axis_index_groups=plane, tile...  13.3 us
    ppermute x1, starting transfers between devices, body(): cross = lax.ppermute(to_cross, 'tile', cross_pairs(tile_count))  13 us
    all_gather x1, blocking collectives, body(): lax.all_gather(summed[2:], 'tile', axis=0, axis_index_groups=steps[0])  7.05 us
    all_gather x1, blocking collectives, body(): sent = lax.all_gather(halves[1], 'tile', axis=0, axis_index_groups=steps[1])  6.86 us
    all_to_all x1, starting transfers between devices, body(): lax.all_to_all(copies, 'tile', 0, 0, axis_index_groups=along_z, tiled=True)  6.28 us
    ppermute x1, waiting for transfers between devices, swap_edges(): cross = lax.ppermute(to_cross, 'tile', cross_pairs(count))  3.2 us
    pallas_call x1, Pallas kernels, respond_all(): pl.pallas_call(respond_kernel, out_shape=(part, part, pltpu.VMEM((section...  2.47 us
  transfers between devices with their start and end apart: 6, of which 2 were waited for; matrix products, arithmetic and copies ran while one was open for 2% of the time, Pallas kernels for 0%

profile of v8, /device:TPU:8, one launch (start us, length us, event | category | flops | bytes accessed | tf_op | source)
XLA Modules:
  0.0 82.9 jit_solution(3847589058341791376)
XLA Ops:
  0.6 1.7 %stage.1 = (bf16[128,128]{1,0:T(8,128)(2,1)S(1)}, bf16[128,128]{1,0:T(8,128)(2,1)S(1)}, bf16[16,32,256]{2,1,0:T(8,128)(2,1)}, f32[256,128]{1,0:T(8,128)S(1)}, f3...) custom-call(s32[1]{0:T(128)} %bitcast.me_ref, bf16[256,128]{1,0:T(8,128)(2,1)} %bitcast.42, ...), custom_call_target="tpu_custom_call" | custom-call | tf_op jit(solution)/shard_map/stage/pallas_call | solution.py:84
  2.4 13.0 %collective-permute-start = (bf16[128,128]{1,0:T(8,128)(2,1)S(1)}, bf16[128,128]{1,0:T(8,128)(2,1)S(1)}, u32[]{:S(2)}, u32[]{:S(2)}) collective-permute-start(bf16[128,128]{1,0:T(8,128)(2,1)S(1)} %get-tuple-element.19), channel_id=1, source_target_pairs={{0,508},{4,8},{8,4},{12,16},{16,12},{20,24},{24,20},{28,32},{32,28... | collective-permute-start | bytes 98312 | tf_op jit(solution)/shard_map/ppermute | solution.py:247
  15.4 6.3 %all-to-all-start = ((bf16[16,32,256]{2,1,0:T(8,128)(2,1)}), bf16[16,32,256]{2,1,0:T(8,128)(2,1)S(1)}, u32[]{:S(2)}, u32[]{:S(2)}) async-start(bf16[16,32,256]{2,1,0:T(8,128)(2,1)} %get-tuple-element.25), calls=%async_computation | async-start | bytes 524288 | tf_op jit(solution)/shard_map/all_to_all | solution.py:245
  21.7 0.0 collective-permute-done
  21.7 1.9 %all-gather = bf16[256,128]{1,0:T(8,128)(2,1)S(1)} all-gather(bf16[128,128]{1,0:T(8,128)(2,1)S(1)} %get-tuple-element.21), channel_id=2, replica_groups={{0,4},{8,12},{16,20},{24,28},{32,36},{40,44},{48,52},{56,60},{64,68},{7..., dimensions={0}, use_global_device_ids=true | all-gather | bytes 98304 | tf_op jit(solution)/shard_map/all_gather | solution.py:249
  23.6 0.1 pad_maximum_fusion
  23.7 0.2 multiply_add_fusion
  23.9 0.2 multiply_convert_fusion
  24.1 0.0 copy-start
  24.2 0.0 copy-start.1
  24.2 13.3 %all-gather.1 = bf16[1088,256]{1,0:T(8,128)(2,1)S(1)} all-gather(bf16[136,256]{1,0:T(8,128)(2,1)S(1)} %pad_maximum_fusion.2), channel_id=3, replica_groups={{0,4,8,12,16,20,24,28},{32,36,40,44,48,52,56,60},{64,68,72,76,80,84,88,..., dimensions={0}, use_global_device_ids=true | all-gather | bytes 626688 | tf_op jit(solution)/shard_map/all_gather | solution.py:267
  37.5 2.4 %all-to-all-done.jac = bf16[16,32,256]{2,1,0:T(8,128)(2,1)S(1)} async-done(((bf16[16,32,256]{2,1,0:T(8,128)(2,1)}), bf16[16,32,256]{2,1,0:T(8,128)(2,1)S(1)}, u32[]{:S(2)}, u32[]{:S(2)}) %all-to-all-start) | async-done | bytes 262176 | tf_op jit(solution)/shard_map/all_to_all | solution.py:245
  39.9 0.0 copy-done
  39.9 0.0 copy-done.1
  39.9 2.5 %respond.1 = (f32[4,128,256]{2,1,0:T(8,128)S(1)}, f32[4,128,256]{2,1,0:T(8,128)S(1)}, f32[64,1,128]{2,1,0:T(1,128)}) custom-call(s32[1]{0:T(128)} %bitcast.me_ref, bf16[8,136,256]{2,1,0:T(8,128)(2,1)S(1)} %bitcast.28, bf16[16,32,256]{2,1,0:T(8,128)(2,1)S(1)} %all-to-all-done.jac, s32[128,256]{1,0:T(8,128)S(1)} %copy-done, f32[128,256]{1,0:T(8,128)S(1)} %copy-done.1), custom_call_target="tpu_custom_call" | custom-call | tf_op jit(solution)/shard_map/respond/pallas_call | solution.py:215
  42.4 1.9 %collective-permute-start.1 = (f32[4,128,256]{2,1,0:T(8,128)S(1)}, f32[4,128,256]{2,1,0:T(8,128)S(1)}, u32[]{:S(2)}, u32[]{:S(2)}) collective-permute-start(f32[4,128,256]{2,1,0:T(8,128)S(1)} %get-tuple-element.27), channel_id=1, source_target_pairs={{0,4},{4,0},{8,12},{12,8},{16,20},{20,16},{24,28},{28,24},{32,36},... | collective-permute-start | bytes 1572872 | tf_op jit(solution)/shard_map/ppermute | solution.py:275
  44.3 13.5 %all-to-all-start.1 = ((f32[64,1,128]{2,1,0:T(1,128)}), f32[64,1,128]{2,1,0:T(1,128)S(1)}, u32[]{:S(2)}, u32[]{:S(2)}) async-start(f32[64,1,128]{2,1,0:T(1,128)} %get-tuple-element.28), calls=%async_computation.1 | async-start | bytes 65536 | tf_op jit(solution)/shard_map/all_to_all | solution.py:274
  57.8 0.0 collective-permute-done.1
  57.8 0.1 add.69
  57.9 7.0 %all-gather.2 = f32[4,128,256]{2,1,0:T(8,128)S(1)} all-gather(f32[2,128,256]{2,1,0:T(8,128)S(1)} %slice.68), channel_id=4, replica_groups={{0,8},{4,28},{12,20},{16,24},{32,40},{36,60},{44,52},{48,56},{64,72},{6..., dimensions={0}, use_global_device_ids=true | all-gather | bytes 786432 | tf_op jit(solution)/shard_map/all_gather | solution.py:283
  65.0 6.9 %all_gather.23 = f32[2,128,256]{2,1,0:T(8,128)S(1)} all-gather(f32[1,128,256]{2,1,0:T(8,128)S(1)} %slice.70), channel_id=1, replica_groups={{0,24},{4,12},{8,16},{20,28},{32,56},{36,44},{40,48},{52,60},{64,88},{6..., dimensions={0}, use_global_device_ids=true | all-gather | bytes 393216 | tf_op jit(solution)/shard_map/all_gather | solution.py:286
  71.9 0.1 add.75
  71.9 0.1 broadcast_multiply_fusion
  72.1 2.3 %collective-permute-start.2 = (f32[2,32,2,128]{3,2,1,0:T(2,128)S(1)}, f32[2,32,2,128]{3,2,1,0:T(2,128)S(1)}, u32[]{:S(2)}, u32[]{:S(2)}) collective-permute-start(f32[2,32,2,128]{3,2,1,0:T(2,128)S(1)} %get-tuple-element.33), channel_id=1, source_target_pairs={{0,508},{4,8},{8,4},{12,16},{16,12},{20,24},{24,20},{28,32},{32,28... | collective-permute-start | bytes 196616 | tf_op jit(solution)/shard_map/ppermute | solution.py:42
  74.4 1.9 %collective-permute-start.3 = (f32[2,32,2,128]{3,2,1,0:T(2,128)S(1)}, f32[2,32,2,128]{3,2,1,0:T(2,128)S(1)}, u32[]{:S(2)}, u32[]{:S(2)}) collective-permute-start(f32[2,32,2,128]{3,2,1,0:T(2,128)S(1)} %get-tuple-element.32), channel_id=1, source_target_pairs={{0,4},{4,0},{8,12},{12,8},{16,20},{20,16},{24,28},{28,24},{32,36},... | collective-permute-start | bytes 196616 | tf_op jit(solution)/shard_map/ppermute | solution.py:43
  76.3 0.0 all-to-all-done.1
  76.4 0.7 slice_reduce_fusion
  77.8 3.2 %collective-permute-done.2 = f32[2,32,2,128]{3,2,1,0:T(2,128)S(1)} collective-permute-done((f32[2,32,2,128]{3,2,1,0:T(2,128)S(1)}, f32[2,32,2,128]{3,2,1,0:T(2,128)S(1)}, u32[]{:S(2)}, u32[]{:S(2)}) %collective-permute-start.2) | collective-permute-done | bytes 65568 | tf_op jit(solution)/shard_map/ppermute | solution.py:42
  81.0 0.0 collective-permute-done.3
  81.0 0.8 diffuse.1
  (13 shorter events, 0.3 us)
Async XLA Ops:
  2.4 19.3 %collective-permute-start = (bf16[128,128]{1,0:T(8,128)(2,1)S(1)}, bf16[128,128]{1,0:T(8,128)(2,1)S(1)}, u32[]{:S(2)}, u32[]{:S(2)}) collective-permute-start(bf16[128,128]{1,0:T(8,128)(2,1)S(1)} %get-tuple-element.19), channel_id=1, source_target_pairs={{0,508},{4,8},{8,4},{12,16},{16,12},{20,24},{24,20},{28,32},{32,28... | collective-permute-start | bytes 98312 | tf_op jit(solution)/shard_map/ppermute | solution.py:247
  15.4 24.5 %all-to-all-start = ((bf16[16,32,256]{2,1,0:T(8,128)(2,1)}), bf16[16,32,256]{2,1,0:T(8,128)(2,1)S(1)}, u32[]{:S(2)}, u32[]{:S(2)}) async-start(bf16[16,32,256]{2,1,0:T(8,128)(2,1)} %get-tuple-element.25), calls=%async_computation | async-start | bytes 524288 | tf_op jit(solution)/shard_map/all_to_all | solution.py:245
  24.1 15.8 %copy-start = (s32[128,256]{1,0:T(8,128)S(1)}, s32[128,256]{1,0:T(8,128)}, u32[]{:S(2)}) copy-start(s32[128,256]{1,0:T(8,128)} %off.1) | copy-start | bytes 393220
  24.2 15.7 %copy-start.1 = (f32[128,256]{1,0:T(8,128)S(1)}, f32[128,256]{1,0:T(8,128)}, u32[]{:S(2)}) copy-start(f32[128,256]{1,0:T(8,128)} %wts.1) | copy-start | bytes 393220
  42.4 15.4 %collective-permute-start.1 = (f32[4,128,256]{2,1,0:T(8,128)S(1)}, f32[4,128,256]{2,1,0:T(8,128)S(1)}, u32[]{:S(2)}, u32[]{:S(2)}) collective-permute-start(f32[4,128,256]{2,1,0:T(8,128)S(1)} %get-tuple-element.27), channel_id=1, source_target_pairs={{0,4},{4,0},{8,12},{12,8},{16,20},{20,16},{24,28},{28,24},{32,36},... | collective-permute-start | bytes 1572872 | tf_op jit(solution)/shard_map/ppermute | solution.py:275
  44.3 32.0 %all-to-all-start.1 = ((f32[64,1,128]{2,1,0:T(1,128)}), f32[64,1,128]{2,1,0:T(1,128)S(1)}, u32[]{:S(2)}, u32[]{:S(2)}) async-start(f32[64,1,128]{2,1,0:T(1,128)} %get-tuple-element.28), calls=%async_computation.1 | async-start | bytes 65536 | tf_op jit(solution)/shard_map/all_to_all | solution.py:274
  72.1 8.9 %collective-permute-start.2 = (f32[2,32,2,128]{3,2,1,0:T(2,128)S(1)}, f32[2,32,2,128]{3,2,1,0:T(2,128)S(1)}, u32[]{:S(2)}, u32[]{:S(2)}) collective-permute-start(f32[2,32,2,128]{3,2,1,0:T(2,128)S(1)} %get-tuple-element.33), channel_id=1, source_target_pairs={{0,508},{4,8},{8,4},{12,16},{16,12},{20,24},{24,20},{28,32},{32,28... | collective-permute-start | bytes 196616 | tf_op jit(solution)/shard_map/ppermute | solution.py:42
  74.4 6.6 %collective-permute-start.3 = (f32[2,32,2,128]{3,2,1,0:T(2,128)S(1)}, f32[2,32,2,128]{3,2,1,0:T(2,128)S(1)}, u32[]{:S(2)}, u32[]{:S(2)}) collective-permute-start(f32[2,32,2,128]{3,2,1,0:T(2,128)S(1)} %get-tuple-element.32), channel_id=1, source_target_pairs={{0,4},{4,0},{8,12},{12,8},{16,20},{20,16},{24,28},{28,24},{32,36},... | collective-permute-start | bytes 196616 | tf_op jit(solution)/shard_map/ppermute | solution.py:43
